TPU v7x, 128 devices: a whole 4x4x4 slice. The times are simulated.
128 devices in a mesh: dp: 2 (over core), space: 64 (over y, z, x).
Axes of the slice: x: 4, y: 4, z: 4, core: 2. Of those that a mesh axis runs over, the one named last changes fastest.
Arguments:
- features: bfloat16 [2, 4096, 16, 1024], P('dp', 'space'), may hold values from -6 to 6
- psi: bfloat16 [2, 4096, 64, 256], P('dp', 'space'), may hold values from -0.75 to 0.75
- neighbors: int32 [2, 4096, 16], P('dp', 'space'), may hold values from 0 to 4095, as said below
- counts: int32 [2, 4096], P('dp', 'space'), may hold values from 4 to 16, as said below
- occupation: float32 [2, 256], P('dp'), may hold values from 0.1 to 1
- weights: bfloat16 [1024, 4096], P(None, 'space'), may hold values from -0.1875 to 0.1875
Outputs:
- energies: float32 [2, 256], P('dp')
- gradient: float32 [4096, 1024], P('space')
Inputs may be any that keep to these rules, and one draw needn't show every extreme that they name: `neighbors`: every neighbor tile lies in the same cluster of 64 consecutive tiles or in one of the two clusters beside it, counted around a closed loop of 64 clusters. `counts`: the first tile of every twist uses all 16 slots.
All inputs are finite; a program needn't handle non-finite values.
Results may differ from a plain program's by a relative error of at most 0.004.
Values may be sent and summed in bfloat16 or wider, within the bound.
No kernel may reach another device: no remote copies, remote signals or barrier semaphores. Data moves between devices by JAX's collectives and lax.ppermute only.
A program may use at most 192 MiB of HBM per device.

v0:
```python
import math

import jax
import jax.numpy as jnp
from jax import lax
from jax.sharding import PartitionSpec as P


def with_halo(value, sides, width):
    for axis, dim in sides:
        size, length = (lax.axis_size(axis), value.shape[dim])
        up = [(i, (i + 1) % size) for i in range(size)]
        down = [(j, i) for i, j in up]
        last = lax.slice_in_dim(value, length - width, length, axis=dim)
        leading = lax.slice_in_dim(value, 0, width, axis=dim)
        before = lax.ppermute(last, axis, up)
        after = lax.ppermute(leading, axis, down)
        value = jnp.concatenate([before, value, after], axis=dim)
    return value


def local(features, psi, neighbors, counts, occupation, weights):
    twists_here, rows, slots, width = features.shape
    orbit = psi.shape[2]
    bands = psi.shape[3]
    nspace = lax.axis_size("space")
    myself = lax.axis_index("space")
    factor = 1.0 / math.sqrt(rows * nspace * slots)
    flat = features.reshape(twists_here * rows * slots, width)
    products = jnp.dot(
        flat,
        lax.all_gather(weights, "space", axis=1, tiled=True),
        preferred_element_type=jnp.float32,
    )
    valid = (
        lax.broadcasted_iota(jnp.int32, (twists_here, rows, slots), 2) < counts[:, :, None]
    ).astype(jnp.bfloat16)
    blocks = (
        products.astype(jnp.bfloat16).reshape(twists_here, rows, slots, orbit, orbit)
        * valid[:, :, :, None, None]
    )
    widened = with_halo(psi, (("space", 1),), rows)
    owners = neighbors // rows
    placed = (owners - myself + 1 + nspace) % nspace * rows + neighbors % rows
    weighted = (psi.astype(jnp.float32) * occupation[:, None, None, :]).astype(jnp.bfloat16)

    def per_slot(carry, inputs):
        block_k, index_k, valid_k = inputs
        fetched = jax.vmap(lambda table, where: table[where])(widened, index_k)
        carry = carry + jnp.einsum(
            "trac,trcb->trab", block_k, fetched, preferred_element_type=jnp.float32
        )
        grad_k = (
            factor
            * jnp.einsum("trab,trcb->trac", weighted, fetched, preferred_element_type=jnp.float32)
        ).astype(jnp.bfloat16)
        return (carry, grad_k * valid_k[:, :, None, None])

    inputs = (jnp.moveaxis(blocks, 2, 0), jnp.moveaxis(placed, 2, 0), jnp.moveaxis(valid, 2, 0))
    applied, dblocks = lax.scan(
        per_slot, jnp.zeros((twists_here, rows, orbit, bands), jnp.float32), inputs
    )
    partial_energy = factor * jnp.sum(psi.astype(jnp.float32) * applied, axis=(1, 2))
    energies = lax.psum(partial_energy, "space")
    square = orbit * orbit
    flat_grads = dblocks.reshape(slots, twists_here, rows, square)
    share = lax.psum_scatter(
        jnp.einsum("strO,trsf->Of", flat_grads, features, preferred_element_type=jnp.float32),
        "space",
        scatter_dimension=0,
        tiled=True,
    )
    gradient = lax.psum(share, "dp")
    return (energies, gradient)


def solution(mesh):
    placed = (
        P("dp", "space", None, None),
        P("dp", "space", None, None),
        P("dp", "space", None),
        P("dp", "space"),
        P("dp", None),
        P(None, "space"),
    )
    return jax.shard_map(
        local,
        mesh=mesh,
        in_specs=placed,
        out_specs=(P("dp", None), P("space", None)),
        check_vma=False,
    )
```

profile of v0, /device:TPU:0, one launch (start us, length us, event | category | flops | bytes accessed | tf_op | source)
XLA Modules:
  0.0 1062.5 jit_solution(6959014675251214178)
XLA Ops:
  9.6 7.3 collective-permute-start.1
  22.7 41.5 %collective-permute-done = bf16[1,64,64,256]{3,2,1,0:T(8,128)(2,1)} collective-permute-done((bf16[1,64,64,256]{3,2,1,0:T(8,128)(2,1)}, bf16[1,64,64,256]{3,2,1,0:T(8,128)(2,1)}, u32[]{:S(2)}, u32[]{:S(2)}) %collective-permute-start) | collective-permute-done | bytes 2097184 | tf_op jit(solution)/shard_map/ppermute | solution.py:16
  64.2 5.5 pad_maximum_fusion
  69.7 51.4 %all-gather.2.cloned.1.call-done = bf16[1024,4096]{0,1:T(8,128)(2,1)} async-done(((bf16[1024,64]{0,1:T(8,128)(2,1)}), bf16[1024,4096]{0,1:T(8,128)(2,1)}) %all-gather.2.cloned.1.call-update) | async-done | bytes 8388624 | tf_op jit(solution)/shard_map/all_gather | solution.py:32
  121.1 14.3 %convolution_convert_fusion = bf16[1024,4096]{1,0:T(8,128)(2,1)} fusion(bf16[1024,1024]{1,0:T(8,128)(2,1)S(1)} %bitcast.74, bf16[1024,4096]{0,1:T(8,128)(2,1)} %all-gather.2.cloned.1.call-done), kind=kOutput, calls=%fused_computation.21 | convolution fusion | flops 8594128896 | bytes 18874368 | tf_op jit(solution)/shard_map/dot_general | solution.py:30
  135.4 23.6 %reshape.163 = bf16[1,64,16,64,64]{4,3,2,1,0:T(8,128)(2,1)} reshape(bf16[1024,4096]{1,0:T(8,128)(2,1)} %convolution_convert_fusion) | data formatting | bytes 16777216 | tf_op jit(solution)/shard_map/reshape | solution.py:39
  159.0 14.0 %fusion.15 = bf16[16,1,64,64,64]{4,3,2,1,0:T(8,128)(2,1)} fusion(bf16[1,64,16,64,64]{4,3,2,1,0:T(8,128)(2,1)} %reshape.163, bf16[64,16]{0,1:T(8,128)(2,1)S(1)} %fusion.24), kind=kLoop, calls=%fused_computation.19 | loop fusion | flops 4194304 | bytes 16779264 | tf_op jit(solution)/shard_map/transpose | solution.py:59
  173.0 274.1 %while.13 = (s32[]{:T(128)}, f32[1,64,64,256]{3,2,1,0:T(8,128)}, bf16[16,1,64,64,64]{4,3,2,0,1:T(8,128)(2,1)}, bf16[16,1,64,64,64]{4,3,2,1,0:T(8,128)(2,1)}, s32...) while((s32[]{:T(128)}, f32[1,64,64,256]{3,2,1,0:T(8,128)}, ...), condition=%wide.region_1.2_spmd.clone, body=%wide.region_0.1_spmd.clone.sunk | while | flops 271319552 | bytes 23071752 | solution.py:60
  189.0 4.8 gather_fusion
  199.3 5.8 bitcast_add_fusion.2
  216.5 5.8 bitcast_add_fusion.2
  223.5 4.8 gather_fusion
  233.7 5.8 bitcast_add_fusion.2
  240.6 4.8 gather_fusion
  250.9 5.8 bitcast_add_fusion.2
  268.1 5.8 bitcast_add_fusion.2
  285.3 5.8 bitcast_add_fusion.2
  292.3 4.8 gather_fusion
  302.5 5.8 bitcast_add_fusion.2
  319.7 5.8 bitcast_add_fusion.2
  326.7 4.8 gather_fusion
  337.0 5.8 bitcast_add_fusion.2
  354.2 5.8 bitcast_add_fusion.2
  371.4 5.8 bitcast_add_fusion.2
  388.5 5.8 bitcast_add_fusion.2
  405.8 5.8 bitcast_add_fusion.2
  423.0 5.8 bitcast_add_fusion.2
  440.2 5.8 bitcast_add_fusion.2
  447.1 22.6 %reshape.164 = bf16[16,64,4096]{2,1,0:T(8,128)(2,1)} reshape(bf16[16,1,64,64,64]{4,3,2,0,1:T(8,128)(2,1)} %get-tuple-element.46) | data formatting | bytes 16777216 | tf_op jit(solution)/shard_map/reshape.16
  469.7 15.7 %convolution_bitcast_fusion = f32[4096,1024]{1,0:T(8,128)} fusion(bf16[16,64,4096]{2,1,0:T(8,128)(2,1)} %reshape.164, bf16[64,16,1024]{2,1,0:T(8,128)(2,1)S(1)} %bitcast.75), kind=kOutput, calls=%fused_computation.20 | convolution fusion | flops 8589934592 | bytes 27262976 | tf_op jit(solution)/shard_map/strO,trsf->Of/dot_general | solution.py:68
  485.4 392.0 %reduce-scatter.2.cloned.1.call-done = f32[64,1024]{1,0:T(8,128)} async-done(((f32[4096,1024]{1,0:T(8,128)}), f32[64,1024]{1,0:T(8,128)}) %reduce-scatter.2.cloned.1.call-update) | async-done | bytes 262160 | tf_op jit(solution)/shard_map/reduce_scatter | solution.py:67
  880.9 173.4 %psum.14 = f32[1,256]{1,0:T(1,128)} all-reduce(f32[1,256]{1,0:T(1,128)S(1)} %bitcast.77), channel_id=1, replica_groups=mesh['dp'=2,'space'=64] {'space'}, use_global_device_ids=true, to_apply=%region_3.4 | all-reduce | flops 256 | bytes 2048 | tf_op jit(solution)/shard_map/psum | solution.py:64
  (146 shorter events, 176.0 us)
Async XLA Ops:
  7.2 114.0 %copy-start = (bf16[1,64,16,1024]{3,2,1,0:T(8,128)(2,1)S(1)}, bf16[1,64,16,1024]{3,2,1,0:T(8,128)(2,1)}, u32[]{:S(2)}) copy-start(bf16[1,64,16,1024]{3,2,1,0:T(8,128)(2,1)} %param.8) | copy-start | bytes 6291460
  7.2 113.9 %all-gather.2.cloned.1.call-start = ((), (), s32[]{:S(2)}) async-start(), calls=%async_computation.1 | async-start | bytes 8519680 | tf_op jit(solution)/shard_map/all_gather | solution.py:32
  7.9 869.5 %reduce-scatter.2.cloned.1.call-start = ((), (), s32[]{:S(2)}) async-start(), calls=%async_computation.2 | async-start | bytes 17039360 | tf_op jit(solution)/shard_map/reduce_scatter | solution.py:67
  8.0 56.2 %collective-permute-start = (bf16[1,64,64,256]{3,2,1,0:T(8,128)(2,1)}, bf16[1,64,64,256]{3,2,1,0:T(8,128)(2,1)}, u32[]{:S(2)}, u32[]{:S(2)}) collective-permute-start(bf16[1,64,64,256]{3,2,1,0:T(8,128)(2,1)} %param.9), channel_id=1, source_target_pairs={{0,1},{1,2},{2,3},{3,4},{4,5},{5,6},{6,7},{7,8},{8,9},{9,10},{10,1... | collective-permute-start | bytes 6291464 | tf_op jit(solution)/shard_map/ppermute | solution.py:16
  9.6 54.6 %collective-permute-start.1 = (bf16[1,64,64,256]{3,2,1,0:T(8,128)(2,1)}, bf16[1,64,64,256]{3,2,1,0:T(8,128)(2,1)}, u32[]{:S(2)}, u32[]{:S(2)}) collective-permute-start(bf16[1,64,64,256]{3,2,1,0:T(8,128)(2,1)} %param.9), channel_id=1, source_target_pairs={{1,0},{2,1},{3,2},{4,3},{5,4},{6,5},{7,6},{8,7},{9,8},{10,9},{11,1... | collective-permute-start | bytes 6291464 | tf_op jit(solution)/shard_map/ppermute | solution.py:17
  16.9 47.3 %copy-start.1 = (bf16[1,64,64,256]{3,2,1,0:T(8,128)(2,1)S(1)}, bf16[1,64,64,256]{3,2,1,0:T(8,128)(2,1)}, u32[]{:S(2)}) copy-start(bf16[1,64,64,256]{3,2,1,0:T(8,128)(2,1)} %param.9) | copy-start | bytes 6291460
  485.4 568.9 %all-reduce.2.cloned.1.call-start = ((), (), s32[]{:S(2)}) async-start(), calls=%async_computation.3 | async-start | bytes 524288 | tf_op jit(solution)/shard_map/psum | solution.py:73
Sparse Core Ops, SparseCore 0:
  10.9 110.2 all-gather.1
  485.5 391.8 reduce-scatter.1
  879.8 18.4 all-reduce.1
where the time goes:
time: 1070 us; the launch traced here: 1060 us
  waiting for transfers between devices  486 us (45%)
  matrix products  184 us (17%)
  blocking collectives  173 us (16%)
  local copies, waits for them, and re-layouts  167 us (16%)
  other arithmetic  28.9 us (3%)
  between operations  13.8 us (1%)
    reduce_scatter x1, waiting for transfers between devices, local(): lax.psum_scatter(jnp.einsum('strO,trsf->Of', flat_grads, features, prefer...  392 us
    psum x1, blocking collectives, local(): energies = lax.psum(partial_energy, 'space')  173 us
    dot_general x16, matrix products, per_slot(): jnp.einsum('trac,trcb->trab', block_k, fetched, preferred_element_type=jn...  92 us
    gather x32, local copies, waits for them, and re-layouts, per_slot(): fetched = jax.vmap(lambda table, where: table[where])(widened, index_k)  76.5 us
    dot_general x16, matrix products, per_slot(): jnp.einsum('trab,trcb->trac', weighted, fetched, preferred_element_type=j...  62.4 us
    all_gather x1, waiting for transfers between devices, local(): lax.all_gather(weights, 'space', axis=1, tiled=True)  51.4 us
    dynamic_update_slice x32, local copies, waits for them, and re-layouts, local(): lax.scan(per_slot, jnp.zeros((twists_here, rows, orbit, bands), jnp.float...  42.7 us
    ppermute x1, waiting for transfers between devices, with_halo(): before = lax.ppermute(last, axis, up)  41.5 us
  transfers between devices with their start and end apart: 5, of which 3 were waited for; matrix products, arithmetic and copies ran while one was open for 1% of the time, Pallas kernels for 0%

commit v1 on v0

v1 whole, which is shorter than its diff:
```python
import functools
import math

import jax
import jax.numpy as jnp
from jax import lax
from jax.experimental import pallas as pl
from jax.experimental.pallas import tpu as pltpu
from jax.sharding import PartitionSpec as P

ORB = 64
BANDS = 256
SLOTS = 16
HALF = SLOTS // 2
TILES = 64
EDGES = TILES * SLOTS
PAIRS = TILES * HALF
FEAT = 1024
PITCH = PAIRS + 8
ZERO_TILE = 3 * TILES
NT = (((1,), (1,)), ((), ()))


def load_table(prev, own, following, table, sems):
    copies = [
        pltpu.make_async_copy(src, table.at[pl.ds(n * TILES, TILES)], sems.at[n])
        for n, src in enumerate((prev, own, following))
    ]
    for copy in copies:
        copy.start()
    table[ZERO_TILE] = jnp.zeros((ORB, BANDS), jnp.bfloat16)
    for copy in copies:
        copy.wait()


def four_tiles(index, table, tile, first):
    picks = [table[index[tile, k]] for k in (first, first + HALF, first + 1, first + 1 + HALF)]
    return jnp.concatenate(picks, axis=0)


def left_lanes(shape):
    return lax.broadcasted_iota(jnp.int32, shape, len(shape) - 1) < ORB


def swap(value):
    return pltpu.roll(value, ORB, value.ndim - 1)


def grad_blocks_kernel(index, prev, own, following, occupation, out, table, strips, sems, *, factor):
    step = pl.program_id(0)

    @pl.when(step == 0)
    def _():
        load_table(prev, own, following, table, sems)
        occ = occupation[...]

        def tile_body(tile, carry):
            weighted = (table[TILES + tile].astype(jnp.float32) * occ).astype(jnp.bfloat16)
            for first in range(0, HALF, 2):
                product = lax.dot_general(
                    weighted,
                    four_tiles(index, table, tile, first),
                    NT,
                    preferred_element_type=jnp.float32,
                )
                row = tile * HALF + first
                strips[pl.ds(row, ORB, stride=PITCH), :] = product[:, :128]
                strips[pl.ds(row + 1, ORB, stride=PITCH), :] = product[:, 128:]
            return carry

        lax.fori_loop(0, TILES, tile_body, 0, unroll=2)

    width = out.shape[1] // ORB
    group = 8

    def group_body(g, carry):
        for pair in range(width // 2):
            base = (step * width + 2 * pair) * PITCH + g * (group * HALF)
            one = strips[pl.ds(pl.multiple_of(base, 8), group * HALF), :] * factor
            two = strips[pl.ds(pl.multiple_of(base + PITCH, 8), group * HALF), :] * factor
            low = left_lanes(one.shape)
            front = jnp.where(low, one, swap(two)).reshape(group, 1, HALF, 128)
            back = jnp.where(low, swap(one), two).reshape(group, 1, HALF, 128)
            both = jnp.concatenate([front, back], axis=1).reshape(group * SLOTS, 128)
            rows = pl.ds(pl.multiple_of(g * (group * SLOTS), 16), group * SLOTS)
            out[rows, pair * 128 : (pair + 1) * 128] = both.astype(jnp.bfloat16)
        return carry

    lax.fori_loop(0, TILES // group, group_body, 0)


def grad_blocks(index, prev, own, following, occupation, factor):
    block = 512
    return pl.pallas_call(
        functools.partial(grad_blocks_kernel, factor=factor),
        grid_spec=pltpu.PrefetchScalarGridSpec(
            num_scalar_prefetch=1,
            grid=(ORB * ORB // block,),
            in_specs=[pl.BlockSpec(memory_space=pl.ANY)] * 3
            + [pl.BlockSpec((1, BANDS), lambda j, index: (0, 0))],
            out_specs=pl.BlockSpec((EDGES, block), lambda j, index: (0, j)),
            scratch_shapes=[
                pltpu.VMEM((ZERO_TILE + 1, ORB, BANDS), jnp.bfloat16),
                pltpu.VMEM((ORB * PITCH, 128), jnp.float32),
                pltpu.SemaphoreType.DMA((3,)),
            ],
        ),
        out_shape=jax.ShapeDtypeStruct((EDGES, ORB * ORB), jnp.bfloat16),
        compiler_params=pltpu.CompilerParams(vmem_limit_bytes=44 * 2**20),
        cost_estimate=pl.CostEstimate(
            flops=2 * EDGES * ORB * ORB * BANDS * 4, bytes_accessed=16 * 2**20, transcendentals=0
        ),
        name="grad_blocks",
    )(index, prev, own, following, occupation)


def energy_kernel(index, prev, own, following, edges, weights, out, table, strips, sems, *, factor):
    step = pl.program_id(0)
    width = weights.shape[0] // ORB
    group = 16

    @pl.when(step == 0)
    def _():
        load_table(prev, own, following, table, sems)

    def group_body(g, carry):
        rows = pl.ds(pl.multiple_of(g * (group * SLOTS), 16), group * SLOTS)
        product = lax.dot_general(
            edges[rows, :], weights[...], NT, preferred_element_type=jnp.float32
        )
        for pair in range(width // 2):
            both = product[:, pair * 128 : (pair + 1) * 128].reshape(group, 2, HALF, 128)
            front = both[:, 0].reshape(group * HALF, 128)
            back = both[:, 1].reshape(group * HALF, 128)
            low = left_lanes(front.shape)
            base = (step * width + 2 * pair) * PITCH + g * (group * HALF)
            strips[pl.ds(pl.multiple_of(base, 8), group * HALF), :] = jnp.where(
                low, front, swap(back)
            )
            strips[pl.ds(pl.multiple_of(base + PITCH, 8), group * HALF), :] = jnp.where(
                low, swap(front), back
            )
        return carry

    lax.fori_loop(0, TILES // group, group_body, 0)

    @pl.when(step == pl.num_programs(0) - 1)
    def _():
        def tile_body(tile, total):
            applied = jnp.zeros((ORB, BANDS), jnp.float32)
            for first in range(0, HALF, 2):
                row = tile * HALF + first
                left = jnp.concatenate(
                    [
                        strips[pl.ds(row, ORB, stride=PITCH), :].astype(jnp.bfloat16),
                        strips[pl.ds(row + 1, ORB, stride=PITCH), :].astype(jnp.bfloat16),
                    ],
                    axis=1,
                )
                applied = applied + jnp.dot(
                    left,
                    four_tiles(index, table, tile, first),
                    preferred_element_type=jnp.float32,
                )
            terms = table[TILES + tile].astype(jnp.float32) * applied
            return total + jnp.sum(terms.reshape(8, 8, BANDS), axis=0)

        total = lax.fori_loop(0, TILES, tile_body, jnp.zeros((8, BANDS), jnp.float32), unroll=2)
        out[...] = jnp.sum(total, axis=0, keepdims=True) * factor


def energy_share(index, prev, own, following, edges, weights, factor):
    block = 256
    return pl.pallas_call(
        functools.partial(energy_kernel, factor=factor),
        grid_spec=pltpu.PrefetchScalarGridSpec(
            num_scalar_prefetch=1,
            grid=(ORB * ORB // block,),
            in_specs=[pl.BlockSpec(memory_space=pl.ANY)] * 3
            + [
                pl.BlockSpec((EDGES, FEAT), lambda j, index: (0, 0)),
                pl.BlockSpec((block, FEAT), lambda j, index: (j, 0)),
            ],
            out_specs=pl.BlockSpec((1, BANDS), lambda j, index: (0, 0)),
            scratch_shapes=[
                pltpu.VMEM((ZERO_TILE + 1, ORB, BANDS), jnp.bfloat16),
                pltpu.VMEM((ORB * PITCH, 128), jnp.float32),
                pltpu.SemaphoreType.DMA((3,)),
            ],
        ),
        out_shape=jax.ShapeDtypeStruct((1, BANDS), jnp.float32),
        compiler_params=pltpu.CompilerParams(vmem_limit_bytes=44 * 2**20),
        cost_estimate=pl.CostEstimate(
            flops=2 * EDGES * ORB * ORB * (FEAT + BANDS * 4), bytes_accessed=16 * 2**20, transcendentals=0
        ),
        name="energy_share",
    )(index, prev, own, following, edges, weights)


def local(features, psi, neighbors, counts, occupation, weights):
    nspace = lax.axis_size("space")
    myself = lax.axis_index("space")
    core = lax.axis_index("dp")
    factor = 1.0 / math.sqrt(TILES * nspace * SLOTS)
    edges = features.reshape(EDGES, FEAT)
    own = psi.reshape(TILES, ORB, BANDS)
    up = [(i, (i + 1) % nspace) for i in range(nspace)]
    down = [(j, i) for i, j in up]
    prev = lax.ppermute(own, "space", up)
    following = lax.ppermute(own, "space", down)
    gathered = lax.all_gather(weights.T, "space", axis=0, tiled=True)

    where = neighbors.reshape(TILES, SLOTS)
    placed = (where // TILES - myself + 1 + nspace) % nspace * TILES + where % TILES
    slot = lax.broadcasted_iota(jnp.int32, (TILES, SLOTS), 1)
    index = jnp.where(slot < counts.reshape(TILES, 1), placed, ZERO_TILE)

    blocks = grad_blocks(index, prev, own, following, occupation, factor)
    half = FEAT // 2
    theirs = lax.dynamic_slice_in_dim(edges, (1 - core) * half, half, 1)
    mine = lax.dynamic_slice_in_dim(edges, core * half, half, 1)
    over_edges = (((0,), (0,)), ((), ()))
    send = lax.dot_general(blocks, theirs, over_edges, preferred_element_type=jnp.float32)
    other = lax.ppermute(send.astype(jnp.bfloat16), "dp", [(0, 1), (1, 0)])
    keep = lax.dot_general(blocks, mine, over_edges, preferred_element_type=jnp.float32)
    summed = (keep + other.astype(jnp.float32)).astype(jnp.bfloat16)
    parts = lax.all_to_all(summed, "space", 0, 0, tiled=True)
    share = jnp.sum(parts.reshape(nspace, ORB, half).astype(jnp.float32), axis=0)
    gradient = lax.all_gather(share, "dp", axis=1, tiled=True)

    partial = energy_share(index, prev, own, following, edges, gathered, factor)
    energies = lax.psum(partial, "space")
    return (energies, gradient)


def solution(mesh):
    placed = (
        P("dp", "space", None, None),
        P("dp", "space", None, None),
        P("dp", "space", None),
        P("dp", "space"),
        P("dp", None),
        P(None, "space"),
    )
    return jax.shard_map(
        local,
        mesh=mesh,
        in_specs=placed,
        out_specs=(P("dp", None), P("space", None)),
        check_vma=False,
    )
```

time: 1070 us -> 411 us (0.38)
  waiting for transfers between devices: 486 us -> 59.6 us
  matrix products: 184 us -> 19.4 us
  local copies, waits for them, and re-layouts: 167 us -> 10 us
  Pallas kernels: 0 us -> 64.8 us
  blocking collectives: 173 us -> 233 us
  other arithmetic: 28.9 us -> 1.36 us
    reduce_scatter x1 -> x0, waiting for transfers between devices: 392 us -> none  [local(): lax.psum_scatter(jnp.einsum('strO,trsf->Of', flat_grads, features, prefer...]
    dot_general x34 -> x2, matrix products: 184 us -> 19.4 us  [the longest x1 10.2 us: local(): lax.dot_general(blocks, theirs, over_edges, preferred_element_type=jnp.fl...]
    gather x32 -> x0, local copies, waits for them, and re-layouts: 76.5 us -> none  [per_slot(): fetched = jax.vmap(lambda table, where: table[where])(widened, index_k)]
    pallas_call x0 -> x2, Pallas kernels: none -> 64.8 us  [the longest x1 39.4 us: energy_share(): pl.pallas_call(functools.partial(energy_kernel, factor=factor), grid_spec...]
    all_to_all x0 -> x1, blocking collectives: none -> 57.7 us  [local(): parts = lax.all_to_all(summed, 'space', 0, 0, tiled=True)]
    all_gather x1, waiting for transfers between devices: 51.4 us -> 0.01 us  [local(): gathered = lax.all_gather(weights.T, 'space', axis=0, tiled=True)]
    dynamic_update_slice x32 -> x0, local copies, waits for them, and re-layouts: 42.7 us -> none  [local(): lax.scan(per_slot, jnp.zeros((twists_here, rows, orbit, bands), jnp.float...]
    reshape x1 -> x0, local copies, waits for them, and re-layouts: 23.6 us -> none  [local(): products.astype(jnp.bfloat16)]
  transfers between devices with their start and end apart: 5 -> 4, of which waited for: 3 -> 3; matrix products, arithmetic and copies ran while one was open for 1% -> 5% of each run, Pallas kernels for 0% -> 6%
where the time goes in v1:
time: 411 us
  blocking collectives  233 us (57%)
  Pallas kernels  64.8 us (16%)
  waiting for transfers between devices  59.6 us (15%)
  matrix products  19.4 us (5%)
  between operations  14.1 us (3%)
  local copies, waits for them, and re-layouts  10 us (2%)
  starting transfers between devices  8.91 us (2%)
    psum x1, blocking collectives, local(): energies = lax.psum(partial, 'space')  173 us
    all_to_all x1, blocking collectives, local(): parts = lax.all_to_all(summed, 'space', 0, 0, tiled=True)  57.7 us
    ppermute x1, waiting for transfers between devices, local(): following = lax.ppermute(own, 'space', down)  45.1 us
    pallas_call x1, Pallas kernels, energy_share(): pl.pallas_call(functools.partial(energy_kernel, factor=factor), grid_spec...  39.4 us
    pallas_call x1, Pallas kernels, grad_blocks(): pl.pallas_call(functools.partial(grad_blocks_kernel, factor=factor), grid...  25.3 us
    dot_general x1, matrix products, local(): lax.dot_general(blocks, theirs, over_edges, preferred_element_type=jnp.fl...  10.2 us
    unnamed x18, local copies, waits for them, and re-layouts  10 us
    dot_general x1, matrix products, local(): lax.dot_general(blocks, mine, over_edges, preferred_element_type=jnp.floa...  9.25 us
  transfers between devices with their start and end apart: 4, of which 3 were waited for; matrix products, arithmetic and copies ran while one was open for 5% of the time, Pallas kernels for 6%

profile of v1, /device:TPU:0, one launch (start us, length us, event | category | flops | bytes accessed | tf_op | source)
XLA Modules:
  0.0 410.9 jit_solution(3875035622335791381)
XLA Ops:
  7.2 0.0 all-gather.2.cloned.1.call-start
  7.2 0.7 all-gather.2.cloned.1.call-update
  7.9 8.9 %collective-permute-start.1 = (bf16[64,64,256]{2,1,0:T(8,128)(2,1)}, bf16[64,64,256]{2,1,0:T(8,128)(2,1)S(1)}, u32[]{:S(2)}, u32[]{:S(2)}) collective-permute-start(bf16[64,64,256]{2,1,0:T(8,128)(2,1)} %bitcast.25), channel_id=1, source_target_pairs={{1,0},{2,1},{3,2},{4,3},{5,4},{6,5},{7,6},{8,7},{9,8},{10,9},{11,1... | collective-permute-start | bytes 6291464 | tf_op jit(solution)/shard_map/ppermute | solution.py:210
  16.8 0.0 collective-permute-start
  16.8 0.8 copy.8
  17.5 0.7 fusion.7.index
  18.3 45.1 %collective-permute-done.1.following = bf16[64,64,256]{2,1,0:T(8,128)(2,1)S(1)} collective-permute-done((bf16[64,64,256]{2,1,0:T(8,128)(2,1)}, bf16[64,64,256]{2,1,0:T(8,128)(2,1)S(1)}, u32[]{:S(2)}, u32[]{:S(2)}) %collective-permute-start.1) | collective-permute-done | bytes 2097184 | tf_op jit(solution)/shard_map/ppermute | solution.py:210
  63.4 0.0 copy-start.4
  63.4 1.3 copy-done.4
  64.7 6.3 %collective-permute-done.prev = bf16[64,64,256]{2,1,0:T(8,128)(2,1)} collective-permute-done((bf16[64,64,256]{2,1,0:T(8,128)(2,1)}, bf16[64,64,256]{2,1,0:T(8,128)(2,1)}, u32[]{:S(2)}, u32[]{:S(2)}) %collective-permute-start) | collective-permute-done | bytes 2097184 | tf_op jit(solution)/shard_map/ppermute | solution.py:209
  71.0 0.0 copy-start
  71.0 1.6 copy-done
  72.6 0.0 copy-start.5
  72.6 1.8 copy-done.5
  74.4 0.0 copy-start.7
  74.4 0.7 copy-done.7
  75.0 0.0 copy-start.2
  75.1 25.3 %grad_blocks.1 = bf16[1024,4096]{1,0:T(8,128)(2,1)} custom-call(s32[64,16]{1,0:T(8,128)S(1)} %fusion.7.index, bf16[64,64,256]{2,1,0:T(8,128)(2,1)} %collective-permute-done.prev, bf16[64,64,256]{2,1,0:T(8,128)(2,1)S(1)} %bitcast.27, bf16[64,64,256]{2,1,0:T(8,128)(2,1)S(1)} %copy-done.5, f32[1,256]{1,0:T(1,128)S(1)} %copy-done.7), custom_call_target="tpu_custom_call" | custom-call | flops 8589934592 | bytes 16777216 | tf_op jit(solution)/shard_map/grad_blocks/pallas_call | solution.py:94
  100.4 0.0 copy-done.2
  100.4 10.2 %convolution_convert_fusion = bf16[4096,512]{1,0:T(8,128)(2,1)} fusion(bf16[1024,4096]{1,0:T(8,128)(2,1)} %grad_blocks.1, bf16[1024,1024]{1,0:T(8,128)(2,1)S(1)} %bitcast.29, s32[]{:T(128)S(6)} %select_n.31), kind=kOutput, calls=%fused_computation.2 | convolution fusion | flops 4297064448 | bytes 13631492 | tf_op jit(solution)/shard_map/dot_general | solution.py:223
  110.6 0.0 collective-permute-start.2
  110.6 7.5 %collective-permute-done.2 = bf16[4096,512]{1,0:T(8,128)(2,1)} collective-permute-done((bf16[4096,512]{1,0:T(8,128)(2,1)}, bf16[4096,512]{1,0:T(8,128)(2,1)}, u32[]{:S(2)}, u32[]{:S(2)}) %collective-permute-start.2) | collective-permute-done | bytes 4194336 | tf_op jit(solution)/shard_map/ppermute | solution.py:224
  118.1 9.3 %add_convert_fusion = bf16[4096,512]{1,0:T(8,128)(2,1)S(1)} fusion(bf16[4096,512]{1,0:T(8,128)(2,1)} %collective-permute-done.2, bf16[1024,4096]{1,0:T(8,128)(2,1)} %grad_blocks.1, bf16[1024,1024]{1,0:T(8,128)(2,1)S(1)} %bitcast.30, s32[]{:T(128)S(6)} %select_n.30), kind=kOutput, calls=%fused_computation.1 | convolution fusion | flops 4301258752 | bytes 17825796 | tf_op jit(solution)/shard_map/dot_general | solution.py:225
  127.3 57.7 %all_to_all.9 = bf16[64,64,512]{2,1,0:T(8,128)(2,1)S(1)} all-to-all(bf16[64,64,512]{2,1,0:T(8,128)(2,1)S(1)} %bitcast.32), channel_id=1, replica_groups=mesh['dp'=2,'space'=64] {'space'}, dimensions={0} | all-to-all | bytes 8388608 | tf_op jit(solution)/shard_map/all_to_all | solution.py:227
  185.0 0.6 convert_reduce_fusion
  185.7 2.0 all_gather.7
  187.6 0.0 copy-done.1
  187.7 1.6 copy-done.3
  189.2 1.6 copy-done.6
  190.8 39.4 %energy_share.1 = f32[1,256]{1,0:T(1,128)S(1)} custom-call(s32[64,16]{1,0:T(8,128)S(1)} %fusion.7.index, bf16[64,64,256]{2,1,0:T(8,128)(2,1)} %collective-permute-done.prev, bf16[64,64,256]{2,1,0:T(8,128)(2,1)S(1)} %bitcast.28, bf16[64,64,256]{2,1,0:T(8,128)(2,1)S(1)} %copy-done.6, bf16[1024,1024]{1,0:T(8,128)(2,1)S(1)} %bitcast.31, ...), custom_call_target="tpu_custom_call" | custom-call | flops 17179869184 | bytes 16777216 | tf_op jit(solution)/shard_map/energy_share/pallas_call | solution.py:174
  230.3 173.1 %psum.7 = f32[1,256]{1,0:T(1,128)} all-reduce(f32[1,256]{1,0:T(1,128)S(1)} %energy_share.1), channel_id=1, replica_groups=mesh['dp'=2,'space'=64] {'space'}, use_global_device_ids=true, to_apply=%region_0.1 | all-reduce | flops 256 | bytes 2048 | tf_op jit(solution)/shard_map/psum | solution.py:232
  403.3 0.7 copy.10
  (4 shorter events, 0.0 us)
Async XLA Ops:
  7.2 180.5 %all-gather.2.cloned.1.call-start = ((), (), s32[]{:S(2)}) async-start(), calls=%async_computation.1 | async-start | bytes 8519680 | tf_op jit(solution)/shard_map/all_gather | solution.py:211
  7.9 55.5 %collective-permute-start.1 = (bf16[64,64,256]{2,1,0:T(8,128)(2,1)}, bf16[64,64,256]{2,1,0:T(8,128)(2,1)S(1)}, u32[]{:S(2)}, u32[]{:S(2)}) collective-permute-start(bf16[64,64,256]{2,1,0:T(8,128)(2,1)} %bitcast.25), channel_id=1, source_target_pairs={{1,0},{2,1},{3,2},{4,3},{5,4},{6,5},{7,6},{8,7},{9,8},{10,9},{11,1... | collective-permute-start | bytes 6291464 | tf_op jit(solution)/shard_map/ppermute | solution.py:210
  16.8 54.3 %collective-permute-start = (bf16[64,64,256]{2,1,0:T(8,128)(2,1)}, bf16[64,64,256]{2,1,0:T(8,128)(2,1)}, u32[]{:S(2)}, u32[]{:S(2)}) collective-permute-start(bf16[64,64,256]{2,1,0:T(8,128)(2,1)} %bitcast.26), channel_id=1, source_target_pairs={{0,1},{1,2},{2,3},{3,4},{4,5},{5,6},{6,7},{7,8},{8,9},{9,10},{10,1... | collective-permute-start | bytes 6291464 | tf_op jit(solution)/shard_map/ppermute | solution.py:209
  63.4 1.3 copy-start.4
  71.0 1.6 copy-start
  72.6 1.8 copy-start.5
  74.4 0.7 copy-start.7
  75.0 25.4 %copy-start.2 = (bf16[1,64,16,1024]{3,2,1,0:T(8,128)(2,1)S(1)}, bf16[1,64,16,1024]{3,2,1,0:T(8,128)(2,1)}, u32[]{:S(2)}) copy-start(bf16[1,64,16,1024]{3,2,1,0:T(8,128)(2,1)} %param.6) | copy-start | bytes 6291460
  110.6 7.5 %collective-permute-start.2 = (bf16[4096,512]{1,0:T(8,128)(2,1)}, bf16[4096,512]{1,0:T(8,128)(2,1)}, u32[]{:S(2)}, u32[]{:S(2)}) collective-permute-start(bf16[4096,512]{1,0:T(8,128)(2,1)} %convolution_convert_fusion), channel_id=1, source_target_pairs={{0,64},{64,0},{1,65},{65,1},{2,66},{66,2},{3,67},{67,3},{4,68},{68... | collective-permute-start | bytes 12582920 | tf_op jit(solution)/shard_map/ppermute | solution.py:224
  185.0 2.6 copy-start.1
  187.7 1.6 copy-start.3
  189.2 1.6 copy-start.6
Sparse Core Ops, SparseCore 0:
  10.8 110.1 all-gather.1

commit v2 on v1

--- a/solution.py
+++ b/solution.py
@@ -197,7 +197,7 @@
     )(index, prev, own, following, edges, weights)
 
 
-def local(features, psi, neighbors, counts, occupation, weights):
+def step(features, psi, neighbors, counts, occupation, weights):
     nspace = lax.axis_size("space")
     myself = lax.axis_index("space")
     core = lax.axis_index("dp")
@@ -224,12 +224,14 @@
     other = lax.ppermute(send.astype(jnp.bfloat16), "dp", [(0, 1), (1, 0)])
     keep = lax.dot_general(blocks, mine, over_edges, preferred_element_type=jnp.float32)
     summed = (keep + other.astype(jnp.float32)).astype(jnp.bfloat16)
+    summed, late_index = lax.optimization_barrier((summed, index))
     parts = lax.all_to_all(summed, "space", 0, 0, tiled=True)
     share = jnp.sum(parts.reshape(nspace, ORB, half).astype(jnp.float32), axis=0)
     gradient = lax.all_gather(share, "dp", axis=1, tiled=True)
 
-    partial = energy_share(index, prev, own, following, edges, gathered, factor)
-    energies = lax.psum(partial, "space")
+    partial = energy_share(late_index, prev, own, following, edges, gathered, factor)
+    copies = jnp.broadcast_to(partial, (nspace, BANDS))
+    energies = jnp.sum(lax.all_to_all(copies, "space", 0, 0, tiled=True), axis=0, keepdims=True)
     return (energies, gradient)
 
 
@@ -243,7 +245,7 @@
         P(None, "space"),
     )
     return jax.shard_map(
-        local,
+        step,
         mesh=mesh,
         in_specs=placed,
         out_specs=(P("dp", None), P("space", None)),

time: 411 us -> 253 us (0.62)
  blocking collectives: 233 us -> 63.9 us
  starting transfers between devices: 8.91 us -> 14.8 us
    psum x1 -> x0, blocking collectives: 173 us -> none  [local(): energies = lax.psum(partial, 'space')]
    all_to_all x0 -> x1, waiting for transfers between devices: none -> 7.59 us  [step(): lax.all_to_all(copies, 'space', 0, 0, tiled=True)]
    all_to_all x0 -> x1, starting transfers between devices: none -> 5.79 us  [step(): lax.all_to_all(copies, 'space', 0, 0, tiled=True)]
    ppermute x3, waiting for transfers between devices: 58.9 us -> 53.2 us  [the longest x1 45.7 us: step(): prev = lax.ppermute(own, 'space', up)]
    all_to_all x1, blocking collectives: 57.7 us -> 61.9 us  [step(): parts = lax.all_to_all(summed, 'space', 0, 0, tiled=True)]
  transfers between devices with their start and end apart: 4 -> 5, of which waited for: 3 -> 3; matrix products, arithmetic and copies ran while one was open for 5% -> 9% of each run, Pallas kernels for 6% -> 10%
where the time goes in v2:
time: 253 us
  Pallas kernels  65.5 us (26%)
  blocking collectives  63.9 us (25%)
  waiting for transfers between devices  61.5 us (24%)
  matrix products  19.3 us (8%)
  starting transfers between devices  14.8 us (6%)
  between operations  14.1 us (6%)
  local copies, waits for them, and re-layouts  11.5 us (5%)
    all_to_all x1, blocking collectives, step(): parts = lax.all_to_all(summed, 'space', 0, 0, tiled=True)  61.9 us
    ppermute x1, waiting for transfers between devices, step(): prev = lax.ppermute(own, 'space', up)  45.7 us
    pallas_call x1, Pallas kernels, energy_share(): pl.pallas_call(functools.partial(energy_kernel, factor=factor), grid_spec...  39.9 us
    pallas_call x1, Pallas kernels, grad_blocks(): pl.pallas_call(functools.partial(grad_blocks_kernel, factor=factor), grid...  25.7 us
    unnamed x18, local copies, waits for them, and re-layouts  10.8 us
    dot_general x1, matrix products, step(): lax.dot_general(blocks, theirs, over_edges, preferred_element_type=jnp.fl...  9.83 us
    dot_general x1, matrix products, step(): lax.dot_general(blocks, mine, over_edges, preferred_element_type=jnp.floa...  9.51 us
    all_to_all x1, waiting for transfers between devices, step(): lax.all_to_all(copies, 'space', 0, 0, tiled=True)  7.59 us
  transfers between devices with their start and end apart: 5, of which 3 were waited for; matrix products, arithmetic and copies ran while one was open for 9% of the time, Pallas kernels for 10%

profile of v2, /device:TPU:0, one launch (start us, length us, event | category | flops | bytes accessed | tf_op | source)
XLA Modules:
  0.0 252.5 jit_solution(2994281641106139609)
XLA Ops:
  7.2 0.0 all-gather.2.cloned.1.call-start
  7.2 0.7 all-gather.2.cloned.1.call-update
  7.9 1.7 collective-permute-start
  9.6 7.3 %collective-permute-start.1 = (bf16[64,64,256]{2,1,0:T(8,128)(2,1)}, bf16[64,64,256]{2,1,0:T(8,128)(2,1)}, u32[]{:S(2)}, u32[]{:S(2)}) collective-permute-start(bf16[64,64,256]{2,1,0:T(8,128)(2,1)} %bitcast.29), channel_id=1, source_target_pairs={{1,0},{2,1},{3,2},{4,3},{5,4},{6,5},{7,6},{8,7},{9,8},{10,9},{11,1... | collective-permute-start | bytes 6291464 | tf_op jit(solution)/shard_map/ppermute | solution.py:210
  16.8 0.8 copy.10
  17.6 0.7 fusion.7.index
  18.4 45.7 %collective-permute-done.prev = bf16[64,64,256]{2,1,0:T(8,128)(2,1)S(1)} collective-permute-done((bf16[64,64,256]{2,1,0:T(8,128)(2,1)}, bf16[64,64,256]{2,1,0:T(8,128)(2,1)S(1)}, u32[]{:S(2)}, u32[]{:S(2)}) %collective-permute-start) | collective-permute-done | bytes 2097184 | tf_op jit(solution)/shard_map/ppermute | solution.py:209
  64.0 0.0 copy-start.4
  64.0 1.3 copy-done.4
  65.4 0.0 collective-permute-done.1.following
  65.4 1.6 copy-done
  67.0 1.6 copy-done.5
  68.5 0.7 copy-done.7
  69.2 25.7 %grad_blocks.1 = bf16[1024,4096]{1,0:T(8,128)(2,1)} custom-call(s32[64,16]{1,0:T(8,128)S(1)} %fusion.7.index, bf16[64,64,256]{2,1,0:T(8,128)(2,1)S(1)} %copy-done.5, bf16[64,64,256]{2,1,0:T(8,128)(2,1)S(1)} %bitcast.30, bf16[64,64,256]{2,1,0:T(8,128)(2,1)} %collective-permute-done.1.following, f32[1,256]{1,0:T(1,128)S(1)} %copy-done.7), custom_call_target="tpu_custom_call" | custom-call | flops 8589934592 | bytes 16777216 | tf_op jit(solution)/shard_map/grad_blocks/pallas_call | solution.py:94
  94.9 0.0 copy-done.2
  94.9 9.8 %convolution_convert_fusion = bf16[4096,512]{1,0:T(8,128)(2,1)} fusion(bf16[1024,4096]{1,0:T(8,128)(2,1)} %grad_blocks.1, bf16[1024,1024]{1,0:T(8,128)(2,1)S(1)} %bitcast.32, s32[]{:T(128)S(6)} %select_n.31), kind=kOutput, calls=%fused_computation.2 | convolution fusion | flops 4297064448 | bytes 13631492 | tf_op jit(solution)/shard_map/dot_general | solution.py:223
  104.7 0.0 collective-permute-start.2
  104.7 7.5 %collective-permute-done.2 = bf16[4096,512]{1,0:T(8,128)(2,1)} collective-permute-done((bf16[4096,512]{1,0:T(8,128)(2,1)}, bf16[4096,512]{1,0:T(8,128)(2,1)}, u32[]{:S(2)}, u32[]{:S(2)}) %collective-permute-start.2) | collective-permute-done | bytes 4194336 | tf_op jit(solution)/shard_map/ppermute | solution.py:224
  112.2 9.5 %add_convert_fusion = bf16[4096,512]{1,0:T(8,128)(2,1)S(1)} fusion(bf16[4096,512]{1,0:T(8,128)(2,1)} %collective-permute-done.2, bf16[1024,4096]{1,0:T(8,128)(2,1)} %grad_blocks.1, bf16[1024,1024]{1,0:T(8,128)(2,1)S(1)} %bitcast.33, s32[]{:T(128)S(6)} %select_n.30), kind=kOutput, calls=%fused_computation.1 | convolution fusion | flops 4301258752 | bytes 17825796 | tf_op jit(solution)/shard_map/dot_general | solution.py:225
  121.8 61.9 %all_to_all.15 = bf16[64,64,512]{2,1,0:T(8,128)(2,1)S(1)} all-to-all(bf16[64,64,512]{2,1,0:T(8,128)(2,1)S(1)} %bitcast.35), channel_id=1, replica_groups=mesh['dp'=2,'space'=64] {'space'}, dimensions={0} | all-to-all | bytes 8388608 | tf_op jit(solution)/shard_map/all_to_all | solution.py:228
  183.6 0.6 convert_reduce_fusion
  184.3 0.0 all-gather.2.cloned.1.call-done.weights
  184.3 0.9 copy-done.1
  185.2 1.6 copy-done.3
  186.8 1.6 copy-done.6
  188.4 39.9 %energy_share.1 = f32[1,256]{1,0:T(1,128)S(1)} custom-call(s32[64,16]{1,0:T(8,128)S(1)} %fusion.7.index, bf16[64,64,256]{2,1,0:T(8,128)(2,1)S(1)} %copy-done.6, bf16[64,64,256]{2,1,0:T(8,128)(2,1)S(1)} %bitcast.31, bf16[64,64,256]{2,1,0:T(8,128)(2,1)} %collective-permute-done.1.following, bf16[1024,1024]{1,0:T(8,128)(2,1)S(1)} %bitcast.34, ...), custom_call_target="tpu_custom_call" | custom-call | flops 17179869184 | bytes 16777216 | tf_op jit(solution)/shard_map/energy_share/pallas_call | solution.py:174
  228.3 0.7 broadcast_in_dim.13
  228.9 5.8 %all-to-all-start = ((f32[64,1,256]{2,1,0:T(1,128)}), f32[64,1,256]{2,1,0:T(1,128)S(1)}, u32[]{:S(2)}, u32[]{:S(2)}) async-start(f32[64,1,256]{2,1,0:T(1,128)} %broadcast_in_dim.13), calls=%async_computation | async-start | bytes 131072 | tf_op jit(solution)/shard_map/all_to_all | solution.py:234
  234.7 2.0 all_gather.7
  236.7 7.6 %all-to-all-done = f32[64,1,256]{2,1,0:T(1,128)S(1)} async-done(((f32[64,1,256]{2,1,0:T(1,128)}), f32[64,1,256]{2,1,0:T(1,128)S(1)}, u32[]{:S(2)}, u32[]{:S(2)}) %all-to-all-start) | async-done | bytes 65568 | tf_op jit(solution)/shard_map/all_to_all | solution.py:234
  244.3 0.7 reduce_sum.18
  245.0 0.7 copy.14
  (7 shorter events, 0.0 us)
Async XLA Ops:
  7.2 177.1 %all-gather.2.cloned.1.call-start = ((), (), s32[]{:S(2)}) async-start(), calls=%async_computation.2 | async-start | bytes 8519680 | tf_op jit(solution)/shard_map/all_gather | solution.py:211
  7.9 56.1 %collective-permute-start = (bf16[64,64,256]{2,1,0:T(8,128)(2,1)}, bf16[64,64,256]{2,1,0:T(8,128)(2,1)S(1)}, u32[]{:S(2)}, u32[]{:S(2)}) collective-permute-start(bf16[64,64,256]{2,1,0:T(8,128)(2,1)} %bitcast.28), channel_id=1, source_target_pairs={{0,1},{1,2},{2,3},{3,4},{4,5},{5,6},{6,7},{7,8},{8,9},{9,10},{10,1... | collective-permute-start | bytes 6291464 | tf_op jit(solution)/shard_map/ppermute | solution.py:209
  9.6 55.8 %collective-permute-start.1 = (bf16[64,64,256]{2,1,0:T(8,128)(2,1)}, bf16[64,64,256]{2,1,0:T(8,128)(2,1)}, u32[]{:S(2)}, u32[]{:S(2)}) collective-permute-start(bf16[64,64,256]{2,1,0:T(8,128)(2,1)} %bitcast.29), channel_id=1, source_target_pairs={{1,0},{2,1},{3,2},{4,3},{5,4},{6,5},{7,6},{8,7},{9,8},{10,9},{11,1... | collective-permute-start | bytes 6291464 | tf_op jit(solution)/shard_map/ppermute | solution.py:210
  64.0 1.3 copy-start.4
  65.4 1.6 copy-start
  66.9 1.6 copy-start.5
  68.5 0.7 copy-start.7
  69.2 25.7 %copy-start.2 = (bf16[1,64,16,1024]{3,2,1,0:T(8,128)(2,1)S(1)}, bf16[1,64,16,1024]{3,2,1,0:T(8,128)(2,1)}, u32[]{:S(2)}) copy-start(bf16[1,64,16,1024]{3,2,1,0:T(8,128)(2,1)} %param.6) | copy-start | bytes 6291460
  104.7 7.5 %collective-permute-start.2 = (bf16[4096,512]{1,0:T(8,128)(2,1)}, bf16[4096,512]{1,0:T(8,128)(2,1)}, u32[]{:S(2)}, u32[]{:S(2)}) collective-permute-start(bf16[4096,512]{1,0:T(8,128)(2,1)} %convolution_convert_fusion), channel_id=1, source_target_pairs={{0,64},{64,0},{1,65},{65,1},{2,66},{66,2},{3,67},{67,3},{4,68},{68... | collective-permute-start | bytes 12582920 | tf_op jit(solution)/shard_map/ppermute | solution.py:224
  183.6 1.6 copy-start.1
  185.2 1.6 copy-start.3
  186.8 1.6 copy-start.6
  228.9 15.4 %all-to-all-start = ((f32[64,1,256]{2,1,0:T(1,128)}), f32[64,1,256]{2,1,0:T(1,128)S(1)}, u32[]{:S(2)}, u32[]{:S(2)}) async-start(f32[64,1,256]{2,1,0:T(1,128)} %broadcast_in_dim.13), calls=%async_computation | async-start | bytes 131072 | tf_op jit(solution)/shard_map/all_to_all | solution.py:234
Sparse Core Ops, SparseCore 0:
  10.8 110.0 all-gather.1

commit v3 on v2

v3 whole, which is shorter than its diff:
```python
import functools
import math

import jax
import jax.numpy as jnp
from jax import lax
from jax.experimental import pallas as pl
from jax.experimental.pallas import tpu as pltpu
from jax.sharding import PartitionSpec as P

ORB = 64
BANDS = 256
SLOTS = 16
TILES = 64
EDGES = TILES * SLOTS
FEAT = 1024
ZERO_TILE = 3 * TILES
CHUNK = 32
ROWS = EDGES // 4
GRAD_PITCH = ROWS + 8
UNROLL = 16
ENERGY_UNROLL = 4
NT = (((1,), (1,)), ((), ()))


def left_lanes(shape):
    return lax.broadcasted_iota(jnp.int32, shape, len(shape) - 1) < ORB


def swap(value):
    return pltpu.roll(value, ORB, value.ndim - 1)


def turn_lanes(strip):
    lane = lax.broadcasted_iota(jnp.int32, strip[0].shape, 1)
    low = lane < 64
    even = lane % 64 < 32
    half = [None] * 4
    for r in range(2):
        half[r] = jnp.where(low, strip[r], pltpu.roll(strip[r + 2], 64, 1))
        half[r + 2] = jnp.where(low, pltpu.roll(strip[r], 64, 1), strip[r + 2])
    turned = [None] * 4
    for r in (0, 2):
        turned[r] = jnp.where(even, half[r], pltpu.roll(half[r + 1], 32, 1))
        turned[r + 1] = jnp.where(even, pltpu.roll(half[r], 96, 1), half[r + 1])
    return turned


def grad_blocks_kernel(
    index, tiles, rows, total, prev, own, following, weighted, out, table, left, strips, sems, *, part, factor
):
    step = pl.program_id(0)

    @pl.when(step == 0)
    def _():
        mine = own.at[:, pl.ds(part * CHUNK, CHUNK), :]
        copies = [
            pltpu.make_async_copy(src, table.at[pl.ds(n * TILES, TILES)], sems.at[n])
            for n, src in enumerate((prev, mine, following))
        ]
        copies.append(pltpu.make_async_copy(weighted, left, sems.at[3]))
        for copy in copies:
            copy.start()
        table[ZERO_TILE] = jnp.zeros((CHUNK, BANDS), jnp.bfloat16)

        def clear(n, carry):
            strips[pl.ds(pl.multiple_of(n * 128, 8), 128), :] = jnp.zeros((128, 128), jnp.float32)
            return carry

        lax.fori_loop(0, ORB * GRAD_PITCH // 128, clear, 0)
        for copy in copies:
            copy.wait()

        def item_body(n, carry):
            at = [rows[n * UNROLL + u] for u in range(UNROLL)]
            who = [tiles[n * UNROLL + u] for u in range(UNROLL)]
            which = [[index[row * 4 + p] for p in range(4)] for row in at]
            products = [
                lax.dot_general(
                    left[who[u]],
                    jnp.concatenate([table[w] for w in which[u]], axis=0),
                    NT,
                    preferred_element_type=jnp.float32,
                )
                for u in range(UNROLL)
            ]
            for row, product in zip(at, products):
                strips[pl.ds(row, ORB, stride=GRAD_PITCH), :] = product
            return carry

        lax.fori_loop(0, (total[0] + UNROLL - 1) // UNROLL, item_body, 0)

    quads = out.shape[1] // 128
    group = 128

    def group_body(g, carry):
        for quad in range(quads):
            base = (step * quads + quad) * 4 * GRAD_PITCH + g * group
            strip = [
                strips[pl.ds(pl.multiple_of(base + r * GRAD_PITCH, 8), group), :] * factor
                for r in range(4)
            ]
            turned = [t.reshape(group // 8, 1, 8, 128) for t in turn_lanes(strip)]
            both = jnp.concatenate(turned, axis=1).reshape(group * 4, 128)
            spot = pl.ds(pl.multiple_of(g * (group * 4), 16), group * 4)
            out[spot, quad * 128 : (quad + 1) * 128] = both.astype(jnp.bfloat16)
        return carry

    lax.fori_loop(0, ROWS // group, group_body, 0)


def grad_blocks(plan, prev, own, following, weighted, part, factor):
    block = 512
    return pl.pallas_call(
        functools.partial(grad_blocks_kernel, part=part, factor=factor),
        grid_spec=pltpu.PrefetchScalarGridSpec(
            num_scalar_prefetch=4,
            grid=(ORB * CHUNK // block,),
            in_specs=[pl.BlockSpec(memory_space=pltpu.MemorySpace.HBM)] * 4,
            out_specs=pl.BlockSpec((EDGES, block), lambda j, *_: (0, j)),
            scratch_shapes=[
                pltpu.VMEM((ZERO_TILE + 1, CHUNK, BANDS), jnp.bfloat16),
                pltpu.VMEM((TILES, ORB, BANDS), jnp.bfloat16),
                pltpu.VMEM((ORB * GRAD_PITCH, 128), jnp.float32),
                pltpu.SemaphoreType.DMA((4,)),
            ],
        ),
        out_shape=jax.ShapeDtypeStruct((EDGES, ORB * CHUNK), jnp.bfloat16),
        compiler_params=pltpu.CompilerParams(vmem_limit_bytes=60 * 2**20),
        cost_estimate=pl.CostEstimate(
            flops=8 * EDGES * ORB * CHUNK * BANDS, bytes_accessed=12 * 2**20, transcendentals=0
        ),
        name="grad_blocks",
    )(*plan, prev, own, following, weighted)


def plan_items(index, counts):
    each = (counts + 3) // 4
    ends = jnp.cumsum(each)
    item = jnp.arange(ROWS, dtype=jnp.int32)
    tile = jnp.sum((ends[None, :] <= item[:, None]).astype(jnp.int32), axis=1)
    hit = lax.broadcasted_iota(jnp.int32, (ROWS, TILES), 1) == tile[:, None]
    start = jnp.sum(jnp.where(hit, (ends - each)[None, :], 0), axis=1)
    used = item < ends[-1]
    rows = jnp.where(used, tile * 4 + item - start, ROWS)
    slots = jnp.concatenate([index.reshape(-1), jnp.full((16,), ZERO_TILE, jnp.int32)])
    return slots, jnp.where(used, tile, 0), rows, ends[-1:]


def energy_kernel(
    index, tiles, rows, total, prev0, prev1, own, following0, following1, edges, weights, out, table, strips, sems, *, factor
):
    step = pl.program_id(0)
    width = weights.shape[0] // ORB
    low = left_lanes((ROWS, 128))
    places = (
        (prev0, table.at[pl.ds(0, TILES), pl.ds(0, CHUNK)]),
        (prev1, table.at[pl.ds(0, TILES), pl.ds(CHUNK, CHUNK)]),
        (own, table.at[pl.ds(TILES, TILES)]),
        (following0, table.at[pl.ds(2 * TILES, TILES), pl.ds(0, CHUNK)]),
        (following1, table.at[pl.ds(2 * TILES, TILES), pl.ds(CHUNK, CHUNK)]),
    )
    copies = [
        pltpu.make_async_copy(src, dst, sems.at[n]) for n, (src, dst) in enumerate(places)
    ]

    @pl.when(step == 0)
    def _():
        for copy in copies:
            copy.start()
        table[ZERO_TILE] = jnp.zeros((ORB, BANDS), jnp.bfloat16)
        for part in (0, 1):
            strips[pl.ds(part * GRAD_PITCH + ROWS, ORB, stride=2 * GRAD_PITCH), :] = jnp.zeros(
                (ORB, 128), jnp.float32
            )

    for pair in range(width // 2):
        product = lax.dot_general(
            edges[...],
            weights[pair * 128 : (pair + 1) * 128, :],
            NT,
            preferred_element_type=jnp.float32,
        ).reshape(TILES // 2, 4, 8, 128)
        base = (step * width + 2 * pair) * (2 * GRAD_PITCH)
        for part in (0, 1):
            front = product[:, 2 * part].reshape(ROWS, 128)
            back = product[:, 2 * part + 1].reshape(ROWS, 128)
            spot = base + part * GRAD_PITCH
            strips[pl.ds(pl.multiple_of(spot, 8), ROWS), :] = jnp.where(low, front, swap(back))
            spot = spot + 2 * GRAD_PITCH
            strips[pl.ds(pl.multiple_of(spot, 8), ROWS), :] = jnp.where(low, swap(front), back)

    @pl.when(step == pl.num_programs(0) - 1)
    def _():
        for copy in copies:
            copy.wait()

        def item_body(n, carry):
            at = [rows[n * ENERGY_UNROLL + u] for u in range(ENERGY_UNROLL)]
            who = [tiles[n * ENERGY_UNROLL + u] for u in range(ENERGY_UNROLL)]
            which = [[index[row * 4 + p] for p in range(4)] for row in at]
            for u in range(ENERGY_UNROLL):
                left = jnp.concatenate(
                    [
                        strips[
                            pl.ds(part * GRAD_PITCH + at[u], ORB, stride=2 * GRAD_PITCH), :
                        ].astype(jnp.bfloat16)
                        for part in (0, 1)
                    ],
                    axis=1,
                )
                right = jnp.concatenate([table[w] for w in which[u]], axis=0)
                applied = jnp.dot(left, right, preferred_element_type=jnp.float32)
                terms = table[TILES + who[u]].astype(jnp.float32) * applied
                carry = carry + jnp.sum(terms.reshape(8, 8, BANDS), axis=0)
            return carry

        trips = (total[0] + ENERGY_UNROLL - 1) // ENERGY_UNROLL
        sums = lax.fori_loop(0, trips, item_body, jnp.zeros((8, BANDS), jnp.float32))
        out[...] = jnp.sum(sums, axis=0, keepdims=True) * factor


def energy_share(plan, prev, own, following, edges, weights, factor):
    block = 512
    return pl.pallas_call(
        functools.partial(energy_kernel, factor=factor),
        grid_spec=pltpu.PrefetchScalarGridSpec(
            num_scalar_prefetch=4,
            grid=(ORB * ORB // block,),
            in_specs=[pl.BlockSpec(memory_space=pltpu.MemorySpace.HBM)] * 5
            + [
                pl.BlockSpec((EDGES, FEAT), lambda j, *_: (0, 0)),
                pl.BlockSpec((block, FEAT), lambda j, *_: (j, 0)),
            ],
            out_specs=pl.BlockSpec((1, BANDS), lambda j, *_: (0, 0)),
            scratch_shapes=[
                pltpu.VMEM((ZERO_TILE + 1, ORB, BANDS), jnp.bfloat16),
                pltpu.VMEM((2 * ORB * GRAD_PITCH, 128), jnp.float32),
                pltpu.SemaphoreType.DMA((5,)),
            ],
        ),
        out_shape=jax.ShapeDtypeStruct((1, BANDS), jnp.float32),
        compiler_params=pltpu.CompilerParams(vmem_limit_bytes=60 * 2**20),
        cost_estimate=pl.CostEstimate(
            flops=2 * EDGES * ORB * ORB * (FEAT + BANDS * 4), bytes_accessed=16 * 2**20, transcendentals=0
        ),
        name="energy_share",
    )(*plan, *prev, own, *following, edges, weights)


def step(features, psi, neighbors, counts, occupation, weights):
    nspace = lax.axis_size("space")
    myself = lax.axis_index("space")
    core = lax.axis_index("dp")
    factor = 1.0 / math.sqrt(TILES * nspace * SLOTS)
    own = psi.reshape(TILES, ORB, BANDS)
    up = [(i, (i + 1) % nspace) for i in range(nspace)]
    down = [(j, i) for i, j in up]
    prev0 = lax.ppermute(own[:, :CHUNK], "space", up)
    following0 = lax.ppermute(own[:, :CHUNK], "space", down)
    gathered = lax.all_gather(weights.T, "space", axis=0, tiled=True)
    second, prev0, following0 = lax.optimization_barrier((own[:, CHUNK:], prev0, following0))
    prev1 = lax.ppermute(second, "space", up)
    following1 = lax.ppermute(second, "space", down)
    prev, following = (prev0, prev1), (following0, following1)

    where = neighbors.reshape(TILES, SLOTS)
    placed = (where // TILES - myself + 1 + nspace) % nspace * TILES + where % TILES
    slot = lax.broadcasted_iota(jnp.int32, (TILES, SLOTS), 1)
    used = counts.reshape(TILES)
    plan = plan_items(jnp.where(slot < used[:, None], placed, ZERO_TILE), used)
    weighted = (own.astype(jnp.float32) * occupation).astype(jnp.bfloat16)
    edges = (
        features.reshape(TILES // 2, 2, 4, 4, FEAT).transpose(0, 3, 1, 2, 4).reshape(EDGES, FEAT)
    )

    half = FEAT // 2
    theirs = lax.dynamic_slice_in_dim(edges, (1 - core) * half, half, 1)
    mine = lax.dynamic_slice_in_dim(edges, core * half, half, 1)
    over_edges = (((0,), (0,)), ((), ()))
    shares = []
    for part in (0, 1):
        blocks = grad_blocks(plan, prev[part], own, following[part], weighted, part, factor)
        send = lax.dot_general(blocks, theirs, over_edges, preferred_element_type=jnp.float32)
        other = lax.ppermute(send.astype(jnp.bfloat16), "dp", [(0, 1), (1, 0)])
        keep = lax.dot_general(blocks, mine, over_edges, preferred_element_type=jnp.float32)
        summed = (keep + other.astype(jnp.float32)).astype(jnp.bfloat16)
        parts = lax.all_to_all(summed, "space", 0, 0, tiled=True)
        shares.append(jnp.sum(parts.reshape(nspace, CHUNK, half).astype(jnp.float32), axis=0))
    gradient = lax.all_gather(jnp.concatenate(shares, axis=0), "dp", axis=1, tiled=True)

    partial = energy_share(plan, prev, own, following, edges, gathered, factor)
    copies = jnp.broadcast_to(partial, (nspace, BANDS))
    energies = jnp.sum(lax.all_to_all(copies, "space", 0, 0, tiled=True), axis=0, keepdims=True)
    return (energies, gradient)


def solution(mesh):
    placed = (
        P("dp", "space", None, None),
        P("dp", "space", None, None),
        P("dp", "space", None),
        P("dp", "space"),
        P("dp", None),
        P(None, "space"),
    )
    return jax.shard_map(
        step,
        mesh=mesh,
        in_specs=placed,
        out_specs=(P("dp", None), P("space", None)),
        check_vma=False,
    )
```

time: 253 us -> 285 us (1.13)
  blocking collectives: 63.9 us -> 1.99 us
  waiting for transfers between devices: 61.5 us -> 117 us
  starting transfers between devices: 14.8 us -> 36.8 us
  matrix products: 19.3 us -> 25.4 us
  local copies, waits for them, and re-layouts: 11.5 us -> 16.6 us
  other arithmetic: 2.02 us -> 6.44 us
    all_to_all x1 -> x0, blocking collectives: 61.9 us -> none  [step(): parts = lax.all_to_all(summed, 'space', 0, 0, tiled=True)]
    all_to_all x0 -> x2, waiting for transfers between devices: none -> 54 us  [step(): parts = lax.all_to_all(summed, 'space', 0, 0, tiled=True)]
    all_to_all x0 -> x2, starting transfers between devices: none -> 15.9 us  [step(): parts = lax.all_to_all(summed, 'space', 0, 0, tiled=True)]
    reshape x0 -> x4, local copies, waits for them, and re-layouts: none -> 9.4 us  [the longest x3 9.32 us: step(): features.reshape(TILES // 2, 2, 4, 4, FEAT).transpose(0, 3, 1, 2, 4)]
    ppermute x2 -> x4, waiting for transfers between devices: 45.7 us -> 54.7 us  [the longest x1 38.8 us: step(): prev1 = lax.ppermute(second, 'space', up)]
    unnamed x18 -> x14, local copies, waits for them, and re-layouts: 10.8 us -> 1.85 us
    ppermute x1 -> x2, waiting for transfers between devices: 7.5 us -> 0.01 us  [step(): other = lax.ppermute(send.astype(jnp.bfloat16), 'dp', [(0, 1), (1, 0)])]
    ppermute x2 -> x4, starting transfers between devices: 8.95 us -> 16.3 us  [the longest x1 7.45 us: step(): following1 = lax.ppermute(second, 'space', down)]
  transfers between devices with their start and end apart: 5 -> 10, of which waited for: 3 -> 6; matrix products, arithmetic and copies ran while one was open for 9% -> 16% of each run, Pallas kernels for 10% -> 11%
where the time goes in v3:
time: 285 us
  waiting for transfers between devices  117 us (41%)
  Pallas kernels  66.2 us (23%)
  starting transfers between devices  36.8 us (13%)
  matrix products  25.4 us (9%)
  local copies, waits for them, and re-layouts  16.6 us (6%)
  between operations  14.2 us (5%)
  other arithmetic  6.44 us (2%)
    all_to_all x2, waiting for transfers between devices, step(): parts = lax.all_to_all(summed, 'space', 0, 0, tiled=True)  54 us
    ppermute x1, waiting for transfers between devices, step(): prev1 = lax.ppermute(second, 'space', up)  38.8 us
    pallas_call x1, Pallas kernels, energy_share(): pl.pallas_call(functools.partial(energy_kernel, factor=factor), grid_spec...  34.9 us
    pallas_call x2, Pallas kernels, grad_blocks(): pl.pallas_call(functools.partial(grad_blocks_kernel, part=part, factor=fa...  31.3 us
    all_to_all x2, starting transfers between devices, step(): parts = lax.all_to_all(summed, 'space', 0, 0, tiled=True)  15.9 us
    dot_general x2, matrix products, step(): lax.dot_general(blocks, mine, over_edges, preferred_element_type=jnp.floa...  13.5 us
    dot_general x2, matrix products, step(): lax.dot_general(blocks, theirs, over_edges, preferred_element_type=jnp.fl...  11.9 us
    ppermute x1, waiting for transfers between devices, step(): prev0 = lax.ppermute(own[:, :CHUNK], 'space', up)  10.4 us
  transfers between devices with their start and end apart: 10, of which 6 were waited for; matrix products, arithmetic and copies ran while one was open for 16% of the time, Pallas kernels for 11%

profile of v3, /device:TPU:0, one launch (start us, length us, event | category | flops | bytes accessed | tf_op | source)
XLA Modules:
  0.0 284.6 jit_solution(9372164799064332045)
XLA Ops:
  7.2 0.7 all-gather.2.cloned.1.call-update
  7.9 2.7 fusion.17
  10.7 1.6 collective-permute-start
  12.3 7.2 %collective-permute-start.1 = (bf16[64,32,256]{2,1,0:T(8,128)(2,1)}, bf16[64,32,256]{2,1,0:T(8,128)(2,1)}, u32[]{:S(2)}, u32[]{:S(2)}) collective-permute-start(bf16[64,32,256]{2,1,0:T(8,128)(2,1)} %get-tuple-element.8), channel_id=1, source_target_pairs={{1,0},{2,1},{3,2},{4,3},{5,4},{6,5},{7,6},{8,7},{9,8},{10,9},{11,1... | collective-permute-start | bytes 3145736 | tf_op jit(solution)/shard_map/ppermute | solution.py:260
  20.7 2.7 reshape.108
  23.5 2.5 copy.22
  26.0 4.1 %reshape.109.edges = bf16[1024,1024]{1,0:T(8,128)(2,1)} reshape(bf16[32,4,2,4,1024]{4,3,2,1,0:T(4,128)(2,1)} %bitcast.38) | data formatting | bytes 4194304 | tf_op jit(solution)/shard_map/reshape | solution.py:274
  30.9 1.2 subtract_select_fusion
  32.1 1.8 multiply_convert_fusion.weighted
  33.9 10.4 %collective-permute-done.prev0.prev = bf16[64,32,256]{2,1,0:T(8,128)(2,1)} collective-permute-done((bf16[64,32,256]{2,1,0:T(8,128)(2,1)}, bf16[64,32,256]{2,1,0:T(8,128)(2,1)}, u32[]{:S(2)}, u32[]{:S(2)}) %collective-permute-start) | collective-permute-done | bytes 1048608 | tf_op jit(solution)/shard_map/ppermute | solution.py:259
  44.2 15.7 %grad_blocks.2 = bf16[1024,2048]{1,0:T(8,128)(2,1)} custom-call(s32[1040]{0:T(1024)} %concatenate.6.index, s32[256]{0:T(256)} %get-tuple-element.11.tiles, s32[256]{0:T(256)} %get-tuple-element.10.rows, s32[1]{0:T(128)} %bitcast.4.total, bf16[64,32,256]{2,1,0:T(8,128)(2,1)} %collective-permute-done.prev0.prev, bf16[64,64,256]{2,1,0:T(8,128)(2,1)} %bitcast.35, ...), custom_call_target="tpu_custom_call" | custom-call | flops 4294967296 | bytes 12582912 | tf_op jit(solution)/shard_map/grad_blocks/pallas_call | solution.py:114
  60.0 5.9 %convolution_convert_fusion.1 = bf16[2048,512]{1,0:T(8,128)(2,1)} fusion(bf16[1024,2048]{1,0:T(8,128)(2,1)} %grad_blocks.2, bf16[1024,1024]{1,0:T(8,128)(2,1)S(1)} %copy-done.1, s32[]{:T(128)S(6)} %select_n.66), kind=kOutput, calls=%fused_computation.6 | convolution fusion | flops 2148532224 | bytes 7340036 | tf_op jit(solution)/shard_map/dot_general | solution.py:284
  65.9 7.5 %collective-permute-start.3 = (bf16[64,32,256]{2,1,0:T(8,128)(2,1)S(1)}, bf16[64,32,256]{2,1,0:T(8,128)(2,1)}, u32[]{:S(2)}, u32[]{:S(2)}) collective-permute-start(bf16[64,32,256]{2,1,0:T(8,128)(2,1)S(1)} %get-tuple-element.6), channel_id=1, source_target_pairs={{1,0},{2,1},{3,2},{4,3},{5,4},{6,5},{7,6},{8,7},{9,8},{10,9},{11,1... | collective-permute-start | bytes 3145736 | tf_op jit(solution)/shard_map/ppermute | solution.py:264
  73.4 38.8 %collective-permute-done.2.prev1.prev = bf16[64,32,256]{2,1,0:T(8,128)(2,1)S(1)} collective-permute-done((bf16[64,32,256]{2,1,0:T(8,128)(2,1)S(1)}, bf16[64,32,256]{2,1,0:T(8,128)(2,1)S(1)}, u32[]{:S(2)}, u32[]{:S(2)}) %collective-permute-start.2) | collective-permute-done | bytes 1048608 | tf_op jit(solution)/shard_map/ppermute | solution.py:263
  112.2 1.0 copy-done.5
  113.2 5.5 %collective-permute-done.3.following1.following = bf16[64,32,256]{2,1,0:T(8,128)(2,1)} collective-permute-done((bf16[64,32,256]{2,1,0:T(8,128)(2,1)S(1)}, bf16[64,32,256]{2,1,0:T(8,128)(2,1)}, u32[]{:S(2)}, u32[]{:S(2)}) %collective-permute-start.3) | collective-permute-done | bytes 1048608 | tf_op jit(solution)/shard_map/ppermute | solution.py:264
  118.7 15.6 %grad_blocks.3 = bf16[1024,2048]{1,0:T(8,128)(2,1)} custom-call(s32[1040]{0:T(1024)} %concatenate.6.index, s32[256]{0:T(256)} %get-tuple-element.11.tiles, s32[256]{0:T(256)} %get-tuple-element.10.rows, s32[1]{0:T(128)} %bitcast.4.total, bf16[64,32,256]{2,1,0:T(8,128)(2,1)} %copy-done.5, bf16[64,64,256]{2,1,0:T(8,128)(2,1)} %bitcast.36, ...), custom_call_target="tpu_custom_call" | custom-call | flops 4294967296 | bytes 12582912 | tf_op jit(solution)/shard_map/grad_blocks/pallas_call | solution.py:114
  134.3 6.0 %convolution_convert_fusion = bf16[2048,512]{1,0:T(8,128)(2,1)} fusion(bf16[1024,2048]{1,0:T(8,128)(2,1)} %grad_blocks.3, bf16[1024,1024]{1,0:T(8,128)(2,1)S(1)} %copy-done.1, s32[]{:T(128)S(6)} %select_n.66), kind=kOutput, calls=%fused_computation.5 | convolution fusion | flops 2148532224 | bytes 7340036 | tf_op jit(solution)/shard_map/dot_general | solution.py:284
  140.3 6.6 %add_convert_fusion.1 = bf16[2048,512]{1,0:T(8,128)(2,1)} fusion(bf16[2048,512]{1,0:T(8,128)(2,1)} %collective-permute-done.4, bf16[1024,2048]{1,0:T(8,128)(2,1)} %grad_blocks.2, bf16[1024,1024]{1,0:T(8,128)(2,1)S(1)} %copy-done.1, s32[]{:T(128)S(6)} %select_n.65), kind=kOutput, calls=%fused_computation.3 | convolution fusion | flops 2150629376 | bytes 9437188 | tf_op jit(solution)/shard_map/dot_general | solution.py:286
  146.9 10.3 %all-to-all-start.1 = ((bf16[64,32,512]{2,1,0:T(8,128)(2,1)}), bf16[64,32,512]{2,1,0:T(8,128)(2,1)S(1)}, u32[]{:S(2)}, u32[]{:S(2)}) async-start(bf16[64,32,512]{2,1,0:T(8,128)(2,1)} %bitcast.39), calls=%async_computation.1 | async-start | bytes 4194304 | tf_op jit(solution)/shard_map/all_to_all | solution.py:288
  157.2 6.9 %add_convert_fusion = bf16[2048,512]{1,0:T(8,128)(2,1)} fusion(bf16[2048,512]{1,0:T(8,128)(2,1)} %collective-permute-done.5, bf16[1024,2048]{1,0:T(8,128)(2,1)} %grad_blocks.3, bf16[1024,1024]{1,0:T(8,128)(2,1)} %reshape.109.edges, s32[]{:T(128)S(6)} %select_n.65), kind=kOutput, calls=%fused_computation.1 | convolution fusion | flops 2150629376 | bytes 9437188 | tf_op jit(solution)/shard_map/dot_general | solution.py:286
  164.1 24.6 %all-to-all-done.1 = bf16[64,32,512]{2,1,0:T(8,128)(2,1)S(1)} async-done(((bf16[64,32,512]{2,1,0:T(8,128)(2,1)}), bf16[64,32,512]{2,1,0:T(8,128)(2,1)S(1)}, u32[]{:S(2)}, u32[]{:S(2)}) %all-to-all-start.1) | async-done | bytes 2097184 | tf_op jit(solution)/shard_map/all_to_all | solution.py:288
  188.7 5.6 %all-to-all-start.2 = ((bf16[64,32,512]{2,1,0:T(8,128)(2,1)}), bf16[64,32,512]{2,1,0:T(8,128)(2,1)}, u32[]{:S(2)}, u32[]{:S(2)}) async-start(bf16[64,32,512]{2,1,0:T(8,128)(2,1)} %bitcast.40), calls=%async_computation.2 | async-start | bytes 4194304 | tf_op jit(solution)/shard_map/all_to_all | solution.py:288
  194.6 29.4 %all-to-all-done.2 = bf16[64,32,512]{2,1,0:T(8,128)(2,1)} async-done(((bf16[64,32,512]{2,1,0:T(8,128)(2,1)}), bf16[64,32,512]{2,1,0:T(8,128)(2,1)}, u32[]{:S(2)}, u32[]{:S(2)}) %all-to-all-start.2) | async-done | bytes 2097184 | tf_op jit(solution)/shard_map/all_to_all | solution.py:288
  224.0 1.9 convert_reduce_fusion
  225.9 34.9 %energy_share.1 = f32[1,256]{1,0:T(1,128)} custom-call(s32[1040]{0:T(1024)} %concatenate.6.index, s32[256]{0:T(256)} %get-tuple-element.11.tiles, s32[256]{0:T(256)} %get-tuple-element.10.rows, s32[1]{0:T(128)} %bitcast.4.total, bf16[64,32,256]{2,1,0:T(8,128)(2,1)} %collective-permute-done.prev0.prev, bf16[64,32,256]{2,1,0:T(8,128)(2,1)} %copy-done.5, ...), custom_call_target="tpu_custom_call" | custom-call | flops 17179869184 | bytes 16777216 | tf_op jit(solution)/shard_map/energy_share/pallas_call | solution.py:225
  260.9 1.3 broadcast_in_dim.44
  262.1 4.6 %all-to-all-start = ((f32[64,1,256]{2,1,0:T(1,128)}), f32[64,1,256]{2,1,0:T(1,128)S(1)}, u32[]{:S(2)}, u32[]{:S(2)}) async-start(f32[64,1,256]{2,1,0:T(1,128)} %broadcast_in_dim.44), calls=%async_computation | async-start | bytes 131072 | tf_op jit(solution)/shard_map/all_to_all | solution.py:294
  266.8 2.0 all_gather.7
  268.8 7.6 %all-to-all-done = f32[64,1,256]{2,1,0:T(1,128)S(1)} async-done(((f32[64,1,256]{2,1,0:T(1,128)}), f32[64,1,256]{2,1,0:T(1,128)S(1)}, u32[]{:S(2)}, u32[]{:S(2)}) %all-to-all-start) | async-done | bytes 65568 | tf_op jit(solution)/shard_map/all_to_all | solution.py:294
  276.4 0.7 reduce_sum.47
  277.0 0.7 copy.24
  (35 shorter events, 2.5 us)
Async XLA Ops:
  7.2 218.8 %all-gather.2.cloned.1.call-start = ((), (), s32[]{:S(2)}) async-start(), calls=%async_computation.3 | async-start | bytes 8519680 | tf_op jit(solution)/shard_map/all_gather | solution.py:261
  7.9 11.6 %copy-start.4 = (s32[1,64]{1,0:T(1,128)S(1)}, s32[1,64]{1,0:T(1,128)}, u32[]{:S(2)}) copy-start(s32[1,64]{1,0:T(1,128)} %param.9) | copy-start | bytes 772
  7.9 11.7 %copy-start.2 = (s32[1,64,16]{1,2,0:T(8,128)S(1)}, s32[1,64,16]{1,2,0:T(8,128)}, u32[]{:S(2)}) copy-start(s32[1,64,16]{1,2,0:T(8,128)} %param.8) | copy-start | bytes 12292
  10.7 33.6 %collective-permute-start = (bf16[64,32,256]{2,1,0:T(8,128)(2,1)}, bf16[64,32,256]{2,1,0:T(8,128)(2,1)}, u32[]{:S(2)}, u32[]{:S(2)}) collective-permute-start(bf16[64,32,256]{2,1,0:T(8,128)(2,1)} %get-tuple-element.8), channel_id=1, source_target_pairs={{0,1},{1,2},{2,3},{3,4},{4,5},{5,6},{6,7},{7,8},{8,9},{9,10},{10,1... | collective-permute-start | bytes 3145736 | tf_op jit(solution)/shard_map/ppermute | solution.py:259
  12.3 32.0 %collective-permute-start.1 = (bf16[64,32,256]{2,1,0:T(8,128)(2,1)}, bf16[64,32,256]{2,1,0:T(8,128)(2,1)}, u32[]{:S(2)}, u32[]{:S(2)}) collective-permute-start(bf16[64,32,256]{2,1,0:T(8,128)(2,1)} %get-tuple-element.8), channel_id=1, source_target_pairs={{1,0},{2,1},{3,2},{4,3},{5,4},{6,5},{7,6},{8,7},{9,8},{10,9},{11,1... | collective-permute-start | bytes 3145736 | tf_op jit(solution)/shard_map/ppermute | solution.py:260
  26.0 6.1 %copy-start = (bf16[1,64,64,256]{3,2,1,0:T(8,128)(2,1)S(1)}, bf16[1,64,64,256]{3,2,1,0:T(8,128)(2,1)}, u32[]{:S(2)}) copy-start(bf16[1,64,64,256]{3,2,1,0:T(8,128)(2,1)} %param.7) | copy-start | bytes 6291460
  26.0 6.1 %copy-start.3 = (f32[1,256]{1,0:T(1,128)S(1)}, f32[1,256]{1,0:T(1,128)}, u32[]{:S(2)}) copy-start(f32[1,256]{1,0:T(1,128)} %param.10) | copy-start | bytes 3076
  44.2 15.7 %copy-start.1 = (bf16[1024,1024]{1,0:T(8,128)(2,1)S(1)}, bf16[1024,1024]{1,0:T(8,128)(2,1)}, u32[]{:S(2)}) copy-start(bf16[1024,1024]{1,0:T(8,128)(2,1)} %reshape.109.edges) | copy-start | bytes 6291460
  65.9 74.4 %collective-permute-start.4 = (bf16[2048,512]{1,0:T(8,128)(2,1)}, bf16[2048,512]{1,0:T(8,128)(2,1)}, u32[]{:S(2)}, u32[]{:S(2)}) collective-permute-start(bf16[2048,512]{1,0:T(8,128)(2,1)} %convolution_convert_fusion.1), channel_id=1, source_target_pairs={{0,64},{64,0},{1,65},{65,1},{2,66},{66,2},{3,67},{67,3},{4,68},{68... | collective-permute-start | bytes 6291464 | tf_op jit(solution)/shard_map/ppermute | solution.py:285
  65.9 46.3 %collective-permute-start.2 = (bf16[64,32,256]{2,1,0:T(8,128)(2,1)S(1)}, bf16[64,32,256]{2,1,0:T(8,128)(2,1)S(1)}, u32[]{:S(2)}, u32[]{:S(2)}) collective-permute-start(bf16[64,32,256]{2,1,0:T(8,128)(2,1)S(1)} %get-tuple-element.6), channel_id=1, source_target_pairs={{0,1},{1,2},{2,3},{3,4},{4,5},{5,6},{6,7},{7,8},{8,9},{9,10},{10,1... | collective-permute-start | bytes 3145736 | tf_op jit(solution)/shard_map/ppermute | solution.py:263
  65.9 52.8 %collective-permute-start.3 = (bf16[64,32,256]{2,1,0:T(8,128)(2,1)S(1)}, bf16[64,32,256]{2,1,0:T(8,128)(2,1)}, u32[]{:S(2)}, u32[]{:S(2)}) collective-permute-start(bf16[64,32,256]{2,1,0:T(8,128)(2,1)S(1)} %get-tuple-element.6), channel_id=1, source_target_pairs={{1,0},{2,1},{3,2},{4,3},{5,4},{6,5},{7,6},{8,7},{9,8},{10,9},{11,1... | collective-permute-start | bytes 3145736 | tf_op jit(solution)/shard_map/ppermute | solution.py:264
  112.2 1.0 copy-start.5
  140.3 16.9 %collective-permute-start.5 = (bf16[2048,512]{1,0:T(8,128)(2,1)}, bf16[2048,512]{1,0:T(8,128)(2,1)}, u32[]{:S(2)}, u32[]{:S(2)}) collective-permute-start(bf16[2048,512]{1,0:T(8,128)(2,1)} %convolution_convert_fusion), channel_id=1, source_target_pairs={{0,64},{64,0},{1,65},{65,1},{2,66},{66,2},{3,67},{67,3},{4,68},{68... | collective-permute-start | bytes 6291464 | tf_op jit(solution)/shard_map/ppermute | solution.py:285
  146.9 41.8 %all-to-all-start.1 = ((bf16[64,32,512]{2,1,0:T(8,128)(2,1)}), bf16[64,32,512]{2,1,0:T(8,128)(2,1)S(1)}, u32[]{:S(2)}, u32[]{:S(2)}) async-start(bf16[64,32,512]{2,1,0:T(8,128)(2,1)} %bitcast.39), calls=%async_computation.1 | async-start | bytes 4194304 | tf_op jit(solution)/shard_map/all_to_all | solution.py:288
  188.7 35.3 %all-to-all-start.2 = ((bf16[64,32,512]{2,1,0:T(8,128)(2,1)}), bf16[64,32,512]{2,1,0:T(8,128)(2,1)}, u32[]{:S(2)}, u32[]{:S(2)}) async-start(bf16[64,32,512]{2,1,0:T(8,128)(2,1)} %bitcast.40), calls=%async_computation.2 | async-start | bytes 4194304 | tf_op jit(solution)/shard_map/all_to_all | solution.py:288
  262.1 14.2 %all-to-all-start = ((f32[64,1,256]{2,1,0:T(1,128)}), f32[64,1,256]{2,1,0:T(1,128)S(1)}, u32[]{:S(2)}, u32[]{:S(2)}) async-start(f32[64,1,256]{2,1,0:T(1,128)} %broadcast_in_dim.44), calls=%async_computation | async-start | bytes 131072 | tf_op jit(solution)/shard_map/all_to_all | solution.py:294
Sparse Core Ops, SparseCore 0:
  10.8 109.4 all-gather.1

commit v4 on v3

--- a/solution.py
+++ b/solution.py
@@ -7,6 +7,7 @@
 from jax.experimental import pallas as pl
 from jax.experimental.pallas import tpu as pltpu
 from jax.sharding import PartitionSpec as P
+
 
 ORB = 64
 BANDS = 256
@@ -17,6 +18,7 @@
 ZERO_TILE = 3 * TILES
 CHUNK = 32
 ROWS = EDGES // 4
+SHEET = 1024
 GRAD_PITCH = ROWS + 8
 UNROLL = 16
 ENERGY_UNROLL = 4
@@ -148,10 +150,9 @@
 
 
 def energy_kernel(
-    index, tiles, rows, total, prev0, prev1, own, following0, following1, edges, weights, out, table, strips, sems, *, factor
+    index, tiles, rows, total, who, prev0, prev1, own, following0, following1, mine, theirs, *rest, factor
 ):
-    step = pl.program_id(0)
-    width = weights.shape[0] // ORB
+    sheets, (out, table, strips, near, far, weights, sems) = rest[:8], rest[8:]
     low = left_lanes((ROWS, 128))
     places = (
         (prev0, table.at[pl.ds(0, TILES), pl.ds(0, CHUNK)]),
@@ -160,83 +161,82 @@
         (following0, table.at[pl.ds(2 * TILES, TILES), pl.ds(0, CHUNK)]),
         (following1, table.at[pl.ds(2 * TILES, TILES), pl.ds(CHUNK, CHUNK)]),
     )
-    copies = [
-        pltpu.make_async_copy(src, dst, sems.at[n]) for n, (src, dst) in enumerate(places)
+    late = [pltpu.make_async_copy(src, dst, sems.at[n]) for n, (src, dst) in enumerate(places)]
+    early = [
+        pltpu.make_async_copy(mine, near, sems.at[5]),
+        pltpu.make_async_copy(theirs, far, sems.at[6]),
     ]
-
-    @pl.when(step == 0)
-    def _():
-        for copy in copies:
-            copy.start()
-        table[ZERO_TILE] = jnp.zeros((ORB, BANDS), jnp.bfloat16)
-        for part in (0, 1):
-            strips[pl.ds(part * GRAD_PITCH + ROWS, ORB, stride=2 * GRAD_PITCH), :] = jnp.zeros(
-                (ORB, 128), jnp.float32
-            )
-
-    for pair in range(width // 2):
+    for n, sheet in enumerate(sheets):
+        spot = weights.at[n // 4, pl.ds(n % 4 * SHEET, SHEET)]
+        early.append(pltpu.make_async_copy(sheet, spot, sems.at[7 + n]))
+    for copy in early + late:
+        copy.start()
+    table[ZERO_TILE] = jnp.zeros((ORB, BANDS), jnp.bfloat16)
+    for part in (0, 1):
+        strips[pl.ds(part * GRAD_PITCH + ROWS, ORB, stride=2 * GRAD_PITCH), :] = jnp.zeros(
+            (ORB, 128), jnp.float32
+        )
+    for copy in early:
+        copy.wait()
+
+    def pair_body(n, carry):
+        spot = pl.ds(pl.multiple_of(n * 128, 128), 128)
         product = lax.dot_general(
-            edges[...],
-            weights[pair * 128 : (pair + 1) * 128, :],
-            NT,
-            preferred_element_type=jnp.float32,
-        ).reshape(TILES // 2, 4, 8, 128)
-        base = (step * width + 2 * pair) * (2 * GRAD_PITCH)
+            near[...], weights[0, spot, :], NT, preferred_element_type=jnp.float32
+        ) + lax.dot_general(far[...], weights[1, spot, :], NT, preferred_element_type=jnp.float32)
+        product = product.reshape(TILES // 2, 4, 8, 128)
+        one, two = (pl.multiple_of(who[2 * n + u] * (2 * GRAD_PITCH), 8) for u in (0, 1))
         for part in (0, 1):
             front = product[:, 2 * part].reshape(ROWS, 128)
             back = product[:, 2 * part + 1].reshape(ROWS, 128)
-            spot = base + part * GRAD_PITCH
-            strips[pl.ds(pl.multiple_of(spot, 8), ROWS), :] = jnp.where(low, front, swap(back))
-            spot = spot + 2 * GRAD_PITCH
-            strips[pl.ds(pl.multiple_of(spot, 8), ROWS), :] = jnp.where(low, swap(front), back)
-
-    @pl.when(step == pl.num_programs(0) - 1)
-    def _():
-        for copy in copies:
-            copy.wait()
-
-        def item_body(n, carry):
-            at = [rows[n * ENERGY_UNROLL + u] for u in range(ENERGY_UNROLL)]
-            who = [tiles[n * ENERGY_UNROLL + u] for u in range(ENERGY_UNROLL)]
-            which = [[index[row * 4 + p] for p in range(4)] for row in at]
-            for u in range(ENERGY_UNROLL):
-                left = jnp.concatenate(
-                    [
-                        strips[
-                            pl.ds(part * GRAD_PITCH + at[u], ORB, stride=2 * GRAD_PITCH), :
-                        ].astype(jnp.bfloat16)
-                        for part in (0, 1)
-                    ],
-                    axis=1,
-                )
-                right = jnp.concatenate([table[w] for w in which[u]], axis=0)
-                applied = jnp.dot(left, right, preferred_element_type=jnp.float32)
-                terms = table[TILES + who[u]].astype(jnp.float32) * applied
-                carry = carry + jnp.sum(terms.reshape(8, 8, BANDS), axis=0)
-            return carry
-
-        trips = (total[0] + ENERGY_UNROLL - 1) // ENERGY_UNROLL
-        sums = lax.fori_loop(0, trips, item_body, jnp.zeros((8, BANDS), jnp.float32))
-        out[...] = jnp.sum(sums, axis=0, keepdims=True) * factor
-
-
-def energy_share(plan, prev, own, following, edges, weights, factor):
-    block = 512
+            strips[pl.ds(one + part * GRAD_PITCH, ROWS), :] = jnp.where(low, front, swap(back))
+            strips[pl.ds(two + part * GRAD_PITCH, ROWS), :] = jnp.where(low, swap(front), back)
+        return carry
+
+    lax.fori_loop(0, ORB // 2, pair_body, 0, unroll=2)
+    for copy in late:
+        copy.wait()
+
+    def item_body(n, carry):
+        at = [rows[n * ENERGY_UNROLL + u] for u in range(ENERGY_UNROLL)]
+        home = [tiles[n * ENERGY_UNROLL + u] for u in range(ENERGY_UNROLL)]
+        which = [[index[row * 4 + p] for p in range(4)] for row in at]
+        for u in range(ENERGY_UNROLL):
+            left = jnp.concatenate(
+                [
+                    strips[
+                        pl.ds(part * GRAD_PITCH + at[u], ORB, stride=2 * GRAD_PITCH), :
+                    ].astype(jnp.bfloat16)
+                    for part in (0, 1)
+                ],
+                axis=1,
+            )
+            right = jnp.concatenate([table[w] for w in which[u]], axis=0)
+            applied = jnp.dot(left, right, preferred_element_type=jnp.float32)
+            terms = table[TILES + home[u]].astype(jnp.float32) * applied
+            carry = carry + jnp.sum(terms.reshape(8, 8, BANDS), axis=0)
+        return carry
+
+    trips = (total[0] + ENERGY_UNROLL - 1) // ENERGY_UNROLL
+    sums = lax.fori_loop(0, trips, item_body, jnp.zeros((8, BANDS), jnp.float32))
+    out[...] = jnp.sum(sums, axis=0, keepdims=True) * factor
+
+
+def energy_share(plan, who, prev, own, following, mine, theirs, sheets, factor):
     return pl.pallas_call(
         functools.partial(energy_kernel, factor=factor),
         grid_spec=pltpu.PrefetchScalarGridSpec(
-            num_scalar_prefetch=4,
-            grid=(ORB * ORB // block,),
-            in_specs=[pl.BlockSpec(memory_space=pltpu.MemorySpace.HBM)] * 5
-            + [
-                pl.BlockSpec((EDGES, FEAT), lambda j, *_: (0, 0)),
-                pl.BlockSpec((block, FEAT), lambda j, *_: (j, 0)),
-            ],
+            num_scalar_prefetch=5,
+            grid=(1,),
+            in_specs=[pl.BlockSpec(memory_space=pltpu.MemorySpace.HBM)] * 15,
             out_specs=pl.BlockSpec((1, BANDS), lambda j, *_: (0, 0)),
             scratch_shapes=[
                 pltpu.VMEM((ZERO_TILE + 1, ORB, BANDS), jnp.bfloat16),
                 pltpu.VMEM((2 * ORB * GRAD_PITCH, 128), jnp.float32),
-                pltpu.SemaphoreType.DMA((5,)),
+                pltpu.VMEM((EDGES, FEAT // 2), jnp.bfloat16),
+                pltpu.VMEM((EDGES, FEAT // 2), jnp.bfloat16),
+                pltpu.VMEM((2, 4 * SHEET, FEAT // 2), jnp.bfloat16),
+                pltpu.SemaphoreType.DMA((15,)),
             ],
         ),
         out_shape=jax.ShapeDtypeStruct((1, BANDS), jnp.float32),
@@ -245,7 +245,20 @@
             flops=2 * EDGES * ORB * ORB * (FEAT + BANDS * 4), bytes_accessed=16 * 2**20, transcendentals=0
         ),
         name="energy_share",
-    )(*plan, *prev, own, *following, edges, weights)
+    )(*plan, who, *prev, own, *following, mine, theirs, *sheets)
+
+
+def ring(axis, hop):
+    pairs = []
+    for i in range(64):
+        spot = [i // 16, i // 4 % 4, i % 4]
+        spot[axis] = (spot[axis] + hop) % 4
+        pairs.append((i, spot[0] * 16 + spot[1] * 4 + spot[2]))
+    return pairs
+
+
+def spread(value, axis):
+    return [value] + [lax.ppermute(value, "space", ring(axis, hop)) for hop in (1, 2, 3)]
 
 
 def step(features, psi, neighbors, counts, occupation, weights):
@@ -258,7 +271,19 @@
     down = [(j, i) for i, j in up]
     prev0 = lax.ppermute(own[:, :CHUNK], "space", up)
     following0 = lax.ppermute(own[:, :CHUNK], "space", down)
-    gathered = lax.all_gather(weights.T, "space", axis=0, tiled=True)
+    half = FEAT // 2
+    swapped = [(0, 1), (1, 0)]
+    sheet = lax.dynamic_slice_in_dim(weights.T, core * half, half, 1)
+    sheet = jnp.concatenate(spread(sheet, 2), axis=0)
+    sheet = jnp.concatenate(spread(sheet, 1), axis=0)
+    sheets = spread(sheet, 0)
+    sheets = sheets + [lax.ppermute(sheet, "dp", swapped) for sheet in sheets]
+    back = jnp.arange(ORB, dtype=jnp.int32)
+    who = (
+        (myself // 16 - back // 16) % 4 * 16
+        + (myself // 4 - back // 4) % 4 * 4
+        + (myself - back) % 4
+    ).astype(jnp.int32)
     second, prev0, following0 = lax.optimization_barrier((own[:, CHUNK:], prev0, following0))
     prev1 = lax.ppermute(second, "space", up)
     following1 = lax.ppermute(second, "space", down)
@@ -274,24 +299,26 @@
         features.reshape(TILES // 2, 2, 4, 4, FEAT).transpose(0, 3, 1, 2, 4).reshape(EDGES, FEAT)
     )
 
-    half = FEAT // 2
     theirs = lax.dynamic_slice_in_dim(edges, (1 - core) * half, half, 1)
     mine = lax.dynamic_slice_in_dim(edges, core * half, half, 1)
     over_edges = (((0,), (0,)), ((), ()))
-    shares = []
+    arrived = []
     for part in (0, 1):
         blocks = grad_blocks(plan, prev[part], own, following[part], weighted, part, factor)
         send = lax.dot_general(blocks, theirs, over_edges, preferred_element_type=jnp.float32)
-        other = lax.ppermute(send.astype(jnp.bfloat16), "dp", [(0, 1), (1, 0)])
+        other = lax.ppermute(send.astype(jnp.bfloat16), "dp", swapped)
         keep = lax.dot_general(blocks, mine, over_edges, preferred_element_type=jnp.float32)
         summed = (keep + other.astype(jnp.float32)).astype(jnp.bfloat16)
         parts = lax.all_to_all(summed, "space", 0, 0, tiled=True)
-        shares.append(jnp.sum(parts.reshape(nspace, CHUNK, half).astype(jnp.float32), axis=0))
-    gradient = lax.all_gather(jnp.concatenate(shares, axis=0), "dp", axis=1, tiled=True)
-
-    partial = energy_share(plan, prev, own, following, edges, gathered, factor)
+        arrived.append(parts)
+    partial = energy_share(plan, who, prev, own, following, mine, theirs, sheets, factor)
+    partial, arrived[1] = lax.optimization_barrier((partial, arrived[1]))
     copies = jnp.broadcast_to(partial, (nspace, BANDS))
     energies = jnp.sum(lax.all_to_all(copies, "space", 0, 0, tiled=True), axis=0, keepdims=True)
+    shares = [
+        jnp.sum(parts.reshape(nspace, CHUNK, half).astype(jnp.float32), axis=0) for parts in arrived
+    ]
+    gradient = lax.all_gather(jnp.concatenate(shares, axis=0), "dp", axis=1, tiled=True)
     return (energies, gradient)
 
 

time: 285 us -> 266 us (0.933)
  waiting for transfers between devices: 117 us -> 85.4 us
  starting transfers between devices: 36.8 us -> 51.1 us
  between operations: 14.2 us -> 0.94 us
  local copies, waits for them, and re-layouts: 16.6 us -> 22 us
  Pallas kernels: 66.2 us -> 71.6 us
    ppermute x2 -> x15, waiting for transfers between devices: 0.01 us -> 73.5 us  [the longest x9 73.4 us: spread(): lax.ppermute(value, 'space', ring(axis, hop))]
    all_to_all x2, waiting for transfers between devices: 54 us -> 0.01 us  [step(): parts = lax.all_to_all(summed, 'space', 0, 0, tiled=True)]
    ppermute x1, waiting for transfers between devices: 38.8 us -> 0.01 us  [step(): prev1 = lax.ppermute(second, 'space', up)]
    ppermute x2 -> x15, starting transfers between devices: 0.01 us -> 10 us  [the longest x9 9.5 us: spread(): lax.ppermute(value, 'space', ring(axis, hop))]
    all_to_all x1, starting transfers between devices: 4.62 us -> 10.5 us  [step(): lax.all_to_all(copies, 'space', 0, 0, tiled=True)]
    ppermute x1, waiting for transfers between devices: 5.5 us -> 0.01 us  [step(): following1 = lax.ppermute(second, 'space', down)]
    pallas_call x1, Pallas kernels: 34.9 us -> 40.1 us  [energy_share(): pl.pallas_call(functools.partial(energy_kernel, factor=factor), grid_spec...]
    ppermute x1, waiting for transfers between devices: 10.4 us -> 6.21 us  [step(): prev0 = lax.ppermute(own[:, :CHUNK], 'space', up)]
  transfers between devices with their start and end apart: 10 -> 22, of which waited for: 6 -> 6; matrix products, arithmetic and copies ran while one was open for 16% -> 18% of each run, Pallas kernels for 11% -> 27%
where the time goes in v4:
time: 266 us; the launch traced here: 265 us
  waiting for transfers between devices  85.4 us (32%)
  Pallas kernels  71.6 us (27%)
  starting transfers between devices  51.1 us (19%)
  matrix products  24.7 us (9%)
  local copies, waits for them, and re-layouts  22 us (8%)
  other arithmetic  7.17 us (3%)
    ppermute x9, waiting for transfers between devices, spread(): lax.ppermute(value, 'space', ring(axis, hop))  73.4 us
    pallas_call x1, Pallas kernels, energy_share(): pl.pallas_call(functools.partial(energy_kernel, factor=factor), grid_spec...  40.1 us
    pallas_call x2, Pallas kernels, grad_blocks(): pl.pallas_call(functools.partial(grad_blocks_kernel, part=part, factor=fa...  31.5 us
    all_to_all x2, starting transfers between devices, step(): parts = lax.all_to_all(summed, 'space', 0, 0, tiled=True)  14.3 us
    dot_general x2, matrix products, step(): lax.dot_general(blocks, mine, over_edges, preferred_element_type=jnp.floa...  12.5 us
    dot_general x2, matrix products, step(): lax.dot_general(blocks, theirs, over_edges, preferred_element_type=jnp.fl...  12.2 us
    all_to_all x1, starting transfers between devices, step(): lax.all_to_all(copies, 'space', 0, 0, tiled=True)  10.5 us
    ppermute x9, starting transfers between devices, spread(): lax.ppermute(value, 'space', ring(axis, hop))  9.5 us
  transfers between devices with their start and end apart: 22, of which 6 were waited for; matrix products, arithmetic and copies ran while one was open for 18% of the time, Pallas kernels for 27%

profile of v4, /device:TPU:0, one launch (start us, length us, event | category | flops | bytes accessed | tf_op | source)
XLA Modules:
  0.0 264.7 jit_solution(3269968915908503682)
XLA Ops:
  0.6 3.0 %fusion.18 = (bf16[64,32,256]{2,1,0:T(8,128)(2,1)}, bf16[64,32,256]{2,1,0:T(8,128)(2,1)}) fusion(bf16[64,64,256]{2,1,0:T(8,128)(2,1)} %bitcast.43), kind=kLoop, calls=%fused_computation.80 | loop fusion | bytes 4194304 | tf_op jit(solution)/shard_map/slice | solution.py:272
  3.7 1.6 collective-permute-start
  5.3 7.2 %collective-permute-start.1 = (bf16[64,32,256]{2,1,0:T(8,128)(2,1)}, bf16[64,32,256]{2,1,0:T(8,128)(2,1)}, u32[]{:S(2)}, u32[]{:S(2)}) collective-permute-start(bf16[64,32,256]{2,1,0:T(8,128)(2,1)} %get-tuple-element.16), channel_id=1, source_target_pairs={{1,0},{2,1},{3,2},{4,3},{5,4},{6,5},{7,6},{8,7},{9,8},{10,9},{11,1... | collective-permute-start | bytes 3145736 | tf_op jit(solution)/shard_map/ppermute | solution.py:273
  13.8 2.7 %reshape.109 = bf16[32,2,4,4,1024]{4,3,2,1,0:T(4,128)(2,1)S(1)} reshape(bf16[1,64,16,1024]{3,2,1,0:T(8,128)(2,1)} %param.6) | data formatting | bytes 4194304 | tf_op jit(solution)/shard_map/reshape | solution.py:299
  16.6 2.4 copy.22
  19.0 4.1 %reshape.110 = bf16[1024,1024]{1,0:T(8,128)(2,1)} reshape(bf16[32,4,2,4,1024]{4,3,2,1,0:T(4,128)(2,1)} %bitcast.47) | data formatting | bytes 4194304 | tf_op jit(solution)/shard_map/reshape | solution.py:299
  23.9 2.7 %constant_dynamic-slice_fusion = (bf16[1024,512]{1,0:T(8,128)(2,1)S(1)}, bf16[1024,512]{1,0:T(8,128)(2,1)}) fusion(bf16[1024,1024]{1,0:T(8,128)(2,1)} %reshape.110, s32[]{:T(128)S(6)} %select_n.101, s32[]{:T(128)S(6)} %select_n.100), kind=kLoop, calls=%fused_computation.66 | loop fusion | bytes 4194312 | tf_op jit(solution)/shard_map/dynamic_slice | solution.py:302
  27.8 2.0 multiply_convert_fusion.weighted
  29.7 6.2 %collective-permute-done.prev0.prev = bf16[64,32,256]{2,1,0:T(8,128)(2,1)} collective-permute-done((bf16[64,32,256]{2,1,0:T(8,128)(2,1)}, bf16[64,32,256]{2,1,0:T(8,128)(2,1)}, u32[]{:S(2)}, u32[]{:S(2)}) %collective-permute-start) | collective-permute-done | bytes 1048608 | tf_op jit(solution)/shard_map/ppermute | solution.py:272
  36.0 7.5 %collective-permute-start.3 = (bf16[64,32,256]{2,1,0:T(8,128)(2,1)}, bf16[64,32,256]{2,1,0:T(8,128)(2,1)}, u32[]{:S(2)}, u32[]{:S(2)}) collective-permute-start(bf16[64,32,256]{2,1,0:T(8,128)(2,1)} %get-tuple-element.8), channel_id=1, source_target_pairs={{1,0},{2,1},{3,2},{4,3},{5,4},{6,5},{7,6},{8,7},{9,8},{10,9},{11,1... | collective-permute-start | bytes 3145736 | tf_op jit(solution)/shard_map/ppermute | solution.py:289
  43.4 15.8 %grad_blocks.3 = bf16[1024,2048]{1,0:T(8,128)(2,1)} custom-call(s32[1040]{0:T(1024)} %concatenate.13.index, s32[256]{0:T(256)} %get-tuple-element.19.tiles, s32[256]{0:T(256)} %get-tuple-element.18.rows, s32[1]{0:T(128)} %bitcast.4.total, bf16[64,32,256]{2,1,0:T(8,128)(2,1)} %collective-permute-done.prev0.prev, bf16[64,64,256]{2,1,0:T(8,128)(2,1)} %bitcast.44, ...), custom_call_target="tpu_custom_call" | custom-call | flops 4294967296 | bytes 12582912 | tf_op jit(solution)/shard_map/grad_blocks/pallas_call | solution.py:116
  59.3 6.0 %convolution_convert_fusion = bf16[2048,512]{1,0:T(8,128)(2,1)} fusion(bf16[1024,2048]{1,0:T(8,128)(2,1)} %grad_blocks.3, bf16[1024,512]{1,0:T(8,128)(2,1)S(1)} %get-tuple-element.14.theirs), kind=kOutput, calls=%fused_computation.5 | convolution fusion | flops 2148532224 | bytes 7340032 | tf_op jit(solution)/shard_map/dot_general | solution.py:308
  65.4 7.0 %collective-permute-done.4 = bf16[64,512]{1,0:T(8,128)(2,1)S(1)} collective-permute-done((bf16[64,512]{1,0:T(8,128)(2,1)S(1)}, bf16[64,512]{1,0:T(8,128)(2,1)S(1)}, u32[]{:S(2)}, u32[]{:S(2)}) %collective-permute-start.4) | collective-permute-done | bytes 65568 | tf_op jit(solution)/shard_map/ppermute | solution.py:261
  72.5 4.3 %collective-permute-done.6 = bf16[64,512]{1,0:T(8,128)(2,1)S(1)} collective-permute-done((bf16[64,512]{1,0:T(8,128)(2,1)S(1)}, bf16[64,512]{1,0:T(8,128)(2,1)S(1)}, u32[]{:S(2)}, u32[]{:S(2)}) %collective-permute-start.6) | collective-permute-done | bytes 65568 | tf_op jit(solution)/shard_map/ppermute | solution.py:261
  77.0 3.4 %collective-permute-start.9 = (bf16[256,512]{1,0:T(8,128)(2,1)S(1)}, bf16[256,512]{1,0:T(8,128)(2,1)}, u32[]{:S(2)}, u32[]{:S(2)}) collective-permute-start(bf16[256,512]{1,0:T(8,128)(2,1)S(1)} %pad_maximum_fusion), channel_id=1, source_target_pairs={{0,12},{1,13},{2,14},{3,15},{4,0},{5,1},{6,2},{7,3},{8,4},{9,5},{1... | collective-permute-start | bytes 786440 | tf_op jit(solution)/shard_map/ppermute | solution.py:261
  80.4 15.6 %grad_blocks.2 = bf16[1024,2048]{1,0:T(8,128)(2,1)} custom-call(s32[1040]{0:T(1024)} %concatenate.13.index, s32[256]{0:T(256)} %get-tuple-element.19.tiles, s32[256]{0:T(256)} %get-tuple-element.18.rows, s32[1]{0:T(128)} %bitcast.4.total, bf16[64,32,256]{2,1,0:T(8,128)(2,1)} %copy-done.9, bf16[64,64,256]{2,1,0:T(8,128)(2,1)} %bitcast.45, ...), custom_call_target="tpu_custom_call" | custom-call | flops 4294967296 | bytes 12582912 | tf_op jit(solution)/shard_map/grad_blocks/pallas_call | solution.py:116
  96.0 6.2 %convolution_convert_fusion.1 = bf16[2048,512]{1,0:T(8,128)(2,1)} fusion(bf16[1024,2048]{1,0:T(8,128)(2,1)} %grad_blocks.2, bf16[1024,512]{1,0:T(8,128)(2,1)S(1)} %get-tuple-element.14.theirs), kind=kOutput, calls=%fused_computation.6 | convolution fusion | flops 2148532224 | bytes 7340032 | tf_op jit(solution)/shard_map/dot_general | solution.py:308
  102.3 5.8 %add_convert_fusion = bf16[2048,512]{1,0:T(8,128)(2,1)} fusion(bf16[2048,512]{1,0:T(8,128)(2,1)} %collective-permute-done.18, bf16[1024,2048]{1,0:T(8,128)(2,1)S(1)} %copy-done.10, bf16[1024,512]{1,0:T(8,128)(2,1)S(1)} %copy-done.2), kind=kOutput, calls=%fused_computation.2 | convolution fusion | flops 2150629376 | bytes 9437184 | tf_op jit(solution)/shard_map/dot_general | solution.py:310
  108.1 5.5 %all-to-all-start.2 = ((bf16[64,32,512]{2,1,0:T(8,128)(2,1)}), bf16[64,32,512]{2,1,0:T(8,128)(2,1)S(1)}, u32[]{:S(2)}, u32[]{:S(2)}) async-start(bf16[64,32,512]{2,1,0:T(8,128)(2,1)} %bitcast.49), calls=%async_computation.2 | async-start | bytes 4194304 | tf_op jit(solution)/shard_map/all_to_all | solution.py:312
  113.6 1.7 constant_dynamic-update-slice_fusion.1
  115.3 1.7 constant_dynamic-update-slice_fusion.rest_0_
  116.9 1.6 collective-permute-start.10
  118.5 2.9 %collective-permute-start.11 = (bf16[1024,512]{1,0:T(8,128)(2,1)}, bf16[1024,512]{1,0:T(8,128)(2,1)}, u32[]{:S(2)}, u32[]{:S(2)}) collective-permute-start(bf16[1024,512]{1,0:T(8,128)(2,1)} %constant_dynamic-update-slice_fusion.rest_0_), channel_id=1, source_target_pairs={{0,32},{1,33},{2,34},{3,35},{4,36},{5,37},{6,38},{7,39},{8,40},{9,... | collective-permute-start | bytes 3145736 | tf_op jit(solution)/shard_map/ppermute | solution.py:261
  122.7 40.1 %collective-permute-done.10.rest_1_ = bf16[1024,512]{1,0:T(8,128)(2,1)} collective-permute-done((bf16[1024,512]{1,0:T(8,128)(2,1)}, bf16[1024,512]{1,0:T(8,128)(2,1)}, u32[]{:S(2)}, u32[]{:S(2)}) %collective-permute-start.10) | collective-permute-done | bytes 1048608 | tf_op jit(solution)/shard_map/ppermute | solution.py:261
  162.8 22.1 %collective-permute-done.11.rest_2_ = bf16[1024,512]{1,0:T(8,128)(2,1)} collective-permute-done((bf16[1024,512]{1,0:T(8,128)(2,1)}, bf16[1024,512]{1,0:T(8,128)(2,1)}, u32[]{:S(2)}, u32[]{:S(2)}) %collective-permute-start.11) | collective-permute-done | bytes 1048608 | tf_op jit(solution)/shard_map/ppermute | solution.py:261
  185.4 6.7 %add_convert_fusion.1 = bf16[2048,512]{1,0:T(8,128)(2,1)} fusion(bf16[2048,512]{1,0:T(8,128)(2,1)} %collective-permute-done.17, bf16[1024,2048]{1,0:T(8,128)(2,1)} %grad_blocks.2, bf16[1024,512]{1,0:T(8,128)(2,1)S(1)} %copy-done.3), kind=kOutput, calls=%fused_computation.3 | convolution fusion | flops 2150629376 | bytes 9437184 | tf_op jit(solution)/shard_map/dot_general | solution.py:310
  192.1 8.8 %all-to-all-start = ((bf16[64,32,512]{2,1,0:T(8,128)(2,1)}), bf16[64,32,512]{2,1,0:T(8,128)(2,1)}, u32[]{:S(2)}, u32[]{:S(2)}) async-start(bf16[64,32,512]{2,1,0:T(8,128)(2,1)} %bitcast.48), calls=%async_computation | async-start | bytes 4194304 | tf_op jit(solution)/shard_map/all_to_all | solution.py:312
  201.5 40.1 %energy_share.1 = f32[1,256]{1,0:T(1,128)} custom-call(s32[1040]{0:T(1024)} %concatenate.13.index, s32[256]{0:T(256)} %get-tuple-element.19.tiles, s32[256]{0:T(256)} %get-tuple-element.18.rows, s32[1]{0:T(128)} %bitcast.4.total, s32[64]{0:T(128)} %fusion.8.who, bf16[64,32,256]{2,1,0:T(8,128)(2,1)} %collective-permute-done.prev0.prev, ...), custom_call_target="tpu_custom_call" | custom-call | flops 17179869184 | bytes 16777216 | tf_op jit(solution)/shard_map/energy_share/pallas_call | solution.py:226
  243.3 10.5 %all-to-all-start.1 = ((f32[64,1,256]{2,1,0:T(1,128)}), f32[64,1,256]{2,1,0:T(1,128)S(1)}, u32[]{:S(2)}, u32[]{:S(2)}) async-start(f32[64,1,256]{2,1,0:T(1,128)} %broadcast_in_dim.44), calls=%async_computation.1 | async-start | bytes 131072 | tf_op jit(solution)/shard_map/all_to_all | solution.py:317
  253.8 1.9 convert_reduce_fusion
  255.7 2.0 all_gather.3
  257.7 5.7 %all-to-all-done.1 = f32[64,1,256]{2,1,0:T(1,128)S(1)} async-done(((f32[64,1,256]{2,1,0:T(1,128)}), f32[64,1,256]{2,1,0:T(1,128)S(1)}, u32[]{:S(2)}, u32[]{:S(2)}) %all-to-all-start.1) | async-done | bytes 65568 | tf_op jit(solution)/shard_map/all_to_all | solution.py:317
  (78 shorter events, 9.2 us)
Async XLA Ops:
  0.6 11.9 %copy-start.8 = (s32[1,64]{1,0:T(1,128)S(1)}, s32[1,64]{1,0:T(1,128)}, u32[]{:S(2)}) copy-start(s32[1,64]{1,0:T(1,128)} %param.9) | copy-start | bytes 772
  0.6 12.9 %copy-start.5 = (s32[1,64,16]{1,2,0:T(8,128)S(1)}, s32[1,64,16]{1,2,0:T(8,128)}, u32[]{:S(2)}) copy-start(s32[1,64,16]{1,2,0:T(8,128)} %param.8) | copy-start | bytes 12292
  3.7 32.3 %collective-permute-start = (bf16[64,32,256]{2,1,0:T(8,128)(2,1)}, bf16[64,32,256]{2,1,0:T(8,128)(2,1)}, u32[]{:S(2)}, u32[]{:S(2)}) collective-permute-start(bf16[64,32,256]{2,1,0:T(8,128)(2,1)} %get-tuple-element.16), channel_id=1, source_target_pairs={{0,1},{1,2},{2,3},{3,4},{4,5},{5,6},{6,7},{7,8},{8,9},{9,10},{10,1... | collective-permute-start | bytes 3145736 | tf_op jit(solution)/shard_map/ppermute | solution.py:272
  5.3 30.7 %collective-permute-start.1 = (bf16[64,32,256]{2,1,0:T(8,128)(2,1)}, bf16[64,32,256]{2,1,0:T(8,128)(2,1)}, u32[]{:S(2)}, u32[]{:S(2)}) collective-permute-start(bf16[64,32,256]{2,1,0:T(8,128)(2,1)} %get-tuple-element.16), channel_id=1, source_target_pairs={{1,0},{2,1},{3,2},{4,3},{5,4},{6,5},{7,6},{8,7},{9,8},{10,9},{11,1... | collective-permute-start | bytes 3145736 | tf_op jit(solution)/shard_map/ppermute | solution.py:273
  19.0 8.8 %copy-start = (bf16[1,64,64,256]{3,2,1,0:T(8,128)(2,1)S(1)}, bf16[1,64,64,256]{3,2,1,0:T(8,128)(2,1)}, u32[]{:S(2)}) copy-start(bf16[1,64,64,256]{3,2,1,0:T(8,128)(2,1)} %param.7) | copy-start | bytes 6291460
  19.0 8.8 %copy-start.7 = (f32[1,256]{1,0:T(1,128)S(1)}, f32[1,256]{1,0:T(1,128)}, u32[]{:S(2)}) copy-start(f32[1,256]{1,0:T(1,128)} %param.10) | copy-start | bytes 3076
  26.5 69.5 %copy-start.1 = (bf16[1024,512]{1,0:T(8,128)(2,1)}, bf16[1024,512]{1,0:T(8,128)(2,1)S(1)}, u32[]{:S(2)}) copy-start(bf16[1024,512]{1,0:T(8,128)(2,1)S(1)} %get-tuple-element.14.theirs) | copy-start | bytes 3145732
  36.0 41.0 %collective-permute-start.2 = (bf16[64,32,256]{2,1,0:T(8,128)(2,1)}, bf16[64,32,256]{2,1,0:T(8,128)(2,1)S(1)}, u32[]{:S(2)}, u32[]{:S(2)}) collective-permute-start(bf16[64,32,256]{2,1,0:T(8,128)(2,1)} %get-tuple-element.8), channel_id=1, source_target_pairs={{0,1},{1,2},{2,3},{3,4},{4,5},{5,6},{6,7},{7,8},{8,9},{9,10},{10,1... | collective-permute-start | bytes 3145736 | tf_op jit(solution)/shard_map/ppermute | solution.py:288
  36.0 44.4 %collective-permute-start.3 = (bf16[64,32,256]{2,1,0:T(8,128)(2,1)}, bf16[64,32,256]{2,1,0:T(8,128)(2,1)}, u32[]{:S(2)}, u32[]{:S(2)}) collective-permute-start(bf16[64,32,256]{2,1,0:T(8,128)(2,1)} %get-tuple-element.8), channel_id=1, source_target_pairs={{1,0},{2,1},{3,2},{4,3},{5,4},{6,5},{7,6},{8,7},{9,8},{10,9},{11,1... | collective-permute-start | bytes 3145736 | tf_op jit(solution)/shard_map/ppermute | solution.py:289
  59.2 6.0 %copy-start.4 = (bf16[1024,64]{0,1:T(8,128)(2,1)S(1)}, bf16[1024,64]{0,1:T(8,128)(2,1)}, u32[]{:S(2)}) copy-start(bf16[1024,64]{0,1:T(8,128)(2,1)} %param.11) | copy-start | bytes 393220
  65.2 37.0 %collective-permute-start.18 = (bf16[2048,512]{1,0:T(8,128)(2,1)}, bf16[2048,512]{1,0:T(8,128)(2,1)}, u32[]{:S(2)}, u32[]{:S(2)}) collective-permute-start(bf16[2048,512]{1,0:T(8,128)(2,1)} %convolution_convert_fusion), channel_id=1, source_target_pairs={{0,64},{64,0},{1,65},{65,1},{2,66},{66,2},{3,67},{67,3},{4,68},{68... | collective-permute-start | bytes 6291464 | tf_op jit(solution)/shard_map/ppermute | solution.py:309
  65.3 7.2 %collective-permute-start.4 = (bf16[64,512]{1,0:T(8,128)(2,1)S(1)}, bf16[64,512]{1,0:T(8,128)(2,1)S(1)}, u32[]{:S(2)}, u32[]{:S(2)}) collective-permute-start(bf16[64,512]{1,0:T(8,128)(2,1)S(1)} %get-tuple-element.13), channel_id=1, source_target_pairs={{0,1},{1,2},{2,3},{3,0},{4,5},{5,6},{6,7},{7,4},{8,9},{9,10},{10,1... | collective-permute-start | bytes 196616 | tf_op jit(solution)/shard_map/ppermute | solution.py:261
  65.3 7.1 %collective-permute-start.5 = (bf16[64,512]{1,0:T(8,128)(2,1)S(1)}, bf16[64,512]{1,0:T(8,128)(2,1)S(1)}, u32[]{:S(2)}, u32[]{:S(2)}) collective-permute-start(bf16[64,512]{1,0:T(8,128)(2,1)S(1)} %get-tuple-element.13), channel_id=1, source_target_pairs={{0,2},{1,3},{2,0},{3,1},{4,6},{5,7},{6,4},{7,5},{8,10},{9,11},{10,... | collective-permute-start | bytes 196616 | tf_op jit(solution)/shard_map/ppermute | solution.py:261
  72.4 4.3 %collective-permute-start.6 = (bf16[64,512]{1,0:T(8,128)(2,1)S(1)}, bf16[64,512]{1,0:T(8,128)(2,1)S(1)}, u32[]{:S(2)}, u32[]{:S(2)}) collective-permute-start(bf16[64,512]{1,0:T(8,128)(2,1)S(1)} %get-tuple-element.13), channel_id=1, source_target_pairs={{0,3},{1,0},{2,1},{3,2},{4,7},{5,4},{6,5},{7,6},{8,11},{9,8},{10,9... | collective-permute-start | bytes 196616 | tf_op jit(solution)/shard_map/ppermute | solution.py:261
  76.7 25.5 %collective-permute-start.7 = (bf16[256,512]{1,0:T(8,128)(2,1)S(1)}, bf16[256,512]{1,0:T(8,128)(2,1)S(1)}, u32[]{:S(2)}, u32[]{:S(2)}) collective-permute-start(bf16[256,512]{1,0:T(8,128)(2,1)S(1)} %pad_maximum_fusion), channel_id=1, source_target_pairs={{0,4},{1,5},{2,6},{3,7},{4,8},{5,9},{6,10},{7,11},{8,12},{9,13},{1... | collective-permute-start | bytes 786440 | tf_op jit(solution)/shard_map/ppermute | solution.py:261
  76.8 36.7 %collective-permute-start.8 = (bf16[256,512]{1,0:T(8,128)(2,1)S(1)}, bf16[256,512]{1,0:T(8,128)(2,1)}, u32[]{:S(2)}, u32[]{:S(2)}) collective-permute-start(bf16[256,512]{1,0:T(8,128)(2,1)S(1)} %pad_maximum_fusion), channel_id=1, source_target_pairs={{0,8},{1,9},{2,10},{3,11},{4,12},{5,13},{6,14},{7,15},{8,0},{9,1},... | collective-permute-start | bytes 786440 | tf_op jit(solution)/shard_map/ppermute | solution.py:261
  77.0 38.3 %collective-permute-start.9 = (bf16[256,512]{1,0:T(8,128)(2,1)S(1)}, bf16[256,512]{1,0:T(8,128)(2,1)}, u32[]{:S(2)}, u32[]{:S(2)}) collective-permute-start(bf16[256,512]{1,0:T(8,128)(2,1)S(1)} %pad_maximum_fusion), channel_id=1, source_target_pairs={{0,12},{1,13},{2,14},{3,15},{4,0},{5,1},{6,2},{7,3},{8,4},{9,5},{1... | collective-permute-start | bytes 786440 | tf_op jit(solution)/shard_map/ppermute | solution.py:261
  96.0 6.2 %copy-start.2 = (bf16[1024,512]{1,0:T(8,128)(2,1)S(1)}, bf16[1024,512]{1,0:T(8,128)(2,1)}, u32[]{:S(2)}) copy-start(bf16[1024,512]{1,0:T(8,128)(2,1)} %get-tuple-element.15.mine) | copy-start | bytes 3145732
  96.0 6.2 %copy-start.10 = (bf16[1024,2048]{1,0:T(8,128)(2,1)S(1)}, bf16[1024,2048]{1,0:T(8,128)(2,1)}, u32[]{:S(2)}) copy-start(bf16[1024,2048]{1,0:T(8,128)(2,1)} %grad_blocks.3) | copy-start | bytes 12582916
  102.2 83.2 %collective-permute-start.17 = (bf16[2048,512]{1,0:T(8,128)(2,1)}, bf16[2048,512]{1,0:T(8,128)(2,1)}, u32[]{:S(2)}, u32[]{:S(2)}) collective-permute-start(bf16[2048,512]{1,0:T(8,128)(2,1)} %convolution_convert_fusion.1), channel_id=1, source_target_pairs={{0,64},{64,0},{1,65},{65,1},{2,66},{66,2},{3,67},{67,3},{4,68},{68... | collective-permute-start | bytes 6291464 | tf_op jit(solution)/shard_map/ppermute | solution.py:309
  102.2 5.8 %copy-start.6 = (bf16[1024,512]{1,0:T(8,128)(2,1)}, bf16[1024,512]{1,0:T(8,128)(2,1)S(1)}, u32[]{:S(2)}) copy-start(bf16[1024,512]{1,0:T(8,128)(2,1)S(1)} %constant_dynamic-update-slice_fusion.2) | copy-start | bytes 3145732
  108.1 77.3 %copy-start.3 = (bf16[1024,512]{1,0:T(8,128)(2,1)S(1)}, bf16[1024,512]{1,0:T(8,128)(2,1)}, u32[]{:S(2)}) copy-start(bf16[1024,512]{1,0:T(8,128)(2,1)} %get-tuple-element.15.mine) | copy-start | bytes 3145732
  108.1 84.1 %all-to-all-start.2 = ((bf16[64,32,512]{2,1,0:T(8,128)(2,1)}), bf16[64,32,512]{2,1,0:T(8,128)(2,1)S(1)}, u32[]{:S(2)}, u32[]{:S(2)}) async-start(bf16[64,32,512]{2,1,0:T(8,128)(2,1)} %bitcast.49), calls=%async_computation.2 | async-start | bytes 4194304 | tf_op jit(solution)/shard_map/all_to_all | solution.py:312
  116.9 45.9 %collective-permute-start.10 = (bf16[1024,512]{1,0:T(8,128)(2,1)}, bf16[1024,512]{1,0:T(8,128)(2,1)}, u32[]{:S(2)}, u32[]{:S(2)}) collective-permute-start(bf16[1024,512]{1,0:T(8,128)(2,1)} %constant_dynamic-update-slice_fusion.rest_0_), channel_id=1, source_target_pairs={{0,16},{1,17},{2,18},{3,19},{4,20},{5,21},{6,22},{7,23},{8,24},{9,... | collective-permute-start | bytes 3145736 | tf_op jit(solution)/shard_map/ppermute | solution.py:261
  118.5 66.4 %collective-permute-start.11 = (bf16[1024,512]{1,0:T(8,128)(2,1)}, bf16[1024,512]{1,0:T(8,128)(2,1)}, u32[]{:S(2)}, u32[]{:S(2)}) collective-permute-start(bf16[1024,512]{1,0:T(8,128)(2,1)} %constant_dynamic-update-slice_fusion.rest_0_), channel_id=1, source_target_pairs={{0,32},{1,33},{2,34},{3,35},{4,36},{5,37},{6,38},{7,39},{8,40},{9,... | collective-permute-start | bytes 3145736 | tf_op jit(solution)/shard_map/ppermute | solution.py:261
  121.4 63.5 %collective-permute-start.12 = (bf16[1024,512]{1,0:T(8,128)(2,1)}, bf16[1024,512]{1,0:T(8,128)(2,1)}, u32[]{:S(2)}, u32[]{:S(2)}) collective-permute-start(bf16[1024,512]{1,0:T(8,128)(2,1)} %constant_dynamic-update-slice_fusion.rest_0_), channel_id=1, source_target_pairs={{0,48},{1,49},{2,50},{3,51},{4,52},{5,53},{6,54},{7,55},{8,56},{9,... | collective-permute-start | bytes 3145736 | tf_op jit(solution)/shard_map/ppermute | solution.py:261
  122.7 78.8 %collective-permute-start.13 = (bf16[1024,512]{1,0:T(8,128)(2,1)}, bf16[1024,512]{1,0:T(8,128)(2,1)}, u32[]{:S(2)}, u32[]{:S(2)}) collective-permute-start(bf16[1024,512]{1,0:T(8,128)(2,1)} %constant_dynamic-update-slice_fusion.rest_0_), channel_id=1, source_target_pairs={{0,64},{64,0},{1,65},{65,1},{2,66},{66,2},{3,67},{67,3},{4,68},{68... | collective-permute-start | bytes 3145736 | tf_op jit(solution)/shard_map/ppermute | solution.py:280
  162.8 38.7 %collective-permute-start.14 = (bf16[1024,512]{1,0:T(8,128)(2,1)}, bf16[1024,512]{1,0:T(8,128)(2,1)}, u32[]{:S(2)}, u32[]{:S(2)}) collective-permute-start(bf16[1024,512]{1,0:T(8,128)(2,1)} %collective-permute-done.10.rest_1_), channel_id=1, source_target_pairs={{0,64},{64,0},{1,65},{65,1},{2,66},{66,2},{3,67},{67,3},{4,68},{68... | collective-permute-start | bytes 3145736 | tf_op jit(solution)/shard_map/ppermute | solution.py:280
  184.9 16.6 %collective-permute-start.15 = (bf16[1024,512]{1,0:T(8,128)(2,1)}, bf16[1024,512]{1,0:T(8,128)(2,1)}, u32[]{:S(2)}, u32[]{:S(2)}) collective-permute-start(bf16[1024,512]{1,0:T(8,128)(2,1)} %collective-permute-done.11.rest_2_), channel_id=1, source_target_pairs={{0,64},{64,0},{1,65},{65,1},{2,66},{66,2},{3,67},{67,3},{4,68},{68... | collective-permute-start | bytes 3145736 | tf_op jit(solution)/shard_map/ppermute | solution.py:280
  184.9 16.6 %collective-permute-start.16 = (bf16[1024,512]{1,0:T(8,128)(2,1)}, bf16[1024,512]{1,0:T(8,128)(2,1)}, u32[]{:S(2)}, u32[]{:S(2)}) collective-permute-start(bf16[1024,512]{1,0:T(8,128)(2,1)} %collective-permute-done.12.rest_3_), channel_id=1, source_target_pairs={{0,64},{64,0},{1,65},{65,1},{2,66},{66,2},{3,67},{67,3},{4,68},{68... | collective-permute-start | bytes 3145736 | tf_op jit(solution)/shard_map/ppermute | solution.py:280
  192.1 49.8 %all-to-all-start = ((bf16[64,32,512]{2,1,0:T(8,128)(2,1)}), bf16[64,32,512]{2,1,0:T(8,128)(2,1)}, u32[]{:S(2)}, u32[]{:S(2)}) async-start(bf16[64,32,512]{2,1,0:T(8,128)(2,1)} %bitcast.48), calls=%async_computation | async-start | bytes 4194304 | tf_op jit(solution)/shard_map/all_to_all | solution.py:312
  243.3 20.1 %all-to-all-start.1 = ((f32[64,1,256]{2,1,0:T(1,128)}), f32[64,1,256]{2,1,0:T(1,128)S(1)}, u32[]{:S(2)}, u32[]{:S(2)}) async-start(f32[64,1,256]{2,1,0:T(1,128)} %broadcast_in_dim.44), calls=%async_computation.1 | async-start | bytes 131072 | tf_op jit(solution)/shard_map/all_to_all | solution.py:317
  (1 other events, 3.4 us)

commit v5 on v4

--- a/solution.py
+++ b/solution.py
@@ -312,9 +312,12 @@
         parts = lax.all_to_all(summed, "space", 0, 0, tiled=True)
         arrived.append(parts)
     partial = energy_share(plan, who, prev, own, following, mine, theirs, sheets, factor)
-    partial, arrived[1] = lax.optimization_barrier((partial, arrived[1]))
-    copies = jnp.broadcast_to(partial, (nspace, BANDS))
-    energies = jnp.sum(lax.all_to_all(copies, "space", 0, 0, tiled=True), axis=0, keepdims=True)
+    energies = partial
+    for axis, place in ((2, myself % 4), (1, myself // 4 % 4), (0, myself // 16)):
+        pieces = jnp.concatenate(spread(energies, axis), axis=0)
+        energies = sum(
+            lax.dynamic_slice_in_dim(pieces, (place - spot) % 4, 1, 0) for spot in range(4)
+        )
     shares = [
         jnp.sum(parts.reshape(nspace, CHUNK, half).astype(jnp.float32), axis=0) for parts in arrived
     ]

time: 266 us -> 271 us (1.019)
  waiting for transfers between devices: 85.4 us -> 94.4 us
  starting transfers between devices: 51.1 us -> 46.7 us
    ppermute x9 -> x18, waiting for transfers between devices: 73.4 us -> 87.9 us  [spread(): lax.ppermute(value, 'space', ring(axis, hop))]
    all_to_all x1 -> x0, starting transfers between devices: 10.5 us -> none  [step(): lax.all_to_all(copies, 'space', 0, 0, tiled=True)]
    ppermute x9 -> x18, starting transfers between devices: 9.5 us -> 15.9 us  [spread(): lax.ppermute(value, 'space', ring(axis, hop))]
    all_to_all x1 -> x0, waiting for transfers between devices: 5.66 us -> none  [step(): lax.all_to_all(copies, 'space', 0, 0, tiled=True)]
    unnamed x30 -> x28, local copies, waits for them, and re-layouts: 2.55 us -> 5.8 us
  transfers between devices with their start and end apart: 22 -> 30, of which waited for: 6 -> 12; matrix products, arithmetic and copies ran while one was open for 18% -> 18% of each run, Pallas kernels for 27% -> 26%
where the time goes in v5:
time: 271 us; the launch traced here: 270 us
  waiting for transfers between devices  94.4 us (35%)
  Pallas kernels  71.1 us (26%)
  starting transfers between devices  46.7 us (17%)
  matrix products  24 us (9%)
  local copies, waits for them, and re-layouts  22.9 us (8%)
  other arithmetic  7.65 us (3%)
    ppermute x18, waiting for transfers between devices, spread(): lax.ppermute(value, 'space', ring(axis, hop))  87.9 us
    pallas_call x1, Pallas kernels, energy_share(): pl.pallas_call(functools.partial(energy_kernel, factor=factor), grid_spec...  40.1 us
    pallas_call x2, Pallas kernels, grad_blocks(): pl.pallas_call(functools.partial(grad_blocks_kernel, part=part, factor=fa...  31.1 us
    ppermute x18, starting transfers between devices, spread(): lax.ppermute(value, 'space', ring(axis, hop))  15.9 us
    all_to_all x2, starting transfers between devices, step(): parts = lax.all_to_all(summed, 'space', 0, 0, tiled=True)  13.9 us
    dot_general x2, matrix products, step(): lax.dot_general(blocks, theirs, over_edges, preferred_element_type=jnp.fl...  12 us
    dot_general x2, matrix products, step(): lax.dot_general(blocks, mine, over_edges, preferred_element_type=jnp.floa...  12 us
    reshape x3, local copies, waits for them, and re-layouts, step(): features.reshape(TILES // 2, 2, 4, 4, FEAT).transpose(0, 3, 1, 2, 4)  9.26 us
  transfers between devices with their start and end apart: 30, of which 12 were waited for; matrix products, arithmetic and copies ran while one was open for 18% of the time, Pallas kernels for 26%

profile of v5, /device:TPU:0, one launch (start us, length us, event | category | flops | bytes accessed | tf_op | source)
XLA Modules:
  0.0 269.7 jit_solution(8585009493697224412)
XLA Ops:
  0.6 3.1 %fusion.27 = (bf16[64,32,256]{2,1,0:T(8,128)(2,1)}, bf16[64,32,256]{2,1,0:T(8,128)(2,1)}) fusion(bf16[64,64,256]{2,1,0:T(8,128)(2,1)} %bitcast.38), kind=kLoop, calls=%fused_computation.104 | loop fusion | bytes 4194304 | tf_op jit(solution)/shard_map/slice | solution.py:272
  3.7 1.6 collective-permute-start
  5.3 7.2 %collective-permute-start.1 = (bf16[64,32,256]{2,1,0:T(8,128)(2,1)}, bf16[64,32,256]{2,1,0:T(8,128)(2,1)}, u32[]{:S(2)}, u32[]{:S(2)}) collective-permute-start(bf16[64,32,256]{2,1,0:T(8,128)(2,1)} %get-tuple-element.12), channel_id=1, source_target_pairs={{1,0},{2,1},{3,2},{4,3},{5,4},{6,5},{7,6},{8,7},{9,8},{10,9},{11,1... | collective-permute-start | bytes 3145736 | tf_op jit(solution)/shard_map/ppermute | solution.py:273
  13.8 2.7 %reshape.102 = bf16[32,2,4,4,1024]{4,3,2,1,0:T(4,128)(2,1)S(1)} reshape(bf16[1,64,16,1024]{3,2,1,0:T(8,128)(2,1)} %param.6) | data formatting | bytes 4194304 | tf_op jit(solution)/shard_map/reshape | solution.py:299
  16.5 2.4 copy.17
  18.9 4.1 %reshape.103 = bf16[1024,1024]{1,0:T(8,128)(2,1)} reshape(bf16[32,4,2,4,1024]{4,3,2,1,0:T(4,128)(2,1)} %bitcast.42) | data formatting | bytes 4194304 | tf_op jit(solution)/shard_map/reshape | solution.py:299
  23.8 2.7 constant_dynamic-slice_fusion.12
  27.6 1.9 multiply_convert_fusion.weighted
  29.5 6.5 %collective-permute-done.prev0.prev = bf16[64,32,256]{2,1,0:T(8,128)(2,1)} collective-permute-done((bf16[64,32,256]{2,1,0:T(8,128)(2,1)}, bf16[64,32,256]{2,1,0:T(8,128)(2,1)}, u32[]{:S(2)}, u32[]{:S(2)}) %collective-permute-start) | collective-permute-done | bytes 1048608 | tf_op jit(solution)/shard_map/ppermute | solution.py:272
  36.0 7.5 %collective-permute-start.3 = (bf16[64,32,256]{2,1,0:T(8,128)(2,1)}, bf16[64,32,256]{2,1,0:T(8,128)(2,1)}, u32[]{:S(2)}, u32[]{:S(2)}) collective-permute-start(bf16[64,32,256]{2,1,0:T(8,128)(2,1)} %get-tuple-element.6), channel_id=1, source_target_pairs={{1,0},{2,1},{3,2},{4,3},{5,4},{6,5},{7,6},{8,7},{9,8},{10,9},{11,1... | collective-permute-start | bytes 3145736 | tf_op jit(solution)/shard_map/ppermute | solution.py:289
  43.4 15.5 %grad_blocks.2 = bf16[1024,2048]{1,0:T(8,128)(2,1)} custom-call(s32[1040]{0:T(1024)} %concatenate.22.index, s32[256]{0:T(256)} %get-tuple-element.15.tiles, s32[256]{0:T(256)} %get-tuple-element.14.rows, s32[1]{0:T(128)} %bitcast.4.total, bf16[64,32,256]{2,1,0:T(8,128)(2,1)} %collective-permute-done.prev0.prev, bf16[64,64,256]{2,1,0:T(8,128)(2,1)} %bitcast.39, ...), custom_call_target="tpu_custom_call" | custom-call | flops 4294967296 | bytes 12582912 | tf_op jit(solution)/shard_map/grad_blocks/pallas_call | solution.py:116
  59.0 6.0 %convolution_convert_fusion.1 = bf16[2048,512]{1,0:T(8,128)(2,1)} fusion(bf16[1024,2048]{1,0:T(8,128)(2,1)} %grad_blocks.2, bf16[1024,512]{1,0:T(8,128)(2,1)S(1)} %get-tuple-element.10.theirs), kind=kOutput, calls=%fused_computation.6 | convolution fusion | flops 2148532224 | bytes 7340032 | tf_op jit(solution)/shard_map/dot_general | solution.py:308
  65.6 7.1 %collective-permute-done.4 = bf16[64,512]{1,0:T(8,128)(2,1)S(1)} collective-permute-done((bf16[64,512]{1,0:T(8,128)(2,1)S(1)}, bf16[64,512]{1,0:T(8,128)(2,1)S(1)}, u32[]{:S(2)}, u32[]{:S(2)}) %collective-permute-start.4) | collective-permute-done | bytes 65568 | tf_op jit(solution)/shard_map/ppermute | solution.py:261
  72.7 4.3 %collective-permute-done.6 = bf16[64,512]{1,0:T(8,128)(2,1)S(1)} collective-permute-done((bf16[64,512]{1,0:T(8,128)(2,1)S(1)}, bf16[64,512]{1,0:T(8,128)(2,1)S(1)}, u32[]{:S(2)}, u32[]{:S(2)}) %collective-permute-start.6) | collective-permute-done | bytes 65568 | tf_op jit(solution)/shard_map/ppermute | solution.py:261
  79.0 11.6 %collective-permute-done.7 = bf16[256,512]{1,0:T(8,128)(2,1)S(1)} collective-permute-done((bf16[256,512]{1,0:T(8,128)(2,1)S(1)}, bf16[256,512]{1,0:T(8,128)(2,1)S(1)}, u32[]{:S(2)}, u32[]{:S(2)}) %collective-permute-start.7) | collective-permute-done | bytes 262176 | tf_op jit(solution)/shard_map/ppermute | solution.py:261
  93.1 15.6 %grad_blocks.3 = bf16[1024,2048]{1,0:T(8,128)(2,1)} custom-call(s32[1040]{0:T(1024)} %concatenate.22.index, s32[256]{0:T(256)} %get-tuple-element.15.tiles, s32[256]{0:T(256)} %get-tuple-element.14.rows, s32[1]{0:T(128)} %bitcast.4.total, bf16[64,32,256]{2,1,0:T(8,128)(2,1)} %copy-done.8, bf16[64,64,256]{2,1,0:T(8,128)(2,1)} %bitcast.40, ...), custom_call_target="tpu_custom_call" | custom-call | flops 4294967296 | bytes 12582912 | tf_op jit(solution)/shard_map/grad_blocks/pallas_call | solution.py:116
  108.7 6.0 %convolution_convert_fusion = bf16[2048,512]{1,0:T(8,128)(2,1)} fusion(bf16[1024,2048]{1,0:T(8,128)(2,1)} %grad_blocks.3, bf16[1024,512]{1,0:T(8,128)(2,1)S(1)} %get-tuple-element.10.theirs), kind=kOutput, calls=%fused_computation.5 | convolution fusion | flops 2148532224 | bytes 7340032 | tf_op jit(solution)/shard_map/dot_general | solution.py:308
  116.5 2.2 collective-permute-start.12
  118.8 5.4 %add_convert_fusion.1 = bf16[2048,512]{1,0:T(8,128)(2,1)} fusion(bf16[2048,512]{1,0:T(8,128)(2,1)} %collective-permute-done.26, bf16[1024,2048]{1,0:T(8,128)(2,1)S(1)} %copy-done.9, bf16[1024,512]{1,0:T(8,128)(2,1)S(1)} %copy-done.2), kind=kOutput, calls=%fused_computation.3 | convolution fusion | flops 2150629376 | bytes 9437184 | tf_op jit(solution)/shard_map/dot_general | solution.py:310
  124.2 7.7 %all-to-all-start = ((bf16[64,32,512]{2,1,0:T(8,128)(2,1)}), bf16[64,32,512]{2,1,0:T(8,128)(2,1)S(1)}, u32[]{:S(2)}, u32[]{:S(2)}) async-start(bf16[64,32,512]{2,1,0:T(8,128)(2,1)} %bitcast.43), calls=%async_computation | async-start | bytes 4194304 | tf_op jit(solution)/shard_map/all_to_all | solution.py:312
  132.0 52.2 %collective-permute-done.10.rest_1_ = bf16[1024,512]{1,0:T(8,128)(2,1)} collective-permute-done((bf16[1024,512]{1,0:T(8,128)(2,1)}, bf16[1024,512]{1,0:T(8,128)(2,1)}, u32[]{:S(2)}, u32[]{:S(2)}) %collective-permute-start.10) | collective-permute-done | bytes 1048608 | tf_op jit(solution)/shard_map/ppermute | solution.py:261
  185.3 6.6 %add_convert_fusion = bf16[2048,512]{1,0:T(8,128)(2,1)} fusion(bf16[2048,512]{1,0:T(8,128)(2,1)} %collective-permute-done.27, bf16[1024,2048]{1,0:T(8,128)(2,1)} %grad_blocks.3, bf16[1024,512]{1,0:T(8,128)(2,1)S(1)} %copy-done.3), kind=kOutput, calls=%fused_computation.1 | convolution fusion | flops 2150629376 | bytes 9437184 | tf_op jit(solution)/shard_map/dot_general | solution.py:310
  191.9 6.2 %all-to-all-start.1 = ((bf16[64,32,512]{2,1,0:T(8,128)(2,1)}), bf16[64,32,512]{2,1,0:T(8,128)(2,1)}, u32[]{:S(2)}, u32[]{:S(2)}) async-start(bf16[64,32,512]{2,1,0:T(8,128)(2,1)} %bitcast.44), calls=%async_computation.1 | async-start | bytes 4194304 | tf_op jit(solution)/shard_map/all_to_all | solution.py:312
  198.2 40.1 %energy_share.1 = f32[1,256]{1,0:T(1,128)} custom-call(s32[1040]{0:T(1024)} %concatenate.22.index, s32[256]{0:T(256)} %get-tuple-element.15.tiles, s32[256]{0:T(256)} %get-tuple-element.14.rows, s32[1]{0:T(128)} %bitcast.4.total, s32[64]{0:T(128)} %fusion.17.who, bf16[64,32,256]{2,1,0:T(8,128)(2,1)} %collective-permute-done.prev0.prev, ...), custom_call_target="tpu_custom_call" | custom-call | flops 17179869184 | bytes 16777216 | tf_op jit(solution)/shard_map/energy_share/pallas_call | solution.py:226
  238.2 2.1 collective-permute-start.19
  242.1 3.5 %collective-permute-done.18 = f32[1,256]{1,0:T(1,128)S(1)} collective-permute-done((f32[1,256]{1,0:T(1,128)}, f32[1,256]{1,0:T(1,128)S(1)}, u32[]{:S(2)}, u32[]{:S(2)}) %collective-permute-start.18) | collective-permute-done | bytes 1056 | tf_op jit(solution)/shard_map/ppermute | solution.py:261
  247.6 2.1 collective-permute-start.22
  251.3 3.4 %collective-permute-done.21 = f32[1,256]{1,0:T(1,128)S(1)} collective-permute-done((f32[1,256]{1,0:T(1,128)S(1)}, f32[1,256]{1,0:T(1,128)S(1)}, u32[]{:S(2)}, u32[]{:S(2)}) %collective-permute-start.21) | collective-permute-done | bytes 1056 | tf_op jit(solution)/shard_map/ppermute | solution.py:261
  255.3 3.7 %collective-permute-start.25 = (f32[1,256]{1,0:T(1,128)S(1)}, f32[1,256]{1,0:T(1,128)S(1)}, u32[]{:S(2)}, u32[]{:S(2)}) collective-permute-start(f32[1,256]{1,0:T(1,128)S(1)} %fusion.12), channel_id=1, source_target_pairs={{0,48},{1,49},{2,50},{3,51},{4,52},{5,53},{6,54},{7,55},{8,56},{9,... | collective-permute-start | bytes 3080 | tf_op jit(solution)/shard_map/ppermute | solution.py:261
  260.3 3.7 %collective-permute-done.24 = f32[1,256]{1,0:T(1,128)S(1)} collective-permute-done((f32[1,256]{1,0:T(1,128)S(1)}, f32[1,256]{1,0:T(1,128)S(1)}, u32[]{:S(2)}, u32[]{:S(2)}) %collective-permute-start.24) | collective-permute-done | bytes 1056 | tf_op jit(solution)/shard_map/ppermute | solution.py:261
  265.1 1.9 convert_reduce_fusion
  267.0 2.0 all_gather.3
  (96 shorter events, 20.5 us)
Async XLA Ops:
  3.7 32.3 %collective-permute-start = (bf16[64,32,256]{2,1,0:T(8,128)(2,1)}, bf16[64,32,256]{2,1,0:T(8,128)(2,1)}, u32[]{:S(2)}, u32[]{:S(2)}) collective-permute-start(bf16[64,32,256]{2,1,0:T(8,128)(2,1)} %get-tuple-element.12), channel_id=1, source_target_pairs={{0,1},{1,2},{2,3},{3,4},{4,5},{5,6},{6,7},{7,8},{8,9},{9,10},{10,1... | collective-permute-start | bytes 3145736 | tf_op jit(solution)/shard_map/ppermute | solution.py:272
  5.3 30.7 %collective-permute-start.1 = (bf16[64,32,256]{2,1,0:T(8,128)(2,1)}, bf16[64,32,256]{2,1,0:T(8,128)(2,1)}, u32[]{:S(2)}, u32[]{:S(2)}) collective-permute-start(bf16[64,32,256]{2,1,0:T(8,128)(2,1)} %get-tuple-element.12), channel_id=1, source_target_pairs={{1,0},{2,1},{3,2},{4,3},{5,4},{6,5},{7,6},{8,7},{9,8},{10,9},{11,1... | collective-permute-start | bytes 3145736 | tf_op jit(solution)/shard_map/ppermute | solution.py:273
  26.5 82.2 %copy-start.1 = (bf16[1024,512]{1,0:T(8,128)(2,1)}, bf16[1024,512]{1,0:T(8,128)(2,1)S(1)}, u32[]{:S(2)}) copy-start(bf16[1024,512]{1,0:T(8,128)(2,1)S(1)} %get-tuple-element.10.theirs) | copy-start | bytes 3145732
  36.0 56.2 %collective-permute-start.2 = (bf16[64,32,256]{2,1,0:T(8,128)(2,1)}, bf16[64,32,256]{2,1,0:T(8,128)(2,1)S(1)}, u32[]{:S(2)}, u32[]{:S(2)}) collective-permute-start(bf16[64,32,256]{2,1,0:T(8,128)(2,1)} %get-tuple-element.6), channel_id=1, source_target_pairs={{0,1},{1,2},{2,3},{3,4},{4,5},{5,6},{6,7},{7,8},{8,9},{9,10},{10,1... | collective-permute-start | bytes 3145736 | tf_op jit(solution)/shard_map/ppermute | solution.py:288
  36.0 56.2 %collective-permute-start.3 = (bf16[64,32,256]{2,1,0:T(8,128)(2,1)}, bf16[64,32,256]{2,1,0:T(8,128)(2,1)}, u32[]{:S(2)}, u32[]{:S(2)}) collective-permute-start(bf16[64,32,256]{2,1,0:T(8,128)(2,1)} %get-tuple-element.6), channel_id=1, source_target_pairs={{1,0},{2,1},{3,2},{4,3},{5,4},{6,5},{7,6},{8,7},{9,8},{10,9},{11,1... | collective-permute-start | bytes 3145736 | tf_op jit(solution)/shard_map/ppermute | solution.py:289
  64.9 53.8 %collective-permute-start.26 = (bf16[2048,512]{1,0:T(8,128)(2,1)}, bf16[2048,512]{1,0:T(8,128)(2,1)}, u32[]{:S(2)}, u32[]{:S(2)}) collective-permute-start(bf16[2048,512]{1,0:T(8,128)(2,1)} %convolution_convert_fusion.1), channel_id=1, source_target_pairs={{0,64},{64,0},{1,65},{65,1},{2,66},{66,2},{3,67},{67,3},{4,68},{68... | collective-permute-start | bytes 6291464 | tf_op jit(solution)/shard_map/ppermute | solution.py:309
  65.6 7.1 %collective-permute-start.4 = (bf16[64,512]{1,0:T(8,128)(2,1)S(1)}, bf16[64,512]{1,0:T(8,128)(2,1)S(1)}, u32[]{:S(2)}, u32[]{:S(2)}) collective-permute-start(bf16[64,512]{1,0:T(8,128)(2,1)S(1)} %get-tuple-element.9), channel_id=1, source_target_pairs={{0,1},{1,2},{2,3},{3,0},{4,5},{5,6},{6,7},{7,4},{8,9},{9,10},{10,1... | collective-permute-start | bytes 196616 | tf_op jit(solution)/shard_map/ppermute | solution.py:261
  65.6 7.1 %collective-permute-start.5 = (bf16[64,512]{1,0:T(8,128)(2,1)S(1)}, bf16[64,512]{1,0:T(8,128)(2,1)S(1)}, u32[]{:S(2)}, u32[]{:S(2)}) collective-permute-start(bf16[64,512]{1,0:T(8,128)(2,1)S(1)} %get-tuple-element.9), channel_id=1, source_target_pairs={{0,2},{1,3},{2,0},{3,1},{4,6},{5,7},{6,4},{7,5},{8,10},{9,11},{10,... | collective-permute-start | bytes 196616 | tf_op jit(solution)/shard_map/ppermute | solution.py:261
  72.7 4.3 %collective-permute-start.6 = (bf16[64,512]{1,0:T(8,128)(2,1)S(1)}, bf16[64,512]{1,0:T(8,128)(2,1)S(1)}, u32[]{:S(2)}, u32[]{:S(2)}) collective-permute-start(bf16[64,512]{1,0:T(8,128)(2,1)S(1)} %get-tuple-element.9), channel_id=1, source_target_pairs={{0,3},{1,0},{2,1},{3,2},{4,7},{5,4},{6,5},{7,6},{8,11},{9,8},{10,9... | collective-permute-start | bytes 196616 | tf_op jit(solution)/shard_map/ppermute | solution.py:261
  77.0 13.7 %collective-permute-start.7 = (bf16[256,512]{1,0:T(8,128)(2,1)S(1)}, bf16[256,512]{1,0:T(8,128)(2,1)S(1)}, u32[]{:S(2)}, u32[]{:S(2)}) collective-permute-start(bf16[256,512]{1,0:T(8,128)(2,1)S(1)} %pad_maximum_fusion), channel_id=1, source_target_pairs={{0,4},{1,5},{2,6},{3,7},{4,8},{5,9},{6,10},{7,11},{8,12},{9,13},{1... | collective-permute-start | bytes 786440 | tf_op jit(solution)/shard_map/ppermute | solution.py:261
  77.1 14.3 %collective-permute-start.8 = (bf16[256,512]{1,0:T(8,128)(2,1)S(1)}, bf16[256,512]{1,0:T(8,128)(2,1)S(1)}, u32[]{:S(2)}, u32[]{:S(2)}) collective-permute-start(bf16[256,512]{1,0:T(8,128)(2,1)S(1)} %pad_maximum_fusion), channel_id=1, source_target_pairs={{0,8},{1,9},{2,10},{3,11},{4,12},{5,13},{6,14},{7,15},{8,0},{9,1},... | collective-permute-start | bytes 786440 | tf_op jit(solution)/shard_map/ppermute | solution.py:261
  90.7 24.1 %collective-permute-start.9 = (bf16[256,512]{1,0:T(8,128)(2,1)S(1)}, bf16[256,512]{1,0:T(8,128)(2,1)S(1)}, u32[]{:S(2)}, u32[]{:S(2)}) collective-permute-start(bf16[256,512]{1,0:T(8,128)(2,1)S(1)} %pad_maximum_fusion), channel_id=1, source_target_pairs={{0,12},{1,13},{2,14},{3,15},{4,0},{5,1},{6,2},{7,3},{8,4},{9,5},{1... | collective-permute-start | bytes 786440 | tf_op jit(solution)/shard_map/ppermute | solution.py:261
  114.8 70.5 %collective-permute-start.27 = (bf16[2048,512]{1,0:T(8,128)(2,1)}, bf16[2048,512]{1,0:T(8,128)(2,1)}, u32[]{:S(2)}, u32[]{:S(2)}) collective-permute-start(bf16[2048,512]{1,0:T(8,128)(2,1)} %convolution_convert_fusion), channel_id=1, source_target_pairs={{0,64},{64,0},{1,65},{65,1},{2,66},{66,2},{3,67},{67,3},{4,68},{68... | collective-permute-start | bytes 6291464 | tf_op jit(solution)/shard_map/ppermute | solution.py:309
  115.5 68.6 %collective-permute-start.10 = (bf16[1024,512]{1,0:T(8,128)(2,1)}, bf16[1024,512]{1,0:T(8,128)(2,1)}, u32[]{:S(2)}, u32[]{:S(2)}) collective-permute-start(bf16[1024,512]{1,0:T(8,128)(2,1)} %constant_dynamic-update-slice_fusion.rest_0_), channel_id=1, source_target_pairs={{0,16},{1,17},{2,18},{3,19},{4,20},{5,21},{6,22},{7,23},{8,24},{9,... | collective-permute-start | bytes 3145736 | tf_op jit(solution)/shard_map/ppermute | solution.py:261
  115.5 68.6 %collective-permute-start.11 = (bf16[1024,512]{1,0:T(8,128)(2,1)}, bf16[1024,512]{1,0:T(8,128)(2,1)}, u32[]{:S(2)}, u32[]{:S(2)}) collective-permute-start(bf16[1024,512]{1,0:T(8,128)(2,1)} %constant_dynamic-update-slice_fusion.rest_0_), channel_id=1, source_target_pairs={{0,32},{1,33},{2,34},{3,35},{4,36},{5,37},{6,38},{7,39},{8,40},{9,... | collective-permute-start | bytes 3145736 | tf_op jit(solution)/shard_map/ppermute | solution.py:261
  116.5 68.1 %collective-permute-start.12 = (bf16[1024,512]{1,0:T(8,128)(2,1)}, bf16[1024,512]{1,0:T(8,128)(2,1)}, u32[]{:S(2)}, u32[]{:S(2)}) collective-permute-start(bf16[1024,512]{1,0:T(8,128)(2,1)} %constant_dynamic-update-slice_fusion.rest_0_), channel_id=1, source_target_pairs={{0,48},{1,49},{2,50},{3,51},{4,52},{5,53},{6,54},{7,55},{8,56},{9,... | collective-permute-start | bytes 3145736 | tf_op jit(solution)/shard_map/ppermute | solution.py:261
  124.2 61.1 %copy-start.3 = (bf16[1024,512]{1,0:T(8,128)(2,1)S(1)}, bf16[1024,512]{1,0:T(8,128)(2,1)}, u32[]{:S(2)}) copy-start(bf16[1024,512]{1,0:T(8,128)(2,1)} %get-tuple-element.11.mine) | copy-start | bytes 3145732
  124.2 67.7 %all-to-all-start = ((bf16[64,32,512]{2,1,0:T(8,128)(2,1)}), bf16[64,32,512]{2,1,0:T(8,128)(2,1)S(1)}, u32[]{:S(2)}, u32[]{:S(2)}) async-start(bf16[64,32,512]{2,1,0:T(8,128)(2,1)} %bitcast.43), calls=%async_computation | async-start | bytes 4194304 | tf_op jit(solution)/shard_map/all_to_all | solution.py:312
  131.9 66.2 %collective-permute-start.13 = (bf16[1024,512]{1,0:T(8,128)(2,1)}, bf16[1024,512]{1,0:T(8,128)(2,1)}, u32[]{:S(2)}, u32[]{:S(2)}) collective-permute-start(bf16[1024,512]{1,0:T(8,128)(2,1)} %constant_dynamic-update-slice_fusion.rest_0_), channel_id=1, source_target_pairs={{0,64},{64,0},{1,65},{65,1},{2,66},{66,2},{3,67},{67,3},{4,68},{68... | collective-permute-start | bytes 3145736 | tf_op jit(solution)/shard_map/ppermute | solution.py:280
  184.1 14.0 %collective-permute-start.14 = (bf16[1024,512]{1,0:T(8,128)(2,1)}, bf16[1024,512]{1,0:T(8,128)(2,1)}, u32[]{:S(2)}, u32[]{:S(2)}) collective-permute-start(bf16[1024,512]{1,0:T(8,128)(2,1)} %collective-permute-done.10.rest_1_), channel_id=1, source_target_pairs={{0,64},{64,0},{1,65},{65,1},{2,66},{66,2},{3,67},{67,3},{4,68},{68... | collective-permute-start | bytes 3145736 | tf_op jit(solution)/shard_map/ppermute | solution.py:280
  184.1 14.0 %collective-permute-start.15 = (bf16[1024,512]{1,0:T(8,128)(2,1)}, bf16[1024,512]{1,0:T(8,128)(2,1)}, u32[]{:S(2)}, u32[]{:S(2)}) collective-permute-start(bf16[1024,512]{1,0:T(8,128)(2,1)} %collective-permute-done.11.rest_2_), channel_id=1, source_target_pairs={{0,64},{64,0},{1,65},{65,1},{2,66},{66,2},{3,67},{67,3},{4,68},{68... | collective-permute-start | bytes 3145736 | tf_op jit(solution)/shard_map/ppermute | solution.py:280
  184.7 13.5 %collective-permute-start.16 = (bf16[1024,512]{1,0:T(8,128)(2,1)}, bf16[1024,512]{1,0:T(8,128)(2,1)}, u32[]{:S(2)}, u32[]{:S(2)}) collective-permute-start(bf16[1024,512]{1,0:T(8,128)(2,1)} %collective-permute-done.12.rest_3_), channel_id=1, source_target_pairs={{0,64},{64,0},{1,65},{65,1},{2,66},{66,2},{3,67},{67,3},{4,68},{68... | collective-permute-start | bytes 3145736 | tf_op jit(solution)/shard_map/ppermute | solution.py:280
  191.9 73.2 %all-to-all-start.1 = ((bf16[64,32,512]{2,1,0:T(8,128)(2,1)}), bf16[64,32,512]{2,1,0:T(8,128)(2,1)}, u32[]{:S(2)}, u32[]{:S(2)}) async-start(bf16[64,32,512]{2,1,0:T(8,128)(2,1)} %bitcast.44), calls=%async_computation.1 | async-start | bytes 4194304 | tf_op jit(solution)/shard_map/all_to_all | solution.py:312
  238.2 3.9 %collective-permute-start.19 = (f32[1,256]{1,0:T(1,128)}, f32[1,256]{1,0:T(1,128)S(1)}, u32[]{:S(2)}, u32[]{:S(2)}) collective-permute-start(f32[1,256]{1,0:T(1,128)} %energy_share.1), channel_id=1, source_target_pairs={{0,3},{1,0},{2,1},{3,2},{4,7},{5,4},{6,5},{7,6},{8,11},{9,8},{10,9... | collective-permute-start | bytes 3080 | tf_op jit(solution)/shard_map/ppermute | solution.py:261
  240.3 5.3 %collective-permute-start.18 = (f32[1,256]{1,0:T(1,128)}, f32[1,256]{1,0:T(1,128)S(1)}, u32[]{:S(2)}, u32[]{:S(2)}) collective-permute-start(f32[1,256]{1,0:T(1,128)} %energy_share.1), channel_id=1, source_target_pairs={{0,2},{1,3},{2,0},{3,1},{4,6},{5,7},{6,4},{7,5},{8,10},{9,11},{10,... | collective-permute-start | bytes 3080 | tf_op jit(solution)/shard_map/ppermute | solution.py:261
  241.9 5.0 %collective-permute-start.17 = (f32[1,256]{1,0:T(1,128)}, f32[1,256]{1,0:T(1,128)S(1)}, u32[]{:S(2)}, u32[]{:S(2)}) collective-permute-start(f32[1,256]{1,0:T(1,128)} %energy_share.1), channel_id=1, source_target_pairs={{0,1},{1,2},{2,3},{3,0},{4,5},{5,6},{6,7},{7,4},{8,9},{9,10},{10,1... | collective-permute-start | bytes 3080 | tf_op jit(solution)/shard_map/ppermute | solution.py:261
  247.6 3.7 %collective-permute-start.22 = (f32[1,256]{1,0:T(1,128)S(1)}, f32[1,256]{1,0:T(1,128)S(1)}, u32[]{:S(2)}, u32[]{:S(2)}) collective-permute-start(f32[1,256]{1,0:T(1,128)S(1)} %fusion.9), channel_id=1, source_target_pairs={{0,12},{1,13},{2,14},{3,15},{4,0},{5,1},{6,2},{7,3},{8,4},{9,5},{1... | collective-permute-start | bytes 3080 | tf_op jit(solution)/shard_map/ppermute | solution.py:261
  249.6 5.1 %collective-permute-start.21 = (f32[1,256]{1,0:T(1,128)S(1)}, f32[1,256]{1,0:T(1,128)S(1)}, u32[]{:S(2)}, u32[]{:S(2)}) collective-permute-start(f32[1,256]{1,0:T(1,128)S(1)} %fusion.9), channel_id=1, source_target_pairs={{0,8},{1,9},{2,10},{3,11},{4,12},{5,13},{6,14},{7,15},{8,0},{9,1},... | collective-permute-start | bytes 3080 | tf_op jit(solution)/shard_map/ppermute | solution.py:261
  250.4 4.8 %collective-permute-start.20 = (f32[1,256]{1,0:T(1,128)S(1)}, f32[1,256]{1,0:T(1,128)S(1)}, u32[]{:S(2)}, u32[]{:S(2)}) collective-permute-start(f32[1,256]{1,0:T(1,128)S(1)} %fusion.9), channel_id=1, source_target_pairs={{0,4},{1,5},{2,6},{3,7},{4,8},{5,9},{6,10},{7,11},{8,12},{9,13},{1... | collective-permute-start | bytes 3080 | tf_op jit(solution)/shard_map/ppermute | solution.py:261
  255.3 5.1 %collective-permute-start.25 = (f32[1,256]{1,0:T(1,128)S(1)}, f32[1,256]{1,0:T(1,128)S(1)}, u32[]{:S(2)}, u32[]{:S(2)}) collective-permute-start(f32[1,256]{1,0:T(1,128)S(1)} %fusion.12), channel_id=1, source_target_pairs={{0,48},{1,49},{2,50},{3,51},{4,52},{5,53},{6,54},{7,55},{8,56},{9,... | collective-permute-start | bytes 3080 | tf_op jit(solution)/shard_map/ppermute | solution.py:261
  259.0 5.1 %collective-permute-start.24 = (f32[1,256]{1,0:T(1,128)S(1)}, f32[1,256]{1,0:T(1,128)S(1)}, u32[]{:S(2)}, u32[]{:S(2)}) collective-permute-start(f32[1,256]{1,0:T(1,128)S(1)} %fusion.12), channel_id=1, source_target_pairs={{0,32},{1,33},{2,34},{3,35},{4,36},{5,37},{6,38},{7,39},{8,40},{9,... | collective-permute-start | bytes 3080 | tf_op jit(solution)/shard_map/ppermute | solution.py:261
  259.4 4.8 %collective-permute-start.23 = (f32[1,256]{1,0:T(1,128)S(1)}, f32[1,256]{1,0:T(1,128)S(1)}, u32[]{:S(2)}, u32[]{:S(2)}) collective-permute-start(f32[1,256]{1,0:T(1,128)S(1)} %fusion.12), channel_id=1, source_target_pairs={{0,16},{1,17},{2,18},{3,19},{4,20},{5,21},{6,22},{7,23},{8,24},{9,... | collective-permute-start | bytes 3080 | tf_op jit(solution)/shard_map/ppermute | solution.py:261
  (8 other events, 69.1 us)

commit v6 on v5

--- a/solution.py
+++ b/solution.py
@@ -16,11 +16,10 @@
 EDGES = TILES * SLOTS
 FEAT = 1024
 ZERO_TILE = 3 * TILES
-CHUNK = 32
 ROWS = EDGES // 4
 SHEET = 1024
 GRAD_PITCH = ROWS + 8
-UNROLL = 16
+UNROLL = 8
 ENERGY_UNROLL = 4
 NT = (((1,), (1,)), ((), ()))
 
@@ -33,53 +32,37 @@
     return pltpu.roll(value, ORB, value.ndim - 1)
 
 
-def turn_lanes(strip):
-    lane = lax.broadcasted_iota(jnp.int32, strip[0].shape, 1)
-    low = lane < 64
-    even = lane % 64 < 32
-    half = [None] * 4
-    for r in range(2):
-        half[r] = jnp.where(low, strip[r], pltpu.roll(strip[r + 2], 64, 1))
-        half[r + 2] = jnp.where(low, pltpu.roll(strip[r], 64, 1), strip[r + 2])
-    turned = [None] * 4
-    for r in (0, 2):
-        turned[r] = jnp.where(even, half[r], pltpu.roll(half[r + 1], 32, 1))
-        turned[r + 1] = jnp.where(even, pltpu.roll(half[r], 96, 1), half[r + 1])
-    return turned
-
-
 def grad_blocks_kernel(
-    index, tiles, rows, total, prev, own, following, weighted, out, table, left, strips, sems, *, part, factor
+    index, tiles, rows, total, prev, own, following, weighted, out, table, left, strips, sems, *, factor
 ):
     step = pl.program_id(0)
 
     @pl.when(step == 0)
     def _():
-        mine = own.at[:, pl.ds(part * CHUNK, CHUNK), :]
         copies = [
             pltpu.make_async_copy(src, table.at[pl.ds(n * TILES, TILES)], sems.at[n])
-            for n, src in enumerate((prev, mine, following))
+            for n, src in enumerate((prev, own, following))
         ]
         copies.append(pltpu.make_async_copy(weighted, left, sems.at[3]))
         for copy in copies:
             copy.start()
-        table[ZERO_TILE] = jnp.zeros((CHUNK, BANDS), jnp.bfloat16)
+        table[ZERO_TILE] = jnp.zeros((ORB, BANDS), jnp.bfloat16)
 
         def clear(n, carry):
-            strips[pl.ds(pl.multiple_of(n * 128, 8), 128), :] = jnp.zeros((128, 128), jnp.float32)
+            strips[pl.ds(pl.multiple_of(n * 256, 8), 256), :] = jnp.zeros((256, 128), jnp.float32)
             return carry
 
-        lax.fori_loop(0, ORB * GRAD_PITCH // 128, clear, 0)
+        lax.fori_loop(0, 2 * ORB * GRAD_PITCH // 256, clear, 0)
         for copy in copies:
             copy.wait()
 
         def item_body(n, carry):
             at = [rows[n * UNROLL + u] for u in range(UNROLL)]
-            who = [tiles[n * UNROLL + u] for u in range(UNROLL)]
+            home = [tiles[n * UNROLL + u] for u in range(UNROLL)]
             which = [[index[row * 4 + p] for p in range(4)] for row in at]
             products = [
                 lax.dot_general(
-                    left[who[u]],
+                    left[home[u]],
                     jnp.concatenate([table[w] for w in which[u]], axis=0),
                     NT,
                     preferred_element_type=jnp.float32,
@@ -87,50 +70,57 @@
                 for u in range(UNROLL)
             ]
             for row, product in zip(at, products):
-                strips[pl.ds(row, ORB, stride=GRAD_PITCH), :] = product
+                for part in (0, 1):
+                    strips[pl.ds(part * GRAD_PITCH + row, ORB, stride=2 * GRAD_PITCH), :] = product[
+                        :, part * 128 : (part + 1) * 128
+                    ]
             return carry
 
         lax.fori_loop(0, (total[0] + UNROLL - 1) // UNROLL, item_body, 0)
 
-    quads = out.shape[1] // 128
-    group = 128
+    pairs = out.shape[1] // 128
+    group = 64
+    low = left_lanes((group, 128))
 
     def group_body(g, carry):
-        for quad in range(quads):
-            base = (step * quads + quad) * 4 * GRAD_PITCH + g * group
-            strip = [
-                strips[pl.ds(pl.multiple_of(base + r * GRAD_PITCH, 8), group), :] * factor
-                for r in range(4)
-            ]
-            turned = [t.reshape(group // 8, 1, 8, 128) for t in turn_lanes(strip)]
+        for pair in range(pairs):
+            base = (step * pairs + pair) * 4 * GRAD_PITCH + g * group
+            turned = []
+            for part in (0, 1):
+                spot = base + part * GRAD_PITCH
+                one = strips[pl.ds(pl.multiple_of(spot, 8), group), :] * factor
+                spot = spot + 2 * GRAD_PITCH
+                two = strips[pl.ds(pl.multiple_of(spot, 8), group), :] * factor
+                turned.append(jnp.where(low, one, swap(two)).reshape(group // 8, 1, 8, 128))
+                turned.append(jnp.where(low, swap(one), two).reshape(group // 8, 1, 8, 128))
             both = jnp.concatenate(turned, axis=1).reshape(group * 4, 128)
             spot = pl.ds(pl.multiple_of(g * (group * 4), 16), group * 4)
-            out[spot, quad * 128 : (quad + 1) * 128] = both.astype(jnp.bfloat16)
+            out[spot, pair * 128 : (pair + 1) * 128] = both.astype(jnp.bfloat16)
         return carry
 
     lax.fori_loop(0, ROWS // group, group_body, 0)
 
 
-def grad_blocks(plan, prev, own, following, weighted, part, factor):
+def grad_blocks(plan, prev, own, following, weighted, factor):
     block = 512
     return pl.pallas_call(
-        functools.partial(grad_blocks_kernel, part=part, factor=factor),
+        functools.partial(grad_blocks_kernel, factor=factor),
         grid_spec=pltpu.PrefetchScalarGridSpec(
             num_scalar_prefetch=4,
-            grid=(ORB * CHUNK // block,),
+            grid=(ORB * ORB // block,),
             in_specs=[pl.BlockSpec(memory_space=pltpu.MemorySpace.HBM)] * 4,
             out_specs=pl.BlockSpec((EDGES, block), lambda j, *_: (0, j)),
             scratch_shapes=[
-                pltpu.VMEM((ZERO_TILE + 1, CHUNK, BANDS), jnp.bfloat16),
+                pltpu.VMEM((ZERO_TILE + 1, ORB, BANDS), jnp.bfloat16),
                 pltpu.VMEM((TILES, ORB, BANDS), jnp.bfloat16),
-                pltpu.VMEM((ORB * GRAD_PITCH, 128), jnp.float32),
+                pltpu.VMEM((2 * ORB * GRAD_PITCH, 128), jnp.float32),
                 pltpu.SemaphoreType.DMA((4,)),
             ],
         ),
-        out_shape=jax.ShapeDtypeStruct((EDGES, ORB * CHUNK), jnp.bfloat16),
+        out_shape=jax.ShapeDtypeStruct((EDGES, ORB * ORB), jnp.bfloat16),
         compiler_params=pltpu.CompilerParams(vmem_limit_bytes=60 * 2**20),
         cost_estimate=pl.CostEstimate(
-            flops=8 * EDGES * ORB * CHUNK * BANDS, bytes_accessed=12 * 2**20, transcendentals=0
+            flops=8 * EDGES * ORB * ORB * BANDS, bytes_accessed=16 * 2**20, transcendentals=0
         ),
         name="grad_blocks",
     )(*plan, prev, own, following, weighted)
@@ -150,25 +140,21 @@
 
 
 def energy_kernel(
-    index, tiles, rows, total, who, prev0, prev1, own, following0, following1, mine, theirs, *rest, factor
+    index, tiles, rows, total, who, prev, own, following, mine, theirs, *rest, factor
 ):
     sheets, (out, table, strips, near, far, weights, sems) = rest[:8], rest[8:]
     low = left_lanes((ROWS, 128))
-    places = (
-        (prev0, table.at[pl.ds(0, TILES), pl.ds(0, CHUNK)]),
-        (prev1, table.at[pl.ds(0, TILES), pl.ds(CHUNK, CHUNK)]),
-        (own, table.at[pl.ds(TILES, TILES)]),
-        (following0, table.at[pl.ds(2 * TILES, TILES), pl.ds(0, CHUNK)]),
-        (following1, table.at[pl.ds(2 * TILES, TILES), pl.ds(CHUNK, CHUNK)]),
-    )
-    late = [pltpu.make_async_copy(src, dst, sems.at[n]) for n, (src, dst) in enumerate(places)]
+    late = [
+        pltpu.make_async_copy(src, table.at[pl.ds(n * TILES, TILES)], sems.at[n])
+        for n, src in enumerate((prev, own, following))
+    ]
     early = [
-        pltpu.make_async_copy(mine, near, sems.at[5]),
-        pltpu.make_async_copy(theirs, far, sems.at[6]),
+        pltpu.make_async_copy(mine, near, sems.at[3]),
+        pltpu.make_async_copy(theirs, far, sems.at[4]),
     ]
     for n, sheet in enumerate(sheets):
         spot = weights.at[n // 4, pl.ds(n % 4 * SHEET, SHEET)]
-        early.append(pltpu.make_async_copy(sheet, spot, sems.at[7 + n]))
+        early.append(pltpu.make_async_copy(sheet, spot, sems.at[5 + n]))
     for copy in early + late:
         copy.start()
     table[ZERO_TILE] = jnp.zeros((ORB, BANDS), jnp.bfloat16)
@@ -228,7 +214,7 @@
         grid_spec=pltpu.PrefetchScalarGridSpec(
             num_scalar_prefetch=5,
             grid=(1,),
-            in_specs=[pl.BlockSpec(memory_space=pltpu.MemorySpace.HBM)] * 15,
+            in_specs=[pl.BlockSpec(memory_space=pltpu.MemorySpace.HBM)] * 13,
             out_specs=pl.BlockSpec((1, BANDS), lambda j, *_: (0, 0)),
             scratch_shapes=[
                 pltpu.VMEM((ZERO_TILE + 1, ORB, BANDS), jnp.bfloat16),
@@ -236,7 +222,7 @@
                 pltpu.VMEM((EDGES, FEAT // 2), jnp.bfloat16),
                 pltpu.VMEM((EDGES, FEAT // 2), jnp.bfloat16),
                 pltpu.VMEM((2, 4 * SHEET, FEAT // 2), jnp.bfloat16),
-                pltpu.SemaphoreType.DMA((15,)),
+                pltpu.SemaphoreType.DMA((13,)),
             ],
         ),
         out_shape=jax.ShapeDtypeStruct((1, BANDS), jnp.float32),
@@ -245,7 +231,7 @@
             flops=2 * EDGES * ORB * ORB * (FEAT + BANDS * 4), bytes_accessed=16 * 2**20, transcendentals=0
         ),
         name="energy_share",
-    )(*plan, who, *prev, own, *following, mine, theirs, *sheets)
+    )(*plan, who, prev, own, following, mine, theirs, *sheets)
 
 
 def ring(axis, hop):
@@ -269,8 +255,8 @@
     own = psi.reshape(TILES, ORB, BANDS)
     up = [(i, (i + 1) % nspace) for i in range(nspace)]
     down = [(j, i) for i, j in up]
-    prev0 = lax.ppermute(own[:, :CHUNK], "space", up)
-    following0 = lax.ppermute(own[:, :CHUNK], "space", down)
+    prev = lax.ppermute(own, "space", up)
+    following = lax.ppermute(own, "space", down)
     half = FEAT // 2
     swapped = [(0, 1), (1, 0)]
     sheet = lax.dynamic_slice_in_dim(weights.T, core * half, half, 1)
@@ -284,11 +270,6 @@
         + (myself // 4 - back // 4) % 4 * 4
         + (myself - back) % 4
     ).astype(jnp.int32)
-    second, prev0, following0 = lax.optimization_barrier((own[:, CHUNK:], prev0, following0))
-    prev1 = lax.ppermute(second, "space", up)
-    following1 = lax.ppermute(second, "space", down)
-    prev, following = (prev0, prev1), (following0, following1)
-
     where = neighbors.reshape(TILES, SLOTS)
     placed = (where // TILES - myself + 1 + nspace) % nspace * TILES + where % TILES
     slot = lax.broadcasted_iota(jnp.int32, (TILES, SLOTS), 1)
@@ -302,15 +283,12 @@
     theirs = lax.dynamic_slice_in_dim(edges, (1 - core) * half, half, 1)
     mine = lax.dynamic_slice_in_dim(edges, core * half, half, 1)
     over_edges = (((0,), (0,)), ((), ()))
-    arrived = []
-    for part in (0, 1):
-        blocks = grad_blocks(plan, prev[part], own, following[part], weighted, part, factor)
-        send = lax.dot_general(blocks, theirs, over_edges, preferred_element_type=jnp.float32)
-        other = lax.ppermute(send.astype(jnp.bfloat16), "dp", swapped)
-        keep = lax.dot_general(blocks, mine, over_edges, preferred_element_type=jnp.float32)
-        summed = (keep + other.astype(jnp.float32)).astype(jnp.bfloat16)
-        parts = lax.all_to_all(summed, "space", 0, 0, tiled=True)
-        arrived.append(parts)
+    blocks = grad_blocks(plan, prev, own, following, weighted, factor)
+    send = lax.dot_general(blocks, theirs, over_edges, preferred_element_type=jnp.float32)
+    other = lax.ppermute(send.astype(jnp.bfloat16), "dp", swapped)
+    keep = lax.dot_general(blocks, mine, over_edges, preferred_element_type=jnp.float32)
+    summed = (keep + other.astype(jnp.float32)).astype(jnp.bfloat16)
+    parts = lax.all_to_all(summed, "space", 0, 0, tiled=True)
     partial = energy_share(plan, who, prev, own, following, mine, theirs, sheets, factor)
     energies = partial
     for axis, place in ((2, myself % 4), (1, myself // 4 % 4), (0, myself // 16)):
@@ -318,10 +296,8 @@
         energies = sum(
             lax.dynamic_slice_in_dim(pieces, (place - spot) % 4, 1, 0) for spot in range(4)
         )
-    shares = [
-        jnp.sum(parts.reshape(nspace, CHUNK, half).astype(jnp.float32), axis=0) for parts in arrived
-    ]
-    gradient = lax.all_gather(jnp.concatenate(shares, axis=0), "dp", axis=1, tiled=True)
+    share = jnp.sum(parts.reshape(nspace, ORB, half).astype(jnp.float32), axis=0)
+    gradient = lax.all_gather(share, "dp", axis=1, tiled=True)
     return (energies, gradient)
 
 

time: 271 us -> 274 us (1.011)
  waiting for transfers between devices: 94.4 us -> 137 us
  starting transfers between devices: 46.7 us -> 31.5 us
  local copies, waits for them, and re-layouts: 22.9 us -> 12.1 us
  matrix products: 24 us -> 14.8 us
  Pallas kernels: 71.1 us -> 63.9 us
    ppermute x4 -> x2, waiting for transfers between devices: 6.5 us -> 36.6 us  [the longest x1 29 us: step(): following = lax.ppermute(own, 'space', down)]
    ppermute x18, waiting for transfers between devices: 87.9 us -> 98.3 us  [spread(): lax.ppermute(value, 'space', ring(axis, hop))]
    ppermute x4 -> x2, starting transfers between devices: 16.3 us -> 8.87 us  [the longest x1 8.86 us: step(): following = lax.ppermute(own, 'space', down)]
    pallas_call x2 -> x1, Pallas kernels: 31.1 us -> 23.8 us  [grad_blocks(): pl.pallas_call(functools.partial(grad_blocks_kernel, factor=factor), grid...]
    all_to_all x2 -> x1, starting transfers between devices: 13.9 us -> 7.35 us  [step(): parts = lax.all_to_all(summed, 'space', 0, 0, tiled=True)]
    dot_general x2 -> x1, matrix products: 12 us -> 6.2 us  [step(): lax.dot_general(blocks, mine, over_edges, preferred_element_type=jnp.floa...]
    unnamed x28, local copies, waits for them, and re-layouts: 5.8 us -> 1.6 us
    dot_general x2 -> x1, matrix products: 12 us -> 8.57 us  [step(): lax.dot_general(blocks, theirs, over_edges, preferred_element_type=jnp.fl...]
  transfers between devices with their start and end apart: 30 -> 26, of which waited for: 12 -> 17; matrix products, arithmetic and copies ran while one was open for 18% -> 9% of each run, Pallas kernels for 26% -> 15%
where the time goes in v6:
time: 274 us; the launch traced here: 272 us
  waiting for transfers between devices  137 us (50%)
  Pallas kernels  63.9 us (23%)
  starting transfers between devices  31.5 us (11%)
  matrix products  14.8 us (5%)
  local copies, waits for them, and re-layouts  12.1 us (4%)
  other arithmetic  9.64 us (4%)
    ppermute x18, waiting for transfers between devices, spread(): lax.ppermute(value, 'space', ring(axis, hop))  98.3 us
    pallas_call x1, Pallas kernels, energy_share(): pl.pallas_call(functools.partial(energy_kernel, factor=factor), grid_spec...  40.1 us
    ppermute x1, waiting for transfers between devices, step(): following = lax.ppermute(own, 'space', down)  29 us
    pallas_call x1, Pallas kernels, grad_blocks(): pl.pallas_call(functools.partial(grad_blocks_kernel, factor=factor), grid...  23.8 us
    ppermute x18, starting transfers between devices, spread(): lax.ppermute(value, 'space', ring(axis, hop))  14.6 us
    ppermute x1, starting transfers between devices, step(): following = lax.ppermute(own, 'space', down)  8.86 us
    dot_general x1, matrix products, step(): lax.dot_general(blocks, theirs, over_edges, preferred_element_type=jnp.fl...  8.57 us
    reshape x3, local copies, waits for them, and re-layouts, step(): features.reshape(TILES // 2, 2, 4, 4, FEAT).transpose(0, 3, 1, 2, 4)  7.72 us
  transfers between devices with their start and end apart: 26, of which 17 were waited for; matrix products, arithmetic and copies ran while one was open for 9% of the time, Pallas kernels for 15%

profile of v6, /device:TPU:0, one launch (start us, length us, event | category | flops | bytes accessed | tf_op | source)
XLA Modules:
  0.0 272.1 jit_solution(10524245175124538809)
XLA Ops:
  0.6 8.9 %collective-permute-start.1 = (bf16[64,64,256]{2,1,0:T(8,128)(2,1)}, bf16[64,64,256]{2,1,0:T(8,128)(2,1)}, u32[]{:S(2)}, u32[]{:S(2)}) collective-permute-start(bf16[64,64,256]{2,1,0:T(8,128)(2,1)} %bitcast.35), channel_id=1, source_target_pairs={{1,0},{2,1},{3,2},{4,3},{5,4},{6,5},{7,6},{8,7},{9,8},{10,9},{11,1... | collective-permute-start | bytes 6291464 | tf_op jit(solution)/shard_map/ppermute | solution.py:259
  12.8 2.7 %reshape.98 = bf16[32,2,4,4,1024]{4,3,2,1,0:T(4,128)(2,1)S(1)} reshape(bf16[1,64,16,1024]{3,2,1,0:T(8,128)(2,1)} %param.6) | data formatting | bytes 4194304 | tf_op jit(solution)/shard_map/reshape | solution.py:280
  15.5 2.4 copy.17
  17.9 2.5 reshape.99
  22.6 1.3 subtract_select_fusion
  23.9 1.8 multiply_convert_fusion.weighted
  25.7 29.0 %collective-permute-done.1.following = bf16[64,64,256]{2,1,0:T(8,128)(2,1)} collective-permute-done((bf16[64,64,256]{2,1,0:T(8,128)(2,1)}, bf16[64,64,256]{2,1,0:T(8,128)(2,1)}, u32[]{:S(2)}, u32[]{:S(2)}) %collective-permute-start.1) | collective-permute-done | bytes 2097184 | tf_op jit(solution)/shard_map/ppermute | solution.py:259
  54.7 7.6 %collective-permute-done.prev = bf16[64,64,256]{2,1,0:T(8,128)(2,1)} collective-permute-done((bf16[64,64,256]{2,1,0:T(8,128)(2,1)}, bf16[64,64,256]{2,1,0:T(8,128)(2,1)}, u32[]{:S(2)}, u32[]{:S(2)}) %collective-permute-start) | collective-permute-done | bytes 2097184 | tf_op jit(solution)/shard_map/ppermute | solution.py:258
  62.3 23.8 %grad_blocks.1 = bf16[1024,4096]{1,0:T(8,128)(2,1)} custom-call(s32[1040]{0:T(1024)} %concatenate.19.index, s32[256]{0:T(256)} %get-tuple-element.7.tiles, s32[256]{0:T(256)} %get-tuple-element.6.rows, s32[1]{0:T(128)} %bitcast.4.total, bf16[64,64,256]{2,1,0:T(8,128)(2,1)} %collective-permute-done.prev, bf16[64,64,256]{2,1,0:T(8,128)(2,1)} %bitcast.37, ...), custom_call_target="tpu_custom_call" | custom-call | flops 8589934592 | bytes 16777216 | tf_op jit(solution)/shard_map/grad_blocks/pallas_call | solution.py:106
  86.1 8.6 %convolution_convert_fusion = bf16[4096,512]{1,0:T(8,128)(2,1)S(1)} fusion(bf16[1024,4096]{1,0:T(8,128)(2,1)} %grad_blocks.1, bf16[1024,512]{1,0:T(8,128)(2,1)S(1)} %get-tuple-element.4.theirs), kind=kOutput, calls=%fused_computation.2 | convolution fusion | flops 4297064448 | bytes 13631488 | tf_op jit(solution)/shard_map/dot_general | solution.py:287
  95.0 1.9 collective-permute-start.2
  96.9 2.9 %collective-permute-done.4 = bf16[64,512]{1,0:T(8,128)(2,1)S(1)} collective-permute-done((bf16[64,512]{1,0:T(8,128)(2,1)S(1)}, bf16[64,512]{1,0:T(8,128)(2,1)S(1)}, u32[]{:S(2)}, u32[]{:S(2)}) %collective-permute-start.4) | collective-permute-done | bytes 65568 | tf_op jit(solution)/shard_map/ppermute | solution.py:247
  101.1 1.3 collective-permute-done.2
  102.6 1.9 collective-permute-start.5
  104.5 13.3 %collective-permute-done.5 = bf16[256,512]{1,0:T(8,128)(2,1)S(1)} collective-permute-done((bf16[256,512]{1,0:T(8,128)(2,1)S(1)}, bf16[256,512]{1,0:T(8,128)(2,1)S(1)}, u32[]{:S(2)}, u32[]{:S(2)}) %collective-permute-start.5) | collective-permute-done | bytes 262176 | tf_op jit(solution)/shard_map/ppermute | solution.py:247
  118.1 1.9 collective-permute-start.8
  120.1 6.2 %add_convert_fusion = bf16[4096,512]{1,0:T(8,128)(2,1)} fusion(bf16[4096,512]{1,0:T(8,128)(2,1)S(1)} %collective-permute-done.24, bf16[1024,4096]{1,0:T(8,128)(2,1)S(1)} %copy-done.9, bf16[1024,512]{1,0:T(8,128)(2,1)S(1)} %copy-done.2), kind=kOutput, calls=%fused_computation.1 | convolution fusion | flops 4301258752 | bytes 17825792 | tf_op jit(solution)/shard_map/dot_general | solution.py:289
  126.3 7.3 %all-to-all-start = ((bf16[64,64,512]{2,1,0:T(8,128)(2,1)}), bf16[64,64,512]{2,1,0:T(8,128)(2,1)}, u32[]{:S(2)}, u32[]{:S(2)}) async-start(bf16[64,64,512]{2,1,0:T(8,128)(2,1)} %bitcast.34), calls=%async_computation | async-start | bytes 8388608 | tf_op jit(solution)/shard_map/all_to_all | solution.py:291
  133.7 31.4 %collective-permute-done.10.rest_3_ = bf16[1024,512]{1,0:T(8,128)(2,1)S(1)} collective-permute-done((bf16[1024,512]{1,0:T(8,128)(2,1)S(1)}, bf16[1024,512]{1,0:T(8,128)(2,1)S(1)}, u32[]{:S(2)}, u32[]{:S(2)}) %collective-permute-start.10) | collective-permute-done | bytes 1048608 | tf_op jit(solution)/shard_map/ppermute | solution.py:247
  165.7 35.4 %collective-permute-done.8.rest_1_ = bf16[1024,512]{1,0:T(8,128)(2,1)} collective-permute-done((bf16[1024,512]{1,0:T(8,128)(2,1)S(1)}, bf16[1024,512]{1,0:T(8,128)(2,1)}, u32[]{:S(2)}, u32[]{:S(2)}) %collective-permute-start.8) | collective-permute-done | bytes 1048608 | tf_op jit(solution)/shard_map/ppermute | solution.py:247
  201.6 2.5 collective-permute-done.12.rest_5_
  204.1 40.1 %energy_share.1 = f32[1,256]{1,0:T(1,128)} custom-call(s32[1040]{0:T(1024)} %concatenate.19.index, s32[256]{0:T(256)} %get-tuple-element.7.tiles, s32[256]{0:T(256)} %get-tuple-element.6.rows, s32[1]{0:T(128)} %bitcast.4.total, s32[64]{0:T(128)} %fusion.17.who, bf16[64,64,256]{2,1,0:T(8,128)(2,1)} %collective-permute-done.prev, ...), custom_call_target="tpu_custom_call" | custom-call | flops 17179869184 | bytes 16777216 | tf_op jit(solution)/shard_map/energy_share/pallas_call | solution.py:212
  244.3 1.4 collective-permute-start.16
  246.3 1.6 collective-permute-done.17
  247.9 1.6 collective-permute-done.16
  251.6 1.9 collective-permute-start.18
  253.5 1.5 collective-permute-done.20
  255.0 1.6 collective-permute-done.19
  257.7 3.2 %collective-permute-start.23 = (f32[1,256]{1,0:T(1,128)S(1)}, f32[1,256]{1,0:T(1,128)S(1)}, u32[]{:S(2)}, u32[]{:S(2)}) collective-permute-start(f32[1,256]{1,0:T(1,128)S(1)} %fusion.12), channel_id=1, source_target_pairs={{0,48},{1,49},{2,50},{3,51},{4,52},{5,53},{6,54},{7,55},{8,56},{9,... | collective-permute-start | bytes 3080 | tf_op jit(solution)/shard_map/ppermute | solution.py:247
  262.2 3.8 %collective-permute-done.22 = f32[1,256]{1,0:T(1,128)S(1)} collective-permute-done((f32[1,256]{1,0:T(1,128)S(1)}, f32[1,256]{1,0:T(1,128)S(1)}, u32[]{:S(2)}, u32[]{:S(2)}) %collective-permute-start.22) | collective-permute-done | bytes 1056 | tf_op jit(solution)/shard_map/ppermute | solution.py:247
  266.6 2.8 %convert_reduce_fusion = f32[64,512]{1,0:T(8,128)S(1)} fusion(bf16[64,64,512]{2,1,0:T(8,128)(2,1)} %all-to-all-done), kind=kLoop, calls=%fused_computation | loop fusion | flops 4161536 | bytes 4325376 | tf_op jit(solution)/shard_map/reduce_sum | solution.py:299
  269.4 2.0 all_gather.3
  (82 shorter events, 14.7 us)
Async XLA Ops:
  0.6 54.1 %collective-permute-start.1 = (bf16[64,64,256]{2,1,0:T(8,128)(2,1)}, bf16[64,64,256]{2,1,0:T(8,128)(2,1)}, u32[]{:S(2)}, u32[]{:S(2)}) collective-permute-start(bf16[64,64,256]{2,1,0:T(8,128)(2,1)} %bitcast.35), channel_id=1, source_target_pairs={{1,0},{2,1},{3,2},{4,3},{5,4},{6,5},{7,6},{8,7},{9,8},{10,9},{11,1... | collective-permute-start | bytes 6291464 | tf_op jit(solution)/shard_map/ppermute | solution.py:259
  9.5 52.8 %collective-permute-start = (bf16[64,64,256]{2,1,0:T(8,128)(2,1)}, bf16[64,64,256]{2,1,0:T(8,128)(2,1)}, u32[]{:S(2)}, u32[]{:S(2)}) collective-permute-start(bf16[64,64,256]{2,1,0:T(8,128)(2,1)} %bitcast.36), channel_id=1, source_target_pairs={{0,1},{1,2},{2,3},{3,4},{4,5},{5,6},{6,7},{7,8},{8,9},{9,10},{10,1... | collective-permute-start | bytes 6291464 | tf_op jit(solution)/shard_map/ppermute | solution.py:258
  22.6 63.5 %copy-start.1 = (bf16[1024,512]{1,0:T(8,128)(2,1)}, bf16[1024,512]{1,0:T(8,128)(2,1)S(1)}, u32[]{:S(2)}) copy-start(bf16[1024,512]{1,0:T(8,128)(2,1)S(1)} %get-tuple-element.4.theirs) | copy-start | bytes 3145732
  86.1 34.0 %copy-start.2 = (bf16[1024,512]{1,0:T(8,128)(2,1)S(1)}, bf16[1024,512]{1,0:T(8,128)(2,1)}, u32[]{:S(2)}) copy-start(bf16[1024,512]{1,0:T(8,128)(2,1)} %get-tuple-element.5.mine) | copy-start | bytes 3145732
  86.1 33.9 %copy-start.9 = (bf16[1024,4096]{1,0:T(8,128)(2,1)S(1)}, bf16[1024,4096]{1,0:T(8,128)(2,1)}, u32[]{:S(2)}) copy-start(bf16[1024,4096]{1,0:T(8,128)(2,1)} %grad_blocks.1) | copy-start | bytes 25165828
  94.7 25.3 %collective-permute-start.24 = (bf16[4096,512]{1,0:T(8,128)(2,1)S(1)}, bf16[4096,512]{1,0:T(8,128)(2,1)S(1)}, u32[]{:S(2)}, u32[]{:S(2)}) collective-permute-start(bf16[4096,512]{1,0:T(8,128)(2,1)S(1)} %convolution_convert_fusion), channel_id=1, source_target_pairs={{0,64},{64,0},{1,65},{65,1},{2,66},{66,2},{3,67},{67,3},{4,68},{68... | collective-permute-start | bytes 12582920 | tf_op jit(solution)/shard_map/ppermute | solution.py:288
  94.8 5.0 %collective-permute-start.4 = (bf16[64,512]{1,0:T(8,128)(2,1)S(1)}, bf16[64,512]{1,0:T(8,128)(2,1)S(1)}, u32[]{:S(2)}, u32[]{:S(2)}) collective-permute-start(bf16[64,512]{1,0:T(8,128)(2,1)S(1)} %get-tuple-element.3), channel_id=1, source_target_pairs={{0,3},{1,0},{2,1},{3,2},{4,7},{5,4},{6,5},{7,6},{8,11},{9,8},{10,9... | collective-permute-start | bytes 196616 | tf_op jit(solution)/shard_map/ppermute | solution.py:247
  94.9 6.1 %collective-permute-start.3 = (bf16[64,512]{1,0:T(8,128)(2,1)S(1)}, bf16[64,512]{1,0:T(8,128)(2,1)S(1)}, u32[]{:S(2)}, u32[]{:S(2)}) collective-permute-start(bf16[64,512]{1,0:T(8,128)(2,1)S(1)} %get-tuple-element.3), channel_id=1, source_target_pairs={{0,2},{1,3},{2,0},{3,1},{4,6},{5,7},{6,4},{7,5},{8,10},{9,11},{10,... | collective-permute-start | bytes 196616 | tf_op jit(solution)/shard_map/ppermute | solution.py:247
  95.0 7.4 %collective-permute-start.2 = (bf16[64,512]{1,0:T(8,128)(2,1)S(1)}, bf16[64,512]{1,0:T(8,128)(2,1)S(1)}, u32[]{:S(2)}, u32[]{:S(2)}) collective-permute-start(bf16[64,512]{1,0:T(8,128)(2,1)S(1)} %get-tuple-element.3), channel_id=1, source_target_pairs={{0,1},{1,2},{2,3},{3,0},{4,5},{5,6},{6,7},{7,4},{8,9},{9,10},{10,1... | collective-permute-start | bytes 196616 | tf_op jit(solution)/shard_map/ppermute | solution.py:247
  102.4 15.5 %collective-permute-start.7 = (bf16[256,512]{1,0:T(8,128)(2,1)S(1)}, bf16[256,512]{1,0:T(8,128)(2,1)S(1)}, u32[]{:S(2)}, u32[]{:S(2)}) collective-permute-start(bf16[256,512]{1,0:T(8,128)(2,1)S(1)} %pad_maximum_fusion), channel_id=1, source_target_pairs={{0,12},{1,13},{2,14},{3,15},{4,0},{5,1},{6,2},{7,3},{8,4},{9,5},{1... | collective-permute-start | bytes 786440 | tf_op jit(solution)/shard_map/ppermute | solution.py:247
  102.5 15.4 %collective-permute-start.6 = (bf16[256,512]{1,0:T(8,128)(2,1)S(1)}, bf16[256,512]{1,0:T(8,128)(2,1)S(1)}, u32[]{:S(2)}, u32[]{:S(2)}) collective-permute-start(bf16[256,512]{1,0:T(8,128)(2,1)S(1)} %pad_maximum_fusion), channel_id=1, source_target_pairs={{0,8},{1,9},{2,10},{3,11},{4,12},{5,13},{6,14},{7,15},{8,0},{9,1},... | collective-permute-start | bytes 786440 | tf_op jit(solution)/shard_map/ppermute | solution.py:247
  102.6 15.3 %collective-permute-start.5 = (bf16[256,512]{1,0:T(8,128)(2,1)S(1)}, bf16[256,512]{1,0:T(8,128)(2,1)S(1)}, u32[]{:S(2)}, u32[]{:S(2)}) collective-permute-start(bf16[256,512]{1,0:T(8,128)(2,1)S(1)} %pad_maximum_fusion), channel_id=1, source_target_pairs={{0,4},{1,5},{2,6},{3,7},{4,8},{5,9},{6,10},{7,11},{8,12},{9,13},{1... | collective-permute-start | bytes 786440 | tf_op jit(solution)/shard_map/ppermute | solution.py:247
  118.0 15.7 %copy-start.4 = (bf16[1024,512]{1,0:T(8,128)(2,1)}, bf16[1024,512]{1,0:T(8,128)(2,1)S(1)}, u32[]{:S(2)}) copy-start(bf16[1024,512]{1,0:T(8,128)(2,1)S(1)} %constant_dynamic-update-slice_fusion.rest_0_) | copy-start | bytes 3145732
  118.0 47.2 %collective-permute-start.10 = (bf16[1024,512]{1,0:T(8,128)(2,1)S(1)}, bf16[1024,512]{1,0:T(8,128)(2,1)S(1)}, u32[]{:S(2)}, u32[]{:S(2)}) collective-permute-start(bf16[1024,512]{1,0:T(8,128)(2,1)S(1)} %constant_dynamic-update-slice_fusion.rest_0_), channel_id=1, source_target_pairs={{0,48},{1,49},{2,50},{3,51},{4,52},{5,53},{6,54},{7,55},{8,56},{9,... | collective-permute-start | bytes 3145736 | tf_op jit(solution)/shard_map/ppermute | solution.py:247
  118.0 47.1 %collective-permute-start.9 = (bf16[1024,512]{1,0:T(8,128)(2,1)S(1)}, bf16[1024,512]{1,0:T(8,128)(2,1)S(1)}, u32[]{:S(2)}, u32[]{:S(2)}) collective-permute-start(bf16[1024,512]{1,0:T(8,128)(2,1)S(1)} %constant_dynamic-update-slice_fusion.rest_0_), channel_id=1, source_target_pairs={{0,32},{1,33},{2,34},{3,35},{4,36},{5,37},{6,38},{7,39},{8,40},{9,... | collective-permute-start | bytes 3145736 | tf_op jit(solution)/shard_map/ppermute | solution.py:247
  118.1 82.9 %collective-permute-start.8 = (bf16[1024,512]{1,0:T(8,128)(2,1)S(1)}, bf16[1024,512]{1,0:T(8,128)(2,1)}, u32[]{:S(2)}, u32[]{:S(2)}) collective-permute-start(bf16[1024,512]{1,0:T(8,128)(2,1)S(1)} %constant_dynamic-update-slice_fusion.rest_0_), channel_id=1, source_target_pairs={{0,16},{1,17},{2,18},{3,19},{4,20},{5,21},{6,22},{7,23},{8,24},{9,... | collective-permute-start | bytes 3145736 | tf_op jit(solution)/shard_map/ppermute | solution.py:247
  126.3 140.3 %all-to-all-start = ((bf16[64,64,512]{2,1,0:T(8,128)(2,1)}), bf16[64,64,512]{2,1,0:T(8,128)(2,1)}, u32[]{:S(2)}, u32[]{:S(2)}) async-start(bf16[64,64,512]{2,1,0:T(8,128)(2,1)} %bitcast.34), calls=%async_computation | async-start | bytes 8388608 | tf_op jit(solution)/shard_map/all_to_all | solution.py:291
  133.6 68.0 %collective-permute-start.11 = (bf16[1024,512]{1,0:T(8,128)(2,1)S(1)}, bf16[1024,512]{1,0:T(8,128)(2,1)}, u32[]{:S(2)}, u32[]{:S(2)}) collective-permute-start(bf16[1024,512]{1,0:T(8,128)(2,1)S(1)} %constant_dynamic-update-slice_fusion.rest_0_), channel_id=1, source_target_pairs={{0,64},{64,0},{1,65},{65,1},{2,66},{66,2},{3,67},{67,3},{4,68},{68... | collective-permute-start | bytes 3145736 | tf_op jit(solution)/shard_map/ppermute | solution.py:266
  165.2 38.9 %copy-start.7 = (bf16[1024,512]{1,0:T(8,128)(2,1)}, bf16[1024,512]{1,0:T(8,128)(2,1)S(1)}, u32[]{:S(2)}) copy-start(bf16[1024,512]{1,0:T(8,128)(2,1)S(1)} %collective-permute-done.10.rest_3_) | copy-start | bytes 3145732
  165.2 36.5 %collective-permute-start.14 = (bf16[1024,512]{1,0:T(8,128)(2,1)S(1)}, bf16[1024,512]{1,0:T(8,128)(2,1)}, u32[]{:S(2)}, u32[]{:S(2)}) collective-permute-start(bf16[1024,512]{1,0:T(8,128)(2,1)S(1)} %collective-permute-done.10.rest_3_), channel_id=1, source_target_pairs={{0,64},{64,0},{1,65},{65,1},{2,66},{66,2},{3,67},{67,3},{4,68},{68... | collective-permute-start | bytes 3145736 | tf_op jit(solution)/shard_map/ppermute | solution.py:266
  165.2 38.9 %copy-start.8 = (bf16[1024,512]{1,0:T(8,128)(2,1)}, bf16[1024,512]{1,0:T(8,128)(2,1)S(1)}, u32[]{:S(2)}) copy-start(bf16[1024,512]{1,0:T(8,128)(2,1)S(1)} %collective-permute-done.9.rest_2_) | copy-start | bytes 3145732
  165.2 36.4 %collective-permute-start.13 = (bf16[1024,512]{1,0:T(8,128)(2,1)S(1)}, bf16[1024,512]{1,0:T(8,128)(2,1)}, u32[]{:S(2)}, u32[]{:S(2)}) collective-permute-start(bf16[1024,512]{1,0:T(8,128)(2,1)S(1)} %collective-permute-done.9.rest_2_), channel_id=1, source_target_pairs={{0,64},{64,0},{1,65},{65,1},{2,66},{66,2},{3,67},{67,3},{4,68},{68... | collective-permute-start | bytes 3145736 | tf_op jit(solution)/shard_map/ppermute | solution.py:266
  201.1 3.0 %collective-permute-start.12 = (bf16[1024,512]{1,0:T(8,128)(2,1)}, bf16[1024,512]{1,0:T(8,128)(2,1)}, u32[]{:S(2)}, u32[]{:S(2)}) collective-permute-start(bf16[1024,512]{1,0:T(8,128)(2,1)} %collective-permute-done.8.rest_1_), channel_id=1, source_target_pairs={{0,64},{64,0},{1,65},{65,1},{2,66},{66,2},{3,67},{67,3},{4,68},{68... | collective-permute-start | bytes 3145736 | tf_op jit(solution)/shard_map/ppermute | solution.py:266
  244.2 3.7 %collective-permute-start.17 = (f32[1,256]{1,0:T(1,128)}, f32[1,256]{1,0:T(1,128)S(1)}, u32[]{:S(2)}, u32[]{:S(2)}) collective-permute-start(f32[1,256]{1,0:T(1,128)} %energy_share.1), channel_id=1, source_target_pairs={{0,3},{1,0},{2,1},{3,2},{4,7},{5,4},{6,5},{7,6},{8,11},{9,8},{10,9... | collective-permute-start | bytes 3080 | tf_op jit(solution)/shard_map/ppermute | solution.py:247
  244.3 5.2 %collective-permute-start.16 = (f32[1,256]{1,0:T(1,128)}, f32[1,256]{1,0:T(1,128)S(1)}, u32[]{:S(2)}, u32[]{:S(2)}) collective-permute-start(f32[1,256]{1,0:T(1,128)} %energy_share.1), channel_id=1, source_target_pairs={{0,2},{1,3},{2,0},{3,1},{4,6},{5,7},{6,4},{7,5},{8,10},{9,11},{10,... | collective-permute-start | bytes 3080 | tf_op jit(solution)/shard_map/ppermute | solution.py:247
  245.8 4.9 %collective-permute-start.15 = (f32[1,256]{1,0:T(1,128)}, f32[1,256]{1,0:T(1,128)S(1)}, u32[]{:S(2)}, u32[]{:S(2)}) collective-permute-start(f32[1,256]{1,0:T(1,128)} %energy_share.1), channel_id=1, source_target_pairs={{0,1},{1,2},{2,3},{3,0},{4,5},{5,6},{6,7},{7,4},{8,9},{9,10},{10,1... | collective-permute-start | bytes 3080 | tf_op jit(solution)/shard_map/ppermute | solution.py:247
  251.4 3.6 %collective-permute-start.20 = (f32[1,256]{1,0:T(1,128)S(1)}, f32[1,256]{1,0:T(1,128)S(1)}, u32[]{:S(2)}, u32[]{:S(2)}) collective-permute-start(f32[1,256]{1,0:T(1,128)S(1)} %fusion.9), channel_id=1, source_target_pairs={{0,12},{1,13},{2,14},{3,15},{4,0},{5,1},{6,2},{7,3},{8,4},{9,5},{1... | collective-permute-start | bytes 3080 | tf_op jit(solution)/shard_map/ppermute | solution.py:247
  251.4 5.2 %collective-permute-start.19 = (f32[1,256]{1,0:T(1,128)S(1)}, f32[1,256]{1,0:T(1,128)S(1)}, u32[]{:S(2)}, u32[]{:S(2)}) collective-permute-start(f32[1,256]{1,0:T(1,128)S(1)} %fusion.9), channel_id=1, source_target_pairs={{0,8},{1,9},{2,10},{3,11},{4,12},{5,13},{6,14},{7,15},{8,0},{9,1},... | collective-permute-start | bytes 3080 | tf_op jit(solution)/shard_map/ppermute | solution.py:247
  251.6 6.1 %collective-permute-start.18 = (f32[1,256]{1,0:T(1,128)S(1)}, f32[1,256]{1,0:T(1,128)S(1)}, u32[]{:S(2)}, u32[]{:S(2)}) collective-permute-start(f32[1,256]{1,0:T(1,128)S(1)} %fusion.9), channel_id=1, source_target_pairs={{0,4},{1,5},{2,6},{3,7},{4,8},{5,9},{6,10},{7,11},{8,12},{9,13},{1... | collective-permute-start | bytes 3080 | tf_op jit(solution)/shard_map/ppermute | solution.py:247
  257.7 4.5 %collective-permute-start.23 = (f32[1,256]{1,0:T(1,128)S(1)}, f32[1,256]{1,0:T(1,128)S(1)}, u32[]{:S(2)}, u32[]{:S(2)}) collective-permute-start(f32[1,256]{1,0:T(1,128)S(1)} %fusion.12), channel_id=1, source_target_pairs={{0,48},{1,49},{2,50},{3,51},{4,52},{5,53},{6,54},{7,55},{8,56},{9,... | collective-permute-start | bytes 3080 | tf_op jit(solution)/shard_map/ppermute | solution.py:247
  260.9 5.1 %collective-permute-start.22 = (f32[1,256]{1,0:T(1,128)S(1)}, f32[1,256]{1,0:T(1,128)S(1)}, u32[]{:S(2)}, u32[]{:S(2)}) collective-permute-start(f32[1,256]{1,0:T(1,128)S(1)} %fusion.12), channel_id=1, source_target_pairs={{0,32},{1,33},{2,34},{3,35},{4,36},{5,37},{6,38},{7,39},{8,40},{9,... | collective-permute-start | bytes 3080 | tf_op jit(solution)/shard_map/ppermute | solution.py:247
  260.9 5.1 %collective-permute-start.21 = (f32[1,256]{1,0:T(1,128)S(1)}, f32[1,256]{1,0:T(1,128)S(1)}, u32[]{:S(2)}, u32[]{:S(2)}) collective-permute-start(f32[1,256]{1,0:T(1,128)S(1)} %fusion.12), channel_id=1, source_target_pairs={{0,16},{1,17},{2,18},{3,19},{4,20},{5,21},{6,22},{7,23},{8,24},{9,... | collective-permute-start | bytes 3080 | tf_op jit(solution)/shard_map/ppermute | solution.py:247
  (4 other events, 23.8 us)

commit v7 on v6

--- a/solution.py
+++ b/solution.py
@@ -7,7 +7,6 @@
 from jax.experimental import pallas as pl
 from jax.experimental.pallas import tpu as pltpu
 from jax.sharding import PartitionSpec as P
-
 
 ORB = 64
 BANDS = 256
@@ -17,10 +16,9 @@
 FEAT = 1024
 ZERO_TILE = 3 * TILES
 ROWS = EDGES // 4
-SHEET = 1024
 GRAD_PITCH = ROWS + 8
 UNROLL = 8
-ENERGY_UNROLL = 4
+ENERGY_UNROLL = 8
 NT = (((1,), (1,)), ((), ()))
 
 
@@ -140,9 +138,9 @@
 
 
 def energy_kernel(
-    index, tiles, rows, total, who, prev, own, following, mine, theirs, *rest, factor
+    index, tiles, rows, total, prev, own, following, mine, theirs, *rest, factor
 ):
-    sheets, (out, table, strips, near, far, weights, sems) = rest[:8], rest[8:]
+    sheets, (out, table, strips, near, far, weights, sems) = rest[:2], rest[2:]
     low = left_lanes((ROWS, 128))
     late = [
         pltpu.make_async_copy(src, table.at[pl.ds(n * TILES, TILES)], sems.at[n])
@@ -153,8 +151,7 @@
         pltpu.make_async_copy(theirs, far, sems.at[4]),
     ]
     for n, sheet in enumerate(sheets):
-        spot = weights.at[n // 4, pl.ds(n % 4 * SHEET, SHEET)]
-        early.append(pltpu.make_async_copy(sheet, spot, sems.at[5 + n]))
+        early.append(pltpu.make_async_copy(sheet, weights.at[n], sems.at[5 + n]))
     for copy in early + late:
         copy.start()
     table[ZERO_TILE] = jnp.zeros((ORB, BANDS), jnp.bfloat16)
@@ -165,21 +162,24 @@
     for copy in early:
         copy.wait()
 
-    def pair_body(n, carry):
-        spot = pl.ds(pl.multiple_of(n * 128, 128), 128)
+    def quad_body(n, carry):
+        spot = pl.ds(pl.multiple_of(n * 256, 256), 256)
         product = lax.dot_general(
             near[...], weights[0, spot, :], NT, preferred_element_type=jnp.float32
         ) + lax.dot_general(far[...], weights[1, spot, :], NT, preferred_element_type=jnp.float32)
-        product = product.reshape(TILES // 2, 4, 8, 128)
-        one, two = (pl.multiple_of(who[2 * n + u] * (2 * GRAD_PITCH), 8) for u in (0, 1))
-        for part in (0, 1):
-            front = product[:, 2 * part].reshape(ROWS, 128)
-            back = product[:, 2 * part + 1].reshape(ROWS, 128)
-            strips[pl.ds(one + part * GRAD_PITCH, ROWS), :] = jnp.where(low, front, swap(back))
-            strips[pl.ds(two + part * GRAD_PITCH, ROWS), :] = jnp.where(low, swap(front), back)
+        for pair in (0, 1):
+            piece = product[:, pair * 128 : (pair + 1) * 128].reshape(TILES // 2, 4, 8, 128)
+            base = (4 * n + 2 * pair) * (2 * GRAD_PITCH)
+            for part in (0, 1):
+                front = piece[:, 2 * part].reshape(ROWS, 128)
+                back = piece[:, 2 * part + 1].reshape(ROWS, 128)
+                one = pl.multiple_of(base + part * GRAD_PITCH, 8)
+                two = pl.multiple_of(base + (2 + part) * GRAD_PITCH, 8)
+                strips[pl.ds(one, ROWS), :] = jnp.where(low, front, swap(back))
+                strips[pl.ds(two, ROWS), :] = jnp.where(low, swap(front), back)
         return carry
 
-    lax.fori_loop(0, ORB // 2, pair_body, 0, unroll=2)
+    lax.fori_loop(0, ORB // 4, quad_body, 0)
     for copy in late:
         copy.wait()
 
@@ -208,21 +208,21 @@
     out[...] = jnp.sum(sums, axis=0, keepdims=True) * factor
 
 
-def energy_share(plan, who, prev, own, following, mine, theirs, sheets, factor):
+def energy_share(plan, prev, own, following, mine, theirs, sheets, factor):
     return pl.pallas_call(
         functools.partial(energy_kernel, factor=factor),
         grid_spec=pltpu.PrefetchScalarGridSpec(
-            num_scalar_prefetch=5,
+            num_scalar_prefetch=4,
             grid=(1,),
-            in_specs=[pl.BlockSpec(memory_space=pltpu.MemorySpace.HBM)] * 13,
+            in_specs=[pl.BlockSpec(memory_space=pltpu.MemorySpace.HBM)] * 7,
             out_specs=pl.BlockSpec((1, BANDS), lambda j, *_: (0, 0)),
             scratch_shapes=[
                 pltpu.VMEM((ZERO_TILE + 1, ORB, BANDS), jnp.bfloat16),
                 pltpu.VMEM((2 * ORB * GRAD_PITCH, 128), jnp.float32),
                 pltpu.VMEM((EDGES, FEAT // 2), jnp.bfloat16),
                 pltpu.VMEM((EDGES, FEAT // 2), jnp.bfloat16),
-                pltpu.VMEM((2, 4 * SHEET, FEAT // 2), jnp.bfloat16),
-                pltpu.SemaphoreType.DMA((13,)),
+                pltpu.VMEM((2, ORB * ORB, FEAT // 2), jnp.bfloat16),
+                pltpu.SemaphoreType.DMA((7,)),
             ],
         ),
         out_shape=jax.ShapeDtypeStruct((1, BANDS), jnp.float32),
@@ -231,7 +231,7 @@
             flops=2 * EDGES * ORB * ORB * (FEAT + BANDS * 4), bytes_accessed=16 * 2**20, transcendentals=0
         ),
         name="energy_share",
-    )(*plan, who, prev, own, following, mine, theirs, *sheets)
+    )(*plan, prev, own, following, mine, theirs, *sheets)
 
 
 def ring(axis, hop):
@@ -260,16 +260,9 @@
     half = FEAT // 2
     swapped = [(0, 1), (1, 0)]
     sheet = lax.dynamic_slice_in_dim(weights.T, core * half, half, 1)
-    sheet = jnp.concatenate(spread(sheet, 2), axis=0)
-    sheet = jnp.concatenate(spread(sheet, 1), axis=0)
-    sheets = spread(sheet, 0)
-    sheets = sheets + [lax.ppermute(sheet, "dp", swapped) for sheet in sheets]
-    back = jnp.arange(ORB, dtype=jnp.int32)
-    who = (
-        (myself // 16 - back // 16) % 4 * 16
-        + (myself // 4 - back // 4) % 4 * 4
-        + (myself - back) % 4
-    ).astype(jnp.int32)
+    sheet = lax.all_gather(sheet, "space", axis=0, tiled=True)
+    sheets = (sheet, lax.ppermute(sheet, "dp", swapped))
+
     where = neighbors.reshape(TILES, SLOTS)
     placed = (where // TILES - myself + 1 + nspace) % nspace * TILES + where % TILES
     slot = lax.broadcasted_iota(jnp.int32, (TILES, SLOTS), 1)
@@ -289,7 +282,7 @@
     keep = lax.dot_general(blocks, mine, over_edges, preferred_element_type=jnp.float32)
     summed = (keep + other.astype(jnp.float32)).astype(jnp.bfloat16)
     parts = lax.all_to_all(summed, "space", 0, 0, tiled=True)
-    partial = energy_share(plan, who, prev, own, following, mine, theirs, sheets, factor)
+    partial = energy_share(plan, prev, own, following, mine, theirs, sheets, factor)
     energies = partial
     for axis, place in ((2, myself % 4), (1, myself // 4 % 4), (0, myself // 16)):
         pieces = jnp.concatenate(spread(energies, axis), axis=0)

time: 274 us -> 206 us (0.75)
  waiting for transfers between devices: 137 us -> 65 us
  between operations: 0.98 us -> 14.5 us
  Pallas kernels: 63.9 us -> 51.6 us
  matrix products: 14.8 us -> 20.4 us
    ppermute x18 -> x9, waiting for transfers between devices: 98.3 us -> 20.9 us  [spread(): lax.ppermute(value, 'space', ring(axis, hop))]
    pallas_call x1, Pallas kernels: 40.1 us -> 27.8 us  [energy_share(): pl.pallas_call(functools.partial(energy_kernel, factor=factor), grid_spec...]
    all_gather x0 -> x1, waiting for transfers between devices: none -> 6.85 us  [step(): sheet = lax.all_gather(sheet, 'space', axis=0, tiled=True)]
    dot_general x1, matrix products: 6.2 us -> 10.6 us  [step(): lax.dot_general(blocks, mine, over_edges, preferred_element_type=jnp.floa...]
    ppermute x18 -> x9, starting transfers between devices: 14.6 us -> 15.8 us  [spread(): lax.ppermute(value, 'space', ring(axis, hop))]
  transfers between devices with their start and end apart: 26 -> 15, of which waited for: 17 -> 9; matrix products, arithmetic and copies ran while one was open for 9% -> 20% of each run, Pallas kernels for 15% -> 25%
where the time goes in v7:
time: 206 us
  waiting for transfers between devices  65 us (32%)
  Pallas kernels  51.6 us (25%)
  starting transfers between devices  30.7 us (15%)
  matrix products  20.4 us (10%)
  between operations  14.5 us (7%)
  local copies, waits for them, and re-layouts  12.6 us (6%)
  other arithmetic  9.11 us (4%)
    ppermute x1, waiting for transfers between devices, step(): following = lax.ppermute(own, 'space', down)  29 us
    pallas_call x1, Pallas kernels, energy_share(): pl.pallas_call(functools.partial(energy_kernel, factor=factor), grid_spec...  27.8 us
    pallas_call x1, Pallas kernels, grad_blocks(): pl.pallas_call(functools.partial(grad_blocks_kernel, factor=factor), grid...  23.7 us
    ppermute x9, waiting for transfers between devices, spread(): lax.ppermute(value, 'space', ring(axis, hop))  20.9 us
    ppermute x9, starting transfers between devices, spread(): lax.ppermute(value, 'space', ring(axis, hop))  15.8 us
    dot_general x1, matrix products, step(): lax.dot_general(blocks, mine, over_edges, preferred_element_type=jnp.floa...  10.6 us
    dot_general x1, matrix products, step(): lax.dot_general(blocks, theirs, over_edges, preferred_element_type=jnp.fl...  9.83 us
    ppermute x1, starting transfers between devices, step(): following = lax.ppermute(own, 'space', down)  8.86 us
  transfers between devices with their start and end apart: 15, of which 9 were waited for; matrix products, arithmetic and copies ran while one was open for 20% of the time, Pallas kernels for 25%

profile of v7, /device:TPU:0, one launch (start us, length us, event | category | flops | bytes accessed | tf_op | source)
XLA Modules:
  0.0 205.9 jit_solution(7432768120731452580)
XLA Ops:
  7.2 8.9 %collective-permute-start.1 = (bf16[64,64,256]{2,1,0:T(8,128)(2,1)}, bf16[64,64,256]{2,1,0:T(8,128)(2,1)}, u32[]{:S(2)}, u32[]{:S(2)}) collective-permute-start(bf16[64,64,256]{2,1,0:T(8,128)(2,1)} %bitcast.34), channel_id=1, source_target_pairs={{1,0},{2,1},{3,2},{4,3},{5,4},{6,5},{7,6},{8,7},{9,8},{10,9},{11,1... | collective-permute-start | bytes 6291464 | tf_op jit(solution)/shard_map/ppermute | solution.py:259
  16.8 0.7 and_select_fusion.1
  18.3 0.7 iota_compare_fusion.2
  19.2 0.8 copy.13
  20.0 2.7 %reshape.98 = bf16[32,2,4,4,1024]{4,3,2,1,0:T(4,128)(2,1)S(1)} reshape(bf16[1,64,16,1024]{3,2,1,0:T(8,128)(2,1)} %param.6) | data formatting | bytes 4194304 | tf_op jit(solution)/shard_map/reshape | solution.py:273
  22.8 2.4 %copy.17 = bf16[32,2,4,4,1024]{4,2,1,3,0:T(4,128)(2,1)} copy(bf16[32,2,4,4,1024]{4,3,2,1,0:T(4,128)(2,1)S(1)} %reshape.98) | data formatting | bytes 4194304 | tf_op jit(solution)/shard_map/reshape | solution.py:273
  25.2 2.6 %reshape.99 = bf16[1024,1024]{1,0:T(8,128)(2,1)S(1)} reshape(bf16[32,4,2,4,1024]{4,3,2,1,0:T(4,128)(2,1)} %bitcast.32) | data formatting | bytes 4194304 | tf_op jit(solution)/shard_map/reshape | solution.py:273
  28.6 1.3 constant_dynamic-slice_fusion.12
  29.9 1.3 subtract_select_fusion
  31.2 1.9 multiply_convert_fusion.weighted
  33.1 29.0 %collective-permute-done.1.following = bf16[64,64,256]{2,1,0:T(8,128)(2,1)} collective-permute-done((bf16[64,64,256]{2,1,0:T(8,128)(2,1)}, bf16[64,64,256]{2,1,0:T(8,128)(2,1)}, u32[]{:S(2)}, u32[]{:S(2)}) %collective-permute-start.1) | collective-permute-done | bytes 2097184 | tf_op jit(solution)/shard_map/ppermute | solution.py:259
  62.0 7.6 %collective-permute-done.prev = bf16[64,64,256]{2,1,0:T(8,128)(2,1)} collective-permute-done((bf16[64,64,256]{2,1,0:T(8,128)(2,1)}, bf16[64,64,256]{2,1,0:T(8,128)(2,1)}, u32[]{:S(2)}, u32[]{:S(2)}) %collective-permute-start) | collective-permute-done | bytes 2097184 | tf_op jit(solution)/shard_map/ppermute | solution.py:258
  69.6 23.7 %grad_blocks.1 = bf16[1024,4096]{1,0:T(8,128)(2,1)} custom-call(s32[1040]{0:T(1024)} %concatenate.12.index, s32[256]{0:T(256)} %get-tuple-element.5.tiles, s32[256]{0:T(256)} %get-tuple-element.4.rows, s32[1]{0:T(128)} %bitcast.4.total, bf16[64,64,256]{2,1,0:T(8,128)(2,1)} %collective-permute-done.prev, bf16[64,64,256]{2,1,0:T(8,128)(2,1)} %bitcast.36, ...), custom_call_target="tpu_custom_call" | custom-call | flops 8589934592 | bytes 16777216 | tf_op jit(solution)/shard_map/grad_blocks/pallas_call | solution.py:104
  93.4 9.8 %convolution_convert_fusion = bf16[4096,512]{1,0:T(8,128)(2,1)} fusion(bf16[1024,4096]{1,0:T(8,128)(2,1)} %grad_blocks.1, bf16[1024,512]{1,0:T(8,128)(2,1)S(1)} %get-tuple-element.2.theirs), kind=kOutput, calls=%fused_computation.2 | convolution fusion | flops 4297064448 | bytes 13631488 | tf_op jit(solution)/shard_map/dot_general | solution.py:280
  103.3 6.8 %all-gather.2.cloned.1.call-done.rest_0_ = bf16[4096,512]{1,0:T(8,128)(2,1)} async-done(((bf16[64,512]{1,0:T(8,128)(2,1)}), bf16[4096,512]{1,0:T(8,128)(2,1)}) %all-gather.2.cloned.1.call-update) | async-done | bytes 4194320 | tf_op jit(solution)/shard_map/all_gather | solution.py:263
  110.8 10.6 %add_convert_fusion = bf16[4096,512]{1,0:T(8,128)(2,1)} fusion(bf16[4096,512]{1,0:T(8,128)(2,1)} %collective-permute-done.12, bf16[1024,4096]{1,0:T(8,128)(2,1)} %grad_blocks.1, bf16[1024,512]{1,0:T(8,128)(2,1)S(1)} %copy-done.3), kind=kOutput, calls=%fused_computation.1 | convolution fusion | flops 4301258752 | bytes 17825792 | tf_op jit(solution)/shard_map/dot_general | solution.py:282
  121.3 6.0 %all-to-all-start = ((bf16[64,64,512]{2,1,0:T(8,128)(2,1)}), bf16[64,64,512]{2,1,0:T(8,128)(2,1)}, u32[]{:S(2)}, u32[]{:S(2)}) async-start(bf16[64,64,512]{2,1,0:T(8,128)(2,1)} %bitcast.33), calls=%async_computation | async-start | bytes 8388608 | tf_op jit(solution)/shard_map/all_to_all | solution.py:284
  127.6 27.8 %energy_share.1 = f32[1,256]{1,0:T(1,128)} custom-call(s32[1040]{0:T(1024)} %concatenate.12.index, s32[256]{0:T(256)} %get-tuple-element.5.tiles, s32[256]{0:T(256)} %get-tuple-element.4.rows, s32[1]{0:T(128)} %bitcast.4.total, bf16[64,64,256]{2,1,0:T(8,128)(2,1)} %collective-permute-done.prev, bf16[64,64,256]{2,1,0:T(8,128)(2,1)} %bitcast.37, ...), custom_call_target="tpu_custom_call" | custom-call | flops 17179869184 | bytes 16777216 | tf_op jit(solution)/shard_map/energy_share/pallas_call | solution.py:212
  155.5 2.4 %collective-permute-start.5 = (f32[1,256]{1,0:T(1,128)}, f32[1,256]{1,0:T(1,128)S(1)}, u32[]{:S(2)}, u32[]{:S(2)}) collective-permute-start(f32[1,256]{1,0:T(1,128)} %energy_share.1), channel_id=1, source_target_pairs={{0,3},{1,0},{2,1},{3,2},{4,7},{5,4},{6,5},{7,6},{8,11},{9,8},{10,9... | collective-permute-start | bytes 3080 | tf_op jit(solution)/shard_map/ppermute | solution.py:247
  157.9 1.2 collective-permute-start.4
  159.2 16.3 %collective-permute-done.5 = f32[1,256]{1,0:T(1,128)S(1)} collective-permute-done((f32[1,256]{1,0:T(1,128)}, f32[1,256]{1,0:T(1,128)S(1)}, u32[]{:S(2)}, u32[]{:S(2)}) %collective-permute-start.5) | collective-permute-done | bytes 1056 | tf_op jit(solution)/shard_map/ppermute | solution.py:247
  175.9 0.7 pad_maximum_fusion
  176.7 4.2 %collective-permute-start.8 = (f32[1,256]{1,0:T(1,128)S(1)}, f32[1,256]{1,0:T(1,128)S(1)}, u32[]{:S(2)}, u32[]{:S(2)}) collective-permute-start(f32[1,256]{1,0:T(1,128)S(1)} %fusion.9), channel_id=1, source_target_pairs={{0,12},{1,13},{2,14},{3,15},{4,0},{5,1},{6,2},{7,3},{8,4},{9,5},{1... | collective-permute-start | bytes 3080 | tf_op jit(solution)/shard_map/ppermute | solution.py:247
  180.9 4.5 %collective-permute-start.7 = (f32[1,256]{1,0:T(1,128)S(1)}, f32[1,256]{1,0:T(1,128)S(1)}, u32[]{:S(2)}, u32[]{:S(2)}) collective-permute-start(f32[1,256]{1,0:T(1,128)S(1)} %fusion.9), channel_id=1, source_target_pairs={{0,8},{1,9},{2,10},{3,11},{4,12},{5,13},{6,14},{7,15},{8,0},{9,1},... | collective-permute-start | bytes 3080 | tf_op jit(solution)/shard_map/ppermute | solution.py:247
  185.4 2.8 %convert_reduce_fusion = f32[64,512]{1,0:T(8,128)S(1)} fusion(bf16[64,64,512]{2,1,0:T(8,128)(2,1)} %all-to-all-done), kind=kLoop, calls=%fused_computation | loop fusion | flops 4161536 | bytes 4325376 | tf_op jit(solution)/shard_map/reduce_sum | solution.py:292
  188.3 1.9 collective-permute-done.6
  190.3 1.7 collective-permute-start.11
  192.0 1.0 collective-permute-start.10
  193.5 2.0 all_gather.7
  195.5 1.6 collective-permute-done.10
  197.0 0.7 collective-permute-done.9
  198.3 0.7 copy.19
  (45 shorter events, 5.0 us)
Async XLA Ops:
  7.2 8.9 %copy-start = (bf16[1024,64]{0,1:T(8,128)(2,1)S(1)}, bf16[1024,64]{0,1:T(8,128)(2,1)}, u32[]{:S(2)}) copy-start(bf16[1024,64]{0,1:T(8,128)(2,1)} %param.11) | copy-start | bytes 393220
  7.2 102.9 %all-gather.2.cloned.1.call-start = ((), (), s32[]{:S(2)}) async-start(), calls=%async_computation.1 | async-start | bytes 4259840 | tf_op jit(solution)/shard_map/all_gather | solution.py:263
  7.2 54.8 %collective-permute-start.1 = (bf16[64,64,256]{2,1,0:T(8,128)(2,1)}, bf16[64,64,256]{2,1,0:T(8,128)(2,1)}, u32[]{:S(2)}, u32[]{:S(2)}) collective-permute-start(bf16[64,64,256]{2,1,0:T(8,128)(2,1)} %bitcast.34), channel_id=1, source_target_pairs={{1,0},{2,1},{3,2},{4,3},{5,4},{6,5},{7,6},{8,7},{9,8},{10,9},{11,1... | collective-permute-start | bytes 6291464 | tf_op jit(solution)/shard_map/ppermute | solution.py:259
  16.1 53.6 %collective-permute-start = (bf16[64,64,256]{2,1,0:T(8,128)(2,1)}, bf16[64,64,256]{2,1,0:T(8,128)(2,1)}, u32[]{:S(2)}, u32[]{:S(2)}) collective-permute-start(bf16[64,64,256]{2,1,0:T(8,128)(2,1)} %bitcast.35), channel_id=1, source_target_pairs={{0,1},{1,2},{2,3},{3,4},{4,5},{5,6},{6,7},{7,8},{8,9},{9,10},{10,1... | collective-permute-start | bytes 6291464 | tf_op jit(solution)/shard_map/ppermute | solution.py:258
  22.8 5.7 %copy-start.5 = (s32[1,64]{1,0:T(1,128)S(1)}, s32[1,64]{1,0:T(1,128)}, u32[]{:S(2)}) copy-start(s32[1,64]{1,0:T(1,128)} %param.9) | copy-start | bytes 772
  25.2 6.0 %copy-start.4 = (f32[1,256]{1,0:T(1,128)S(1)}, f32[1,256]{1,0:T(1,128)}, u32[]{:S(2)}) copy-start(f32[1,256]{1,0:T(1,128)} %param.10) | copy-start | bytes 3076
  27.8 3.4 %copy-start.1 = (bf16[1,64,64,256]{3,2,1,0:T(8,128)(2,1)S(1)}, bf16[1,64,64,256]{3,2,1,0:T(8,128)(2,1)}, u32[]{:S(2)}) copy-start(bf16[1,64,64,256]{3,2,1,0:T(8,128)(2,1)} %param.7) | copy-start | bytes 6291460
  29.9 63.5 %copy-start.2 = (bf16[1024,512]{1,0:T(8,128)(2,1)}, bf16[1024,512]{1,0:T(8,128)(2,1)S(1)}, u32[]{:S(2)}) copy-start(bf16[1024,512]{1,0:T(8,128)(2,1)S(1)} %get-tuple-element.2.theirs) | copy-start | bytes 3145732
  93.4 17.3 %copy-start.3 = (bf16[1024,512]{1,0:T(8,128)(2,1)S(1)}, bf16[1024,512]{1,0:T(8,128)(2,1)}, u32[]{:S(2)}) copy-start(bf16[1024,512]{1,0:T(8,128)(2,1)} %get-tuple-element.3.mine) | copy-start | bytes 3145732
  103.2 7.5 %collective-permute-start.12 = (bf16[4096,512]{1,0:T(8,128)(2,1)}, bf16[4096,512]{1,0:T(8,128)(2,1)}, u32[]{:S(2)}, u32[]{:S(2)}) collective-permute-start(bf16[4096,512]{1,0:T(8,128)(2,1)} %convolution_convert_fusion), channel_id=1, source_target_pairs={{0,64},{64,0},{1,65},{65,1},{2,66},{66,2},{3,67},{67,3},{4,68},{68... | collective-permute-start | bytes 12582920 | tf_op jit(solution)/shard_map/ppermute | solution.py:281
  110.1 17.5 %collective-permute-start.2 = (bf16[4096,512]{1,0:T(8,128)(2,1)}, bf16[4096,512]{1,0:T(8,128)(2,1)}, u32[]{:S(2)}, u32[]{:S(2)}) collective-permute-start(bf16[4096,512]{1,0:T(8,128)(2,1)} %all-gather.2.cloned.1.call-done.rest_0_), channel_id=1, source_target_pairs={{0,64},{64,0},{1,65},{65,1},{2,66},{66,2},{3,67},{67,3},{4,68},{68... | collective-permute-start | bytes 12582920 | tf_op jit(solution)/shard_map/ppermute | solution.py:264
  121.3 64.1 %all-to-all-start = ((bf16[64,64,512]{2,1,0:T(8,128)(2,1)}), bf16[64,64,512]{2,1,0:T(8,128)(2,1)}, u32[]{:S(2)}, u32[]{:S(2)}) async-start(bf16[64,64,512]{2,1,0:T(8,128)(2,1)} %bitcast.33), calls=%async_computation | async-start | bytes 8388608 | tf_op jit(solution)/shard_map/all_to_all | solution.py:284
  155.5 20.1 %collective-permute-start.5 = (f32[1,256]{1,0:T(1,128)}, f32[1,256]{1,0:T(1,128)S(1)}, u32[]{:S(2)}, u32[]{:S(2)}) collective-permute-start(f32[1,256]{1,0:T(1,128)} %energy_share.1), channel_id=1, source_target_pairs={{0,3},{1,0},{2,1},{3,2},{4,7},{5,4},{6,5},{7,6},{8,11},{9,8},{10,9... | collective-permute-start | bytes 3080 | tf_op jit(solution)/shard_map/ppermute | solution.py:247
  157.9 18.0 %collective-permute-start.4 = (f32[1,256]{1,0:T(1,128)}, f32[1,256]{1,0:T(1,128)S(1)}, u32[]{:S(2)}, u32[]{:S(2)}) collective-permute-start(f32[1,256]{1,0:T(1,128)} %energy_share.1), channel_id=1, source_target_pairs={{0,2},{1,3},{2,0},{3,1},{4,6},{5,7},{6,4},{7,5},{8,10},{9,11},{10,... | collective-permute-start | bytes 3080 | tf_op jit(solution)/shard_map/ppermute | solution.py:247
  159.1 16.9 %collective-permute-start.3 = (f32[1,256]{1,0:T(1,128)}, f32[1,256]{1,0:T(1,128)S(1)}, u32[]{:S(2)}, u32[]{:S(2)}) collective-permute-start(f32[1,256]{1,0:T(1,128)} %energy_share.1), channel_id=1, source_target_pairs={{0,1},{1,2},{2,3},{3,0},{4,5},{5,6},{6,7},{7,4},{8,9},{9,10},{10,1... | collective-permute-start | bytes 3080 | tf_op jit(solution)/shard_map/ppermute | solution.py:247
  176.7 11.6 %collective-permute-start.8 = (f32[1,256]{1,0:T(1,128)S(1)}, f32[1,256]{1,0:T(1,128)S(1)}, u32[]{:S(2)}, u32[]{:S(2)}) collective-permute-start(f32[1,256]{1,0:T(1,128)S(1)} %fusion.9), channel_id=1, source_target_pairs={{0,12},{1,13},{2,14},{3,15},{4,0},{5,1},{6,2},{7,3},{8,4},{9,5},{1... | collective-permute-start | bytes 3080 | tf_op jit(solution)/shard_map/ppermute | solution.py:247
  180.9 7.4 %collective-permute-start.7 = (f32[1,256]{1,0:T(1,128)S(1)}, f32[1,256]{1,0:T(1,128)S(1)}, u32[]{:S(2)}, u32[]{:S(2)}) collective-permute-start(f32[1,256]{1,0:T(1,128)S(1)} %fusion.9), channel_id=1, source_target_pairs={{0,8},{1,9},{2,10},{3,11},{4,12},{5,13},{6,14},{7,15},{8,0},{9,1},... | collective-permute-start | bytes 3080 | tf_op jit(solution)/shard_map/ppermute | solution.py:247
  185.4 4.8 %collective-permute-start.6 = (f32[1,256]{1,0:T(1,128)S(1)}, f32[1,256]{1,0:T(1,128)S(1)}, u32[]{:S(2)}, u32[]{:S(2)}) collective-permute-start(f32[1,256]{1,0:T(1,128)S(1)} %fusion.9), channel_id=1, source_target_pairs={{0,4},{1,5},{2,6},{3,7},{4,8},{5,9},{6,10},{7,11},{8,12},{9,13},{1... | collective-permute-start | bytes 3080 | tf_op jit(solution)/shard_map/ppermute | solution.py:247
  190.3 5.2 %collective-permute-start.11 = (f32[1,256]{1,0:T(1,128)S(1)}, f32[1,256]{1,0:T(1,128)S(1)}, u32[]{:S(2)}, u32[]{:S(2)}) collective-permute-start(f32[1,256]{1,0:T(1,128)S(1)} %fusion.12), channel_id=1, source_target_pairs={{0,48},{1,49},{2,50},{3,51},{4,52},{5,53},{6,54},{7,55},{8,56},{9,... | collective-permute-start | bytes 3080 | tf_op jit(solution)/shard_map/ppermute | solution.py:247
  192.0 5.1 %collective-permute-start.10 = (f32[1,256]{1,0:T(1,128)S(1)}, f32[1,256]{1,0:T(1,128)S(1)}, u32[]{:S(2)}, u32[]{:S(2)}) collective-permute-start(f32[1,256]{1,0:T(1,128)S(1)} %fusion.12), channel_id=1, source_target_pairs={{0,32},{1,33},{2,34},{3,35},{4,36},{5,37},{6,38},{7,39},{8,40},{9,... | collective-permute-start | bytes 3080 | tf_op jit(solution)/shard_map/ppermute | solution.py:247
  193.0 4.8 %collective-permute-start.9 = (f32[1,256]{1,0:T(1,128)S(1)}, f32[1,256]{1,0:T(1,128)S(1)}, u32[]{:S(2)}, u32[]{:S(2)}) collective-permute-start(f32[1,256]{1,0:T(1,128)S(1)} %fusion.12), channel_id=1, source_target_pairs={{0,16},{1,17},{2,18},{3,19},{4,20},{5,21},{6,22},{7,23},{8,24},{9,... | collective-permute-start | bytes 3080 | tf_op jit(solution)/shard_map/ppermute | solution.py:247
Sparse Core Ops, SparseCore 0:
  16.9 93.1 all-gather.1

commit v8 on v6

--- a/solution.py
+++ b/solution.py
@@ -20,7 +20,7 @@
 SHEET = 1024
 GRAD_PITCH = ROWS + 8
 UNROLL = 8
-ENERGY_UNROLL = 4
+ENERGY_UNROLL = 8
 NT = (((1,), (1,)), ((), ()))
 
 
@@ -165,21 +165,24 @@
     for copy in early:
         copy.wait()
 
-    def pair_body(n, carry):
-        spot = pl.ds(pl.multiple_of(n * 128, 128), 128)
+    def quad_body(n, carry):
+        spot = pl.ds(pl.multiple_of(n * 256, 256), 256)
         product = lax.dot_general(
             near[...], weights[0, spot, :], NT, preferred_element_type=jnp.float32
         ) + lax.dot_general(far[...], weights[1, spot, :], NT, preferred_element_type=jnp.float32)
-        product = product.reshape(TILES // 2, 4, 8, 128)
-        one, two = (pl.multiple_of(who[2 * n + u] * (2 * GRAD_PITCH), 8) for u in (0, 1))
-        for part in (0, 1):
-            front = product[:, 2 * part].reshape(ROWS, 128)
-            back = product[:, 2 * part + 1].reshape(ROWS, 128)
-            strips[pl.ds(one + part * GRAD_PITCH, ROWS), :] = jnp.where(low, front, swap(back))
-            strips[pl.ds(two + part * GRAD_PITCH, ROWS), :] = jnp.where(low, swap(front), back)
+        for pair in (0, 1):
+            piece = product[:, pair * 128 : (pair + 1) * 128].reshape(TILES // 2, 4, 8, 128)
+            bases = [who[4 * n + 2 * pair + u] * (2 * GRAD_PITCH) for u in (0, 1)]
+            for part in (0, 1):
+                front = piece[:, 2 * part].reshape(ROWS, 128)
+                back = piece[:, 2 * part + 1].reshape(ROWS, 128)
+                one = pl.multiple_of(bases[0] + part * GRAD_PITCH, 8)
+                two = pl.multiple_of(bases[1] + part * GRAD_PITCH, 8)
+                strips[pl.ds(one, ROWS), :] = jnp.where(low, front, swap(back))
+                strips[pl.ds(two, ROWS), :] = jnp.where(low, swap(front), back)
         return carry
 
-    lax.fori_loop(0, ORB // 2, pair_body, 0, unroll=2)
+    lax.fori_loop(0, ORB // 4, quad_body, 0)
     for copy in late:
         copy.wait()
 
@@ -221,7 +224,7 @@
                 pltpu.VMEM((2 * ORB * GRAD_PITCH, 128), jnp.float32),
                 pltpu.VMEM((EDGES, FEAT // 2), jnp.bfloat16),
                 pltpu.VMEM((EDGES, FEAT // 2), jnp.bfloat16),
-                pltpu.VMEM((2, 4 * SHEET, FEAT // 2), jnp.bfloat16),
+                pltpu.VMEM((2, ORB * ORB, FEAT // 2), jnp.bfloat16),
                 pltpu.SemaphoreType.DMA((13,)),
             ],
         ),
@@ -270,6 +273,7 @@
         + (myself // 4 - back // 4) % 4 * 4
         + (myself - back) % 4
     ).astype(jnp.int32)
+
     where = neighbors.reshape(TILES, SLOTS)
     placed = (where // TILES - myself + 1 + nspace) % nspace * TILES + where % TILES
     slot = lax.broadcasted_iota(jnp.int32, (TILES, SLOTS), 1)
@@ -284,10 +288,16 @@
     mine = lax.dynamic_slice_in_dim(edges, core * half, half, 1)
     over_edges = (((0,), (0,)), ((), ()))
     blocks = grad_blocks(plan, prev, own, following, weighted, factor)
-    send = lax.dot_general(blocks, theirs, over_edges, preferred_element_type=jnp.float32)
-    other = lax.ppermute(send.astype(jnp.bfloat16), "dp", swapped)
-    keep = lax.dot_general(blocks, mine, over_edges, preferred_element_type=jnp.float32)
-    summed = (keep + other.astype(jnp.float32)).astype(jnp.bfloat16)
+    pieces = [blocks[:, : blocks.shape[1] // 2], blocks[:, blocks.shape[1] // 2 :]]
+    others = []
+    for piece in pieces:
+        send = lax.dot_general(piece, theirs, over_edges, preferred_element_type=jnp.float32)
+        others.append(lax.ppermute(send.astype(jnp.bfloat16), "dp", swapped))
+    summed = []
+    for piece, other in zip(pieces, others):
+        keep = lax.dot_general(piece, mine, over_edges, preferred_element_type=jnp.float32)
+        summed.append((keep + other.astype(jnp.float32)).astype(jnp.bfloat16))
+    summed = jnp.concatenate(summed, axis=0)
     parts = lax.all_to_all(summed, "space", 0, 0, tiled=True)
     partial = energy_share(plan, who, prev, own, following, mine, theirs, sheets, factor)
     energies = partial

time: 274 us -> 258 us (0.942)
  waiting for transfers between devices: 137 us -> 124 us
  Pallas kernels: 63.9 us -> 52.7 us
  starting transfers between devices: 31.5 us -> 42.6 us
  matrix products: 14.8 us -> 11.9 us
    ppermute x1, waiting for transfers between devices: 29 us -> 0.01 us  [step(): following = lax.ppermute(own, 'space', down)]
    ppermute x1, waiting for transfers between devices: 7.63 us -> 31.1 us  [step(): prev = lax.ppermute(own, 'space', up)]
    pallas_call x1, Pallas kernels: 40.1 us -> 29 us  [energy_share(): pl.pallas_call(functools.partial(energy_kernel, factor=factor), grid_spec...]
    ppermute x18, starting transfers between devices: 14.6 us -> 24.5 us  [spread(): lax.ppermute(value, 'space', ring(axis, hop))]
    ppermute x18, waiting for transfers between devices: 98.3 us -> 89.1 us  [spread(): lax.ppermute(value, 'space', ring(axis, hop))]
    dot_general x2 -> x4, matrix products: 14.8 us -> 11.9 us  [the longest x2 7.1 us: step(): lax.dot_general(piece, theirs, over_edges, preferred_element_type=jnp.flo...]
  transfers between devices with their start and end apart: 26 -> 27, of which waited for: 17 -> 19; matrix products, arithmetic and copies ran while one was open for 9% -> 10% of each run, Pallas kernels for 15% -> 11%
where the time goes in v8:
time: 258 us; the launch traced here: 256 us
  waiting for transfers between devices  124 us (48%)
  Pallas kernels  52.7 us (20%)
  starting transfers between devices  42.6 us (17%)
  matrix products  11.9 us (5%)
  local copies, waits for them, and re-layouts  11.3 us (4%)
  other arithmetic  11.2 us (4%)
    ppermute x18, waiting for transfers between devices, spread(): lax.ppermute(value, 'space', ring(axis, hop))  89.1 us
    ppermute x1, waiting for transfers between devices, step(): prev = lax.ppermute(own, 'space', up)  31.1 us
    pallas_call x1, Pallas kernels, energy_share(): pl.pallas_call(functools.partial(energy_kernel, factor=factor), grid_spec...  29 us
    ppermute x18, starting transfers between devices, spread(): lax.ppermute(value, 'space', ring(axis, hop))  24.5 us
    pallas_call x1, Pallas kernels, grad_blocks(): pl.pallas_call(functools.partial(grad_blocks_kernel, factor=factor), grid...  23.6 us
    all_to_all x1, starting transfers between devices, step(): parts = lax.all_to_all(summed, 'space', 0, 0, tiled=True)  7.95 us
    reshape x3, local copies, waits for them, and re-layouts, step(): features.reshape(TILES // 2, 2, 4, 4, FEAT).transpose(0, 3, 1, 2, 4)  7.72 us
    ppermute x1, starting transfers between devices, step(): following = lax.ppermute(own, 'space', down)  7.28 us
  transfers between devices with their start and end apart: 27, of which 19 were waited for; matrix products, arithmetic and copies ran while one was open for 10% of the time, Pallas kernels for 11%

profile of v8, /device:TPU:0, one launch (start us, length us, event | category | flops | bytes accessed | tf_op | source)
XLA Modules:
  0.0 256.3 jit_solution(4539251345068531447)
XLA Ops:
  0.6 1.7 collective-permute-start
  2.3 7.3 %collective-permute-start.1 = (bf16[64,64,256]{2,1,0:T(8,128)(2,1)}, bf16[64,64,256]{2,1,0:T(8,128)(2,1)}, u32[]{:S(2)}, u32[]{:S(2)}) collective-permute-start(bf16[64,64,256]{2,1,0:T(8,128)(2,1)} %bitcast.36), channel_id=1, source_target_pairs={{1,0},{2,1},{3,2},{4,3},{5,4},{6,5},{7,6},{8,7},{9,8},{10,9},{11,1... | collective-permute-start | bytes 6291464 | tf_op jit(solution)/shard_map/ppermute | solution.py:262
  11.1 2.7 %reshape.98 = bf16[32,2,4,4,1024]{4,3,2,1,0:T(4,128)(2,1)S(1)} reshape(bf16[1,64,16,1024]{3,2,1,0:T(8,128)(2,1)} %param.6) | data formatting | bytes 4194304 | tf_op jit(solution)/shard_map/reshape | solution.py:284
  13.8 2.4 copy.17
  16.3 2.5 reshape.99
  22.5 1.8 multiply_convert_fusion.weighted
  24.3 31.1 %collective-permute-done.prev = bf16[64,64,256]{2,1,0:T(8,128)(2,1)} collective-permute-done((bf16[64,64,256]{2,1,0:T(8,128)(2,1)}, bf16[64,64,256]{2,1,0:T(8,128)(2,1)}, u32[]{:S(2)}, u32[]{:S(2)}) %collective-permute-start) | collective-permute-done | bytes 2097184 | tf_op jit(solution)/shard_map/ppermute | solution.py:261
  55.4 23.6 %grad_blocks.1 = bf16[1024,4096]{1,0:T(8,128)(2,1)} custom-call(s32[1040]{0:T(1024)} %concatenate.22.index, s32[256]{0:T(256)} %get-tuple-element.7.tiles, s32[256]{0:T(256)} %get-tuple-element.6.rows, s32[1]{0:T(128)} %bitcast.4.total, bf16[64,64,256]{2,1,0:T(8,128)(2,1)} %collective-permute-done.prev, bf16[64,64,256]{2,1,0:T(8,128)(2,1)} %bitcast.37, ...), custom_call_target="tpu_custom_call" | custom-call | flops 8589934592 | bytes 16777216 | tf_op jit(solution)/shard_map/grad_blocks/pallas_call | solution.py:106
  79.1 4.7 %fusion.8 = bf16[2048,512]{1,0:T(8,128)(2,1)S(1)} fusion(bf16[1024,512]{1,0:T(8,128)(2,1)S(1)} %get-tuple-element.4.theirs, bf16[1024,4096]{1,0:T(8,128)(2,1)} %grad_blocks.1), kind=kOutput, calls=%fused_computation.13 | convolution fusion | flops 2148532224 | bytes 7340032 | tf_op jit(solution)/shard_map/dot_general | solution.py:294
  84.0 2.4 fusion.11
  87.5 2.8 %collective-permute-start.4 = (bf16[64,512]{1,0:T(8,128)(2,1)S(1)}, bf16[64,512]{1,0:T(8,128)(2,1)S(1)}, u32[]{:S(2)}, u32[]{:S(2)}) collective-permute-start(bf16[64,512]{1,0:T(8,128)(2,1)S(1)} %get-tuple-element.3), channel_id=1, source_target_pairs={{0,3},{1,0},{2,1},{3,2},{4,7},{5,4},{6,5},{7,6},{8,11},{9,8},{10,9... | collective-permute-start | bytes 196616 | tf_op jit(solution)/shard_map/ppermute | solution.py:250
  90.2 3.4 %collective-permute-done.2 = bf16[64,512]{1,0:T(8,128)(2,1)S(1)} collective-permute-done((bf16[64,512]{1,0:T(8,128)(2,1)S(1)}, bf16[64,512]{1,0:T(8,128)(2,1)S(1)}, u32[]{:S(2)}, u32[]{:S(2)}) %collective-permute-start.2) | collective-permute-done | bytes 65568 | tf_op jit(solution)/shard_map/ppermute | solution.py:250
  94.3 3.1 %collective-permute-start.6 = (bf16[256,512]{1,0:T(8,128)(2,1)S(1)}, bf16[256,512]{1,0:T(8,128)(2,1)S(1)}, u32[]{:S(2)}, u32[]{:S(2)}) collective-permute-start(bf16[256,512]{1,0:T(8,128)(2,1)S(1)} %pad_maximum_fusion.1), channel_id=1, source_target_pairs={{0,8},{1,9},{2,10},{3,11},{4,12},{5,13},{6,14},{7,15},{8,0},{9,1},... | collective-permute-start | bytes 786440 | tf_op jit(solution)/shard_map/ppermute | solution.py:250
  97.6 10.8 %collective-permute-done.5 = bf16[256,512]{1,0:T(8,128)(2,1)S(1)} collective-permute-done((bf16[256,512]{1,0:T(8,128)(2,1)S(1)}, bf16[256,512]{1,0:T(8,128)(2,1)S(1)}, u32[]{:S(2)}, u32[]{:S(2)}) %collective-permute-start.5) | collective-permute-done | bytes 262176 | tf_op jit(solution)/shard_map/ppermute | solution.py:250
  110.1 4.6 %collective-permute-start.9 = (bf16[1024,512]{1,0:T(8,128)(2,1)S(1)}, bf16[1024,512]{1,0:T(8,128)(2,1)}, u32[]{:S(2)}, u32[]{:S(2)}) collective-permute-start(bf16[1024,512]{1,0:T(8,128)(2,1)S(1)} %constant_dynamic-update-slice_fusion.rest_0_), channel_id=1, source_target_pairs={{0,32},{1,33},{2,34},{3,35},{4,36},{5,37},{6,38},{7,39},{8,40},{9,... | collective-permute-start | bytes 3145736 | tf_op jit(solution)/shard_map/ppermute | solution.py:250
  114.7 2.4 add_convert_fusion.1
  117.1 2.4 add_convert_fusion
  119.5 2.3 pad_maximum_fusion
  121.8 7.9 %all-to-all-start = ((bf16[64,64,512]{2,1,0:T(8,128)(2,1)}), bf16[64,64,512]{2,1,0:T(8,128)(2,1)}, u32[]{:S(2)}, u32[]{:S(2)}) async-start(bf16[64,64,512]{2,1,0:T(8,128)(2,1)} %bitcast.33), calls=%async_computation | async-start | bytes 8388608 | tf_op jit(solution)/shard_map/all_to_all | solution.py:301
  129.9 63.5 %collective-permute-done.8.rest_1_ = bf16[1024,512]{1,0:T(8,128)(2,1)S(1)} collective-permute-done((bf16[1024,512]{1,0:T(8,128)(2,1)S(1)}, bf16[1024,512]{1,0:T(8,128)(2,1)S(1)}, u32[]{:S(2)}, u32[]{:S(2)}) %collective-permute-start.8) | collective-permute-done | bytes 1048608 | tf_op jit(solution)/shard_map/ppermute | solution.py:250
  193.4 1.6 collective-permute-done.9.rest_2_
  196.2 1.8 collective-permute-done.13.rest_6_
  199.5 29.0 %energy_share.1 = f32[1,256]{1,0:T(1,128)} custom-call(s32[1040]{0:T(1024)} %concatenate.22.index, s32[256]{0:T(256)} %get-tuple-element.7.tiles, s32[256]{0:T(256)} %get-tuple-element.6.rows, s32[1]{0:T(128)} %bitcast.4.total, s32[64]{0:T(128)} %fusion.35.who, bf16[64,64,256]{2,1,0:T(8,128)(2,1)} %collective-permute-done.prev, ...), custom_call_target="tpu_custom_call" | custom-call | flops 17179869184 | bytes 16777216 | tf_op jit(solution)/shard_map/energy_share/pallas_call | solution.py:215
  228.6 5.6 %collective-permute-start.16 = (f32[1,256]{1,0:T(1,128)}, f32[1,256]{1,0:T(1,128)S(1)}, u32[]{:S(2)}, u32[]{:S(2)}) collective-permute-start(f32[1,256]{1,0:T(1,128)} %energy_share.1), channel_id=1, source_target_pairs={{0,2},{1,3},{2,0},{3,1},{4,6},{5,7},{6,4},{7,5},{8,10},{9,11},{10,... | collective-permute-start | bytes 3080 | tf_op jit(solution)/shard_map/ppermute | solution.py:250
  236.0 2.0 collective-permute-done.17
  238.7 1.6 collective-permute-start.19
  240.3 1.7 collective-permute-start.20
  242.0 1.5 collective-permute-done.18
  244.5 1.7 collective-permute-start.22
  246.2 1.6 collective-permute-start.23
  250.7 2.8 %convert_reduce_fusion = f32[64,512]{1,0:T(8,128)S(1)} fusion(bf16[64,64,512]{2,1,0:T(8,128)(2,1)} %all-to-all-done), kind=kLoop, calls=%fused_computation | loop fusion | flops 4161536 | bytes 4325376 | tf_op jit(solution)/shard_map/reduce_sum | solution.py:309
  253.6 2.0 all_gather.3
  (89 shorter events, 18.8 us)
Async XLA Ops:
  0.6 54.8 %collective-permute-start = (bf16[64,64,256]{2,1,0:T(8,128)(2,1)}, bf16[64,64,256]{2,1,0:T(8,128)(2,1)}, u32[]{:S(2)}, u32[]{:S(2)}) collective-permute-start(bf16[64,64,256]{2,1,0:T(8,128)(2,1)} %bitcast.35), channel_id=1, source_target_pairs={{0,1},{1,2},{2,3},{3,4},{4,5},{5,6},{6,7},{7,8},{8,9},{9,10},{10,1... | collective-permute-start | bytes 6291464 | tf_op jit(solution)/shard_map/ppermute | solution.py:261
  2.3 53.1 %collective-permute-start.1 = (bf16[64,64,256]{2,1,0:T(8,128)(2,1)}, bf16[64,64,256]{2,1,0:T(8,128)(2,1)}, u32[]{:S(2)}, u32[]{:S(2)}) collective-permute-start(bf16[64,64,256]{2,1,0:T(8,128)(2,1)} %bitcast.36), channel_id=1, source_target_pairs={{1,0},{2,1},{3,2},{4,3},{5,4},{6,5},{7,6},{8,7},{9,8},{10,9},{11,1... | collective-permute-start | bytes 6291464 | tf_op jit(solution)/shard_map/ppermute | solution.py:262
  16.3 6.2 %copy-start.6 = (f32[1,256]{1,0:T(1,128)S(1)}, f32[1,256]{1,0:T(1,128)}, u32[]{:S(2)}) copy-start(f32[1,256]{1,0:T(1,128)} %param.10) | copy-start | bytes 3076
  21.3 62.7 %copy-start.1 = (bf16[1024,512]{1,0:T(8,128)(2,1)}, bf16[1024,512]{1,0:T(8,128)(2,1)S(1)}, u32[]{:S(2)}) copy-start(bf16[1024,512]{1,0:T(8,128)(2,1)S(1)} %get-tuple-element.4.theirs) | copy-start | bytes 3145732
  83.8 30.9 %copy-start.2 = (bf16[1024,512]{1,0:T(8,128)(2,1)S(1)}, bf16[1024,512]{1,0:T(8,128)(2,1)}, u32[]{:S(2)}) copy-start(bf16[1024,512]{1,0:T(8,128)(2,1)} %get-tuple-element.5.mine) | copy-start | bytes 3145732
  83.9 30.8 %collective-permute-start.24 = (bf16[2048,512]{1,0:T(8,128)(2,1)S(1)}, bf16[2048,512]{1,0:T(8,128)(2,1)S(1)}, u32[]{:S(2)}, u32[]{:S(2)}) collective-permute-start(bf16[2048,512]{1,0:T(8,128)(2,1)S(1)} %fusion.8), channel_id=1, source_target_pairs={{0,64},{64,0},{1,65},{65,1},{2,66},{66,2},{3,67},{67,3},{4,68},{68... | collective-permute-start | bytes 6291464 | tf_op jit(solution)/shard_map/ppermute | solution.py:295
  86.4 30.7 %collective-permute-start.25 = (bf16[2048,512]{1,0:T(8,128)(2,1)S(1)}, bf16[2048,512]{1,0:T(8,128)(2,1)S(1)}, u32[]{:S(2)}, u32[]{:S(2)}) collective-permute-start(bf16[2048,512]{1,0:T(8,128)(2,1)S(1)} %fusion.11), channel_id=1, source_target_pairs={{0,64},{64,0},{1,65},{65,1},{2,66},{66,2},{3,67},{67,3},{4,68},{68... | collective-permute-start | bytes 6291464 | tf_op jit(solution)/shard_map/ppermute | solution.py:295
  86.9 6.7 %collective-permute-start.2 = (bf16[64,512]{1,0:T(8,128)(2,1)S(1)}, bf16[64,512]{1,0:T(8,128)(2,1)S(1)}, u32[]{:S(2)}, u32[]{:S(2)}) collective-permute-start(bf16[64,512]{1,0:T(8,128)(2,1)S(1)} %get-tuple-element.3), channel_id=1, source_target_pairs={{0,1},{1,2},{2,3},{3,0},{4,5},{5,6},{6,7},{7,4},{8,9},{9,10},{10,1... | collective-permute-start | bytes 196616 | tf_op jit(solution)/shard_map/ppermute | solution.py:250
  87.0 6.6 %collective-permute-start.3 = (bf16[64,512]{1,0:T(8,128)(2,1)S(1)}, bf16[64,512]{1,0:T(8,128)(2,1)S(1)}, u32[]{:S(2)}, u32[]{:S(2)}) collective-permute-start(bf16[64,512]{1,0:T(8,128)(2,1)S(1)} %get-tuple-element.3), channel_id=1, source_target_pairs={{0,2},{1,3},{2,0},{3,1},{4,6},{5,7},{6,4},{7,5},{8,10},{9,11},{10,... | collective-permute-start | bytes 196616 | tf_op jit(solution)/shard_map/ppermute | solution.py:250
  87.5 6.8 %collective-permute-start.4 = (bf16[64,512]{1,0:T(8,128)(2,1)S(1)}, bf16[64,512]{1,0:T(8,128)(2,1)S(1)}, u32[]{:S(2)}, u32[]{:S(2)}) collective-permute-start(bf16[64,512]{1,0:T(8,128)(2,1)S(1)} %get-tuple-element.3), channel_id=1, source_target_pairs={{0,3},{1,0},{2,1},{3,2},{4,7},{5,4},{6,5},{7,6},{8,11},{9,8},{10,9... | collective-permute-start | bytes 196616 | tf_op jit(solution)/shard_map/ppermute | solution.py:250
  94.3 14.2 %collective-permute-start.5 = (bf16[256,512]{1,0:T(8,128)(2,1)S(1)}, bf16[256,512]{1,0:T(8,128)(2,1)S(1)}, u32[]{:S(2)}, u32[]{:S(2)}) collective-permute-start(bf16[256,512]{1,0:T(8,128)(2,1)S(1)} %pad_maximum_fusion.1), channel_id=1, source_target_pairs={{0,4},{1,5},{2,6},{3,7},{4,8},{5,9},{6,10},{7,11},{8,12},{9,13},{1... | collective-permute-start | bytes 786440 | tf_op jit(solution)/shard_map/ppermute | solution.py:250
  94.3 14.1 %collective-permute-start.6 = (bf16[256,512]{1,0:T(8,128)(2,1)S(1)}, bf16[256,512]{1,0:T(8,128)(2,1)S(1)}, u32[]{:S(2)}, u32[]{:S(2)}) collective-permute-start(bf16[256,512]{1,0:T(8,128)(2,1)S(1)} %pad_maximum_fusion.1), channel_id=1, source_target_pairs={{0,8},{1,9},{2,10},{3,11},{4,12},{5,13},{6,14},{7,15},{8,0},{9,1},... | collective-permute-start | bytes 786440 | tf_op jit(solution)/shard_map/ppermute | solution.py:250
  97.5 11.6 %collective-permute-start.7 = (bf16[256,512]{1,0:T(8,128)(2,1)S(1)}, bf16[256,512]{1,0:T(8,128)(2,1)S(1)}, u32[]{:S(2)}, u32[]{:S(2)}) collective-permute-start(bf16[256,512]{1,0:T(8,128)(2,1)S(1)} %pad_maximum_fusion.1), channel_id=1, source_target_pairs={{0,12},{1,13},{2,14},{3,15},{4,0},{5,1},{6,2},{7,3},{8,4},{9,5},{1... | collective-permute-start | bytes 786440 | tf_op jit(solution)/shard_map/ppermute | solution.py:250
  109.1 20.7 %copy-start.5 = (bf16[1024,512]{1,0:T(8,128)(2,1)}, bf16[1024,512]{1,0:T(8,128)(2,1)S(1)}, u32[]{:S(2)}) copy-start(bf16[1024,512]{1,0:T(8,128)(2,1)S(1)} %constant_dynamic-update-slice_fusion.rest_0_) | copy-start | bytes 3145732
  109.1 84.3 %collective-permute-start.8 = (bf16[1024,512]{1,0:T(8,128)(2,1)S(1)}, bf16[1024,512]{1,0:T(8,128)(2,1)S(1)}, u32[]{:S(2)}, u32[]{:S(2)}) collective-permute-start(bf16[1024,512]{1,0:T(8,128)(2,1)S(1)} %constant_dynamic-update-slice_fusion.rest_0_), channel_id=1, source_target_pairs={{0,16},{1,17},{2,18},{3,19},{4,20},{5,21},{6,22},{7,23},{8,24},{9,... | collective-permute-start | bytes 3145736 | tf_op jit(solution)/shard_map/ppermute | solution.py:250
  110.1 84.9 %collective-permute-start.9 = (bf16[1024,512]{1,0:T(8,128)(2,1)S(1)}, bf16[1024,512]{1,0:T(8,128)(2,1)}, u32[]{:S(2)}, u32[]{:S(2)}) collective-permute-start(bf16[1024,512]{1,0:T(8,128)(2,1)S(1)} %constant_dynamic-update-slice_fusion.rest_0_), channel_id=1, source_target_pairs={{0,32},{1,33},{2,34},{3,35},{4,36},{5,37},{6,38},{7,39},{8,40},{9,... | collective-permute-start | bytes 3145736 | tf_op jit(solution)/shard_map/ppermute | solution.py:250
  114.7 80.3 %collective-permute-start.10 = (bf16[1024,512]{1,0:T(8,128)(2,1)S(1)}, bf16[1024,512]{1,0:T(8,128)(2,1)}, u32[]{:S(2)}, u32[]{:S(2)}) collective-permute-start(bf16[1024,512]{1,0:T(8,128)(2,1)S(1)} %constant_dynamic-update-slice_fusion.rest_0_), channel_id=1, source_target_pairs={{0,48},{1,49},{2,50},{3,51},{4,52},{5,53},{6,54},{7,55},{8,56},{9,... | collective-permute-start | bytes 3145736 | tf_op jit(solution)/shard_map/ppermute | solution.py:250
  121.8 128.9 %all-to-all-start = ((bf16[64,64,512]{2,1,0:T(8,128)(2,1)}), bf16[64,64,512]{2,1,0:T(8,128)(2,1)}, u32[]{:S(2)}, u32[]{:S(2)}) async-start(bf16[64,64,512]{2,1,0:T(8,128)(2,1)} %bitcast.33), calls=%async_computation | async-start | bytes 8388608 | tf_op jit(solution)/shard_map/all_to_all | solution.py:301
  129.8 66.3 %collective-permute-start.11 = (bf16[1024,512]{1,0:T(8,128)(2,1)S(1)}, bf16[1024,512]{1,0:T(8,128)(2,1)S(1)}, u32[]{:S(2)}, u32[]{:S(2)}) collective-permute-start(bf16[1024,512]{1,0:T(8,128)(2,1)S(1)} %constant_dynamic-update-slice_fusion.rest_0_), channel_id=1, source_target_pairs={{0,64},{64,0},{1,65},{65,1},{2,66},{66,2},{3,67},{67,3},{4,68},{68... | collective-permute-start | bytes 3145736 | tf_op jit(solution)/shard_map/ppermute | solution.py:269
  193.4 6.1 %copy-start.8 = (bf16[1024,512]{1,0:T(8,128)(2,1)}, bf16[1024,512]{1,0:T(8,128)(2,1)S(1)}, u32[]{:S(2)}) copy-start(bf16[1024,512]{1,0:T(8,128)(2,1)S(1)} %collective-permute-done.8.rest_1_) | copy-start | bytes 3145732
  193.4 2.8 %collective-permute-start.12 = (bf16[1024,512]{1,0:T(8,128)(2,1)S(1)}, bf16[1024,512]{1,0:T(8,128)(2,1)}, u32[]{:S(2)}, u32[]{:S(2)}) collective-permute-start(bf16[1024,512]{1,0:T(8,128)(2,1)S(1)} %collective-permute-done.8.rest_1_), channel_id=1, source_target_pairs={{0,64},{64,0},{1,65},{65,1},{2,66},{66,2},{3,67},{67,3},{4,68},{68... | collective-permute-start | bytes 3145736 | tf_op jit(solution)/shard_map/ppermute | solution.py:269
  195.0 3.0 %collective-permute-start.13 = (bf16[1024,512]{1,0:T(8,128)(2,1)}, bf16[1024,512]{1,0:T(8,128)(2,1)}, u32[]{:S(2)}, u32[]{:S(2)}) collective-permute-start(bf16[1024,512]{1,0:T(8,128)(2,1)} %collective-permute-done.9.rest_2_), channel_id=1, source_target_pairs={{0,64},{64,0},{1,65},{65,1},{2,66},{66,2},{3,67},{67,3},{4,68},{68... | collective-permute-start | bytes 3145736 | tf_op jit(solution)/shard_map/ppermute | solution.py:269
  195.0 4.5 %collective-permute-start.14 = (bf16[1024,512]{1,0:T(8,128)(2,1)}, bf16[1024,512]{1,0:T(8,128)(2,1)}, u32[]{:S(2)}, u32[]{:S(2)}) collective-permute-start(bf16[1024,512]{1,0:T(8,128)(2,1)} %collective-permute-done.10.rest_3_), channel_id=1, source_target_pairs={{0,64},{64,0},{1,65},{65,1},{2,66},{66,2},{3,67},{67,3},{4,68},{68... | collective-permute-start | bytes 3145736 | tf_op jit(solution)/shard_map/ppermute | solution.py:269
  228.5 6.0 %collective-permute-start.15 = (f32[1,256]{1,0:T(1,128)}, f32[1,256]{1,0:T(1,128)S(1)}, u32[]{:S(2)}, u32[]{:S(2)}) collective-permute-start(f32[1,256]{1,0:T(1,128)} %energy_share.1), channel_id=1, source_target_pairs={{0,1},{1,2},{2,3},{3,0},{4,5},{5,6},{6,7},{7,4},{8,9},{9,10},{10,1... | collective-permute-start | bytes 3080 | tf_op jit(solution)/shard_map/ppermute | solution.py:250
  228.6 7.4 %collective-permute-start.16 = (f32[1,256]{1,0:T(1,128)}, f32[1,256]{1,0:T(1,128)S(1)}, u32[]{:S(2)}, u32[]{:S(2)}) collective-permute-start(f32[1,256]{1,0:T(1,128)} %energy_share.1), channel_id=1, source_target_pairs={{0,2},{1,3},{2,0},{3,1},{4,6},{5,7},{6,4},{7,5},{8,10},{9,11},{10,... | collective-permute-start | bytes 3080 | tf_op jit(solution)/shard_map/ppermute | solution.py:250
  234.2 3.8 %collective-permute-start.17 = (f32[1,256]{1,0:T(1,128)}, f32[1,256]{1,0:T(1,128)S(1)}, u32[]{:S(2)}, u32[]{:S(2)}) collective-permute-start(f32[1,256]{1,0:T(1,128)} %energy_share.1), channel_id=1, source_target_pairs={{0,3},{1,0},{2,1},{3,2},{4,7},{5,4},{6,5},{7,6},{8,11},{9,8},{10,9... | collective-permute-start | bytes 3080 | tf_op jit(solution)/shard_map/ppermute | solution.py:250
  238.6 4.9 %collective-permute-start.18 = (f32[1,256]{1,0:T(1,128)S(1)}, f32[1,256]{1,0:T(1,128)S(1)}, u32[]{:S(2)}, u32[]{:S(2)}) collective-permute-start(f32[1,256]{1,0:T(1,128)S(1)} %fusion.27), channel_id=1, source_target_pairs={{0,4},{1,5},{2,6},{3,7},{4,8},{5,9},{6,10},{7,11},{8,12},{9,13},{1... | collective-permute-start | bytes 3080 | tf_op jit(solution)/shard_map/ppermute | solution.py:250
  238.7 5.2 %collective-permute-start.19 = (f32[1,256]{1,0:T(1,128)S(1)}, f32[1,256]{1,0:T(1,128)S(1)}, u32[]{:S(2)}, u32[]{:S(2)}) collective-permute-start(f32[1,256]{1,0:T(1,128)S(1)} %fusion.27), channel_id=1, source_target_pairs={{0,8},{1,9},{2,10},{3,11},{4,12},{5,13},{6,14},{7,15},{8,0},{9,1},... | collective-permute-start | bytes 3080 | tf_op jit(solution)/shard_map/ppermute | solution.py:250
  240.3 4.1 %collective-permute-start.20 = (f32[1,256]{1,0:T(1,128)S(1)}, f32[1,256]{1,0:T(1,128)S(1)}, u32[]{:S(2)}, u32[]{:S(2)}) collective-permute-start(f32[1,256]{1,0:T(1,128)S(1)} %fusion.27), channel_id=1, source_target_pairs={{0,12},{1,13},{2,14},{3,15},{4,0},{5,1},{6,2},{7,3},{8,4},{9,5},{1... | collective-permute-start | bytes 3080 | tf_op jit(solution)/shard_map/ppermute | solution.py:250
  244.4 4.9 %collective-permute-start.21 = (f32[1,256]{1,0:T(1,128)S(1)}, f32[1,256]{1,0:T(1,128)S(1)}, u32[]{:S(2)}, u32[]{:S(2)}) collective-permute-start(f32[1,256]{1,0:T(1,128)S(1)} %fusion.30), channel_id=1, source_target_pairs={{0,16},{1,17},{2,18},{3,19},{4,20},{5,21},{6,22},{7,23},{8,24},{9,... | collective-permute-start | bytes 3080 | tf_op jit(solution)/shard_map/ppermute | solution.py:250
  244.5 5.2 %collective-permute-start.22 = (f32[1,256]{1,0:T(1,128)S(1)}, f32[1,256]{1,0:T(1,128)S(1)}, u32[]{:S(2)}, u32[]{:S(2)}) collective-permute-start(f32[1,256]{1,0:T(1,128)S(1)} %fusion.30), channel_id=1, source_target_pairs={{0,32},{1,33},{2,34},{3,35},{4,36},{5,37},{6,38},{7,39},{8,40},{9,... | collective-permute-start | bytes 3080 | tf_op jit(solution)/shard_map/ppermute | solution.py:250
  246.2 4.0 %collective-permute-start.23 = (f32[1,256]{1,0:T(1,128)S(1)}, f32[1,256]{1,0:T(1,128)S(1)}, u32[]{:S(2)}, u32[]{:S(2)}) collective-permute-start(f32[1,256]{1,0:T(1,128)S(1)} %fusion.30), channel_id=1, source_target_pairs={{0,48},{1,49},{2,50},{3,51},{4,52},{5,53},{6,54},{7,55},{8,56},{9,... | collective-permute-start | bytes 3080 | tf_op jit(solution)/shard_map/ppermute | solution.py:250
  (6 other events, 24.9 us)

commit v9 on v8

--- a/solution.py
+++ b/solution.py
@@ -280,9 +280,8 @@
     used = counts.reshape(TILES)
     plan = plan_items(jnp.where(slot < used[:, None], placed, ZERO_TILE), used)
     weighted = (own.astype(jnp.float32) * occupation).astype(jnp.bfloat16)
-    edges = (
-        features.reshape(TILES // 2, 2, 4, 4, FEAT).transpose(0, 3, 1, 2, 4).reshape(EDGES, FEAT)
-    )
+    edges = features.reshape(TILES // 2, 2, 4, 4, FEAT).transpose(0, 3, 1, 2, 4)
+    edges = edges.reshape(EDGES, FEAT)
 
     theirs = lax.dynamic_slice_in_dim(edges, (1 - core) * half, half, 1)
     mine = lax.dynamic_slice_in_dim(edges, core * half, half, 1)

time: 258 us -> 258 us (level)
  no operation moved by 1% of the time
where the time goes in v9:
time: 258 us; the launch traced here: 256 us
  waiting for transfers between devices  124 us (48%)
  Pallas kernels  52.7 us (20%)
  starting transfers between devices  42.6 us (17%)
  matrix products  11.9 us (5%)
  local copies, waits for them, and re-layouts  11.3 us (4%)
  other arithmetic  11.2 us (4%)
    ppermute x18, waiting for transfers between devices, spread(): lax.ppermute(value, 'space', ring(axis, hop))  89.1 us
    ppermute x1, waiting for transfers between devices, step(): prev = lax.ppermute(own, 'space', up)  31.1 us
    pallas_call x1, Pallas kernels, energy_share(): pl.pallas_call(functools.partial(energy_kernel, factor=factor), grid_spec...  29 us
    ppermute x18, starting transfers between devices, spread(): lax.ppermute(value, 'space', ring(axis, hop))  24.5 us
    pallas_call x1, Pallas kernels, grad_blocks(): pl.pallas_call(functools.partial(grad_blocks_kernel, factor=factor), grid...  23.6 us
    all_to_all x1, starting transfers between devices, step(): parts = lax.all_to_all(summed, 'space', 0, 0, tiled=True)  7.95 us
    ppermute x1, starting transfers between devices, step(): following = lax.ppermute(own, 'space', down)  7.28 us
    dot_general x2, matrix products, step(): lax.dot_general(piece, theirs, over_edges, preferred_element_type=jnp.flo...  7.1 us
  transfers between devices with their start and end apart: 27, of which 19 were waited for; matrix products, arithmetic and copies ran while one was open for 10% of the time, Pallas kernels for 11%

profile of v9, /device:TPU:0, one launch (start us, length us, event | category | flops | bytes accessed | tf_op | source)
XLA Modules:
  0.0 256.3 jit_solution(4539251345068531447)
XLA Ops:
  0.6 1.7 collective-permute-start
  2.3 7.3 %collective-permute-start.1 = (bf16[64,64,256]{2,1,0:T(8,128)(2,1)}, bf16[64,64,256]{2,1,0:T(8,128)(2,1)}, u32[]{:S(2)}, u32[]{:S(2)}) collective-permute-start(bf16[64,64,256]{2,1,0:T(8,128)(2,1)} %bitcast.36), channel_id=1, source_target_pairs={{1,0},{2,1},{3,2},{4,3},{5,4},{6,5},{7,6},{8,7},{9,8},{10,9},{11,1... | collective-permute-start | bytes 6291464 | tf_op jit(solution)/shard_map/ppermute | solution.py:262
  11.1 2.7 %reshape.98 = bf16[32,2,4,4,1024]{4,3,2,1,0:T(4,128)(2,1)S(1)} reshape(bf16[1,64,16,1024]{3,2,1,0:T(8,128)(2,1)} %param.6) | data formatting | bytes 4194304 | tf_op jit(solution)/shard_map/reshape | solution.py:283
  13.8 2.4 copy.17
  16.3 2.5 reshape.99
  22.5 1.8 multiply_convert_fusion.weighted
  24.3 31.1 %collective-permute-done.prev = bf16[64,64,256]{2,1,0:T(8,128)(2,1)} collective-permute-done((bf16[64,64,256]{2,1,0:T(8,128)(2,1)}, bf16[64,64,256]{2,1,0:T(8,128)(2,1)}, u32[]{:S(2)}, u32[]{:S(2)}) %collective-permute-start) | collective-permute-done | bytes 2097184 | tf_op jit(solution)/shard_map/ppermute | solution.py:261
  55.4 23.6 %grad_blocks.1 = bf16[1024,4096]{1,0:T(8,128)(2,1)} custom-call(s32[1040]{0:T(1024)} %concatenate.22.index, s32[256]{0:T(256)} %get-tuple-element.7.tiles, s32[256]{0:T(256)} %get-tuple-element.6.rows, s32[1]{0:T(128)} %bitcast.4.total, bf16[64,64,256]{2,1,0:T(8,128)(2,1)} %collective-permute-done.prev, bf16[64,64,256]{2,1,0:T(8,128)(2,1)} %bitcast.37, ...), custom_call_target="tpu_custom_call" | custom-call | flops 8589934592 | bytes 16777216 | tf_op jit(solution)/shard_map/grad_blocks/pallas_call | solution.py:106
  79.1 4.7 %fusion.8 = bf16[2048,512]{1,0:T(8,128)(2,1)S(1)} fusion(bf16[1024,512]{1,0:T(8,128)(2,1)S(1)} %get-tuple-element.4.theirs, bf16[1024,4096]{1,0:T(8,128)(2,1)} %grad_blocks.1), kind=kOutput, calls=%fused_computation.13 | convolution fusion | flops 2148532224 | bytes 7340032 | tf_op jit(solution)/shard_map/dot_general | solution.py:293
  84.0 2.4 fusion.11
  87.5 2.8 %collective-permute-start.4 = (bf16[64,512]{1,0:T(8,128)(2,1)S(1)}, bf16[64,512]{1,0:T(8,128)(2,1)S(1)}, u32[]{:S(2)}, u32[]{:S(2)}) collective-permute-start(bf16[64,512]{1,0:T(8,128)(2,1)S(1)} %get-tuple-element.3), channel_id=1, source_target_pairs={{0,3},{1,0},{2,1},{3,2},{4,7},{5,4},{6,5},{7,6},{8,11},{9,8},{10,9... | collective-permute-start | bytes 196616 | tf_op jit(solution)/shard_map/ppermute | solution.py:250
  90.2 3.4 %collective-permute-done.2 = bf16[64,512]{1,0:T(8,128)(2,1)S(1)} collective-permute-done((bf16[64,512]{1,0:T(8,128)(2,1)S(1)}, bf16[64,512]{1,0:T(8,128)(2,1)S(1)}, u32[]{:S(2)}, u32[]{:S(2)}) %collective-permute-start.2) | collective-permute-done | bytes 65568 | tf_op jit(solution)/shard_map/ppermute | solution.py:250
  94.3 3.1 %collective-permute-start.6 = (bf16[256,512]{1,0:T(8,128)(2,1)S(1)}, bf16[256,512]{1,0:T(8,128)(2,1)S(1)}, u32[]{:S(2)}, u32[]{:S(2)}) collective-permute-start(bf16[256,512]{1,0:T(8,128)(2,1)S(1)} %pad_maximum_fusion.1), channel_id=1, source_target_pairs={{0,8},{1,9},{2,10},{3,11},{4,12},{5,13},{6,14},{7,15},{8,0},{9,1},... | collective-permute-start | bytes 786440 | tf_op jit(solution)/shard_map/ppermute | solution.py:250
  97.6 10.8 %collective-permute-done.5 = bf16[256,512]{1,0:T(8,128)(2,1)S(1)} collective-permute-done((bf16[256,512]{1,0:T(8,128)(2,1)S(1)}, bf16[256,512]{1,0:T(8,128)(2,1)S(1)}, u32[]{:S(2)}, u32[]{:S(2)}) %collective-permute-start.5) | collective-permute-done | bytes 262176 | tf_op jit(solution)/shard_map/ppermute | solution.py:250
  110.1 4.6 %collective-permute-start.9 = (bf16[1024,512]{1,0:T(8,128)(2,1)S(1)}, bf16[1024,512]{1,0:T(8,128)(2,1)}, u32[]{:S(2)}, u32[]{:S(2)}) collective-permute-start(bf16[1024,512]{1,0:T(8,128)(2,1)S(1)} %constant_dynamic-update-slice_fusion.rest_0_), channel_id=1, source_target_pairs={{0,32},{1,33},{2,34},{3,35},{4,36},{5,37},{6,38},{7,39},{8,40},{9,... | collective-permute-start | bytes 3145736 | tf_op jit(solution)/shard_map/ppermute | solution.py:250
  114.7 2.4 add_convert_fusion.1
  117.1 2.4 add_convert_fusion
  119.5 2.3 pad_maximum_fusion
  121.8 7.9 %all-to-all-start = ((bf16[64,64,512]{2,1,0:T(8,128)(2,1)}), bf16[64,64,512]{2,1,0:T(8,128)(2,1)}, u32[]{:S(2)}, u32[]{:S(2)}) async-start(bf16[64,64,512]{2,1,0:T(8,128)(2,1)} %bitcast.33), calls=%async_computation | async-start | bytes 8388608 | tf_op jit(solution)/shard_map/all_to_all | solution.py:300
  129.9 63.5 %collective-permute-done.8.rest_1_ = bf16[1024,512]{1,0:T(8,128)(2,1)S(1)} collective-permute-done((bf16[1024,512]{1,0:T(8,128)(2,1)S(1)}, bf16[1024,512]{1,0:T(8,128)(2,1)S(1)}, u32[]{:S(2)}, u32[]{:S(2)}) %collective-permute-start.8) | collective-permute-done | bytes 1048608 | tf_op jit(solution)/shard_map/ppermute | solution.py:250
  193.4 1.6 collective-permute-done.9.rest_2_
  196.2 1.8 collective-permute-done.13.rest_6_
  199.5 29.0 %energy_share.1 = f32[1,256]{1,0:T(1,128)} custom-call(s32[1040]{0:T(1024)} %concatenate.22.index, s32[256]{0:T(256)} %get-tuple-element.7.tiles, s32[256]{0:T(256)} %get-tuple-element.6.rows, s32[1]{0:T(128)} %bitcast.4.total, s32[64]{0:T(128)} %fusion.35.who, bf16[64,64,256]{2,1,0:T(8,128)(2,1)} %collective-permute-done.prev, ...), custom_call_target="tpu_custom_call" | custom-call | flops 17179869184 | bytes 16777216 | tf_op jit(solution)/shard_map/energy_share/pallas_call | solution.py:215
  228.6 5.6 %collective-permute-start.16 = (f32[1,256]{1,0:T(1,128)}, f32[1,256]{1,0:T(1,128)S(1)}, u32[]{:S(2)}, u32[]{:S(2)}) collective-permute-start(f32[1,256]{1,0:T(1,128)} %energy_share.1), channel_id=1, source_target_pairs={{0,2},{1,3},{2,0},{3,1},{4,6},{5,7},{6,4},{7,5},{8,10},{9,11},{10,... | collective-permute-start | bytes 3080 | tf_op jit(solution)/shard_map/ppermute | solution.py:250
  236.0 2.0 collective-permute-done.17
  238.7 1.6 collective-permute-start.19
  240.3 1.7 collective-permute-start.20
  242.0 1.5 collective-permute-done.18
  244.5 1.7 collective-permute-start.22
  246.2 1.6 collective-permute-start.23
  250.7 2.8 %convert_reduce_fusion = f32[64,512]{1,0:T(8,128)S(1)} fusion(bf16[64,64,512]{2,1,0:T(8,128)(2,1)} %all-to-all-done), kind=kLoop, calls=%fused_computation | loop fusion | flops 4161536 | bytes 4325376 | tf_op jit(solution)/shard_map/reduce_sum | solution.py:308
  253.6 2.0 all_gather.3
  (89 shorter events, 18.8 us)
Async XLA Ops:
  0.6 54.8 %collective-permute-start = (bf16[64,64,256]{2,1,0:T(8,128)(2,1)}, bf16[64,64,256]{2,1,0:T(8,128)(2,1)}, u32[]{:S(2)}, u32[]{:S(2)}) collective-permute-start(bf16[64,64,256]{2,1,0:T(8,128)(2,1)} %bitcast.35), channel_id=1, source_target_pairs={{0,1},{1,2},{2,3},{3,4},{4,5},{5,6},{6,7},{7,8},{8,9},{9,10},{10,1... | collective-permute-start | bytes 6291464 | tf_op jit(solution)/shard_map/ppermute | solution.py:261
  2.3 53.1 %collective-permute-start.1 = (bf16[64,64,256]{2,1,0:T(8,128)(2,1)}, bf16[64,64,256]{2,1,0:T(8,128)(2,1)}, u32[]{:S(2)}, u32[]{:S(2)}) collective-permute-start(bf16[64,64,256]{2,1,0:T(8,128)(2,1)} %bitcast.36), channel_id=1, source_target_pairs={{1,0},{2,1},{3,2},{4,3},{5,4},{6,5},{7,6},{8,7},{9,8},{10,9},{11,1... | collective-permute-start | bytes 6291464 | tf_op jit(solution)/shard_map/ppermute | solution.py:262
  16.3 6.2 %copy-start.6 = (f32[1,256]{1,0:T(1,128)S(1)}, f32[1,256]{1,0:T(1,128)}, u32[]{:S(2)}) copy-start(f32[1,256]{1,0:T(1,128)} %param.10) | copy-start | bytes 3076
  21.3 62.7 %copy-start.1 = (bf16[1024,512]{1,0:T(8,128)(2,1)}, bf16[1024,512]{1,0:T(8,128)(2,1)S(1)}, u32[]{:S(2)}) copy-start(bf16[1024,512]{1,0:T(8,128)(2,1)S(1)} %get-tuple-element.4.theirs) | copy-start | bytes 3145732
  83.8 30.9 %copy-start.2 = (bf16[1024,512]{1,0:T(8,128)(2,1)S(1)}, bf16[1024,512]{1,0:T(8,128)(2,1)}, u32[]{:S(2)}) copy-start(bf16[1024,512]{1,0:T(8,128)(2,1)} %get-tuple-element.5.mine) | copy-start | bytes 3145732
  83.9 30.8 %collective-permute-start.24 = (bf16[2048,512]{1,0:T(8,128)(2,1)S(1)}, bf16[2048,512]{1,0:T(8,128)(2,1)S(1)}, u32[]{:S(2)}, u32[]{:S(2)}) collective-permute-start(bf16[2048,512]{1,0:T(8,128)(2,1)S(1)} %fusion.8), channel_id=1, source_target_pairs={{0,64},{64,0},{1,65},{65,1},{2,66},{66,2},{3,67},{67,3},{4,68},{68... | collective-permute-start | bytes 6291464 | tf_op jit(solution)/shard_map/ppermute | solution.py:294
  86.4 30.7 %collective-permute-start.25 = (bf16[2048,512]{1,0:T(8,128)(2,1)S(1)}, bf16[2048,512]{1,0:T(8,128)(2,1)S(1)}, u32[]{:S(2)}, u32[]{:S(2)}) collective-permute-start(bf16[2048,512]{1,0:T(8,128)(2,1)S(1)} %fusion.11), channel_id=1, source_target_pairs={{0,64},{64,0},{1,65},{65,1},{2,66},{66,2},{3,67},{67,3},{4,68},{68... | collective-permute-start | bytes 6291464 | tf_op jit(solution)/shard_map/ppermute | solution.py:294
  86.9 6.7 %collective-permute-start.2 = (bf16[64,512]{1,0:T(8,128)(2,1)S(1)}, bf16[64,512]{1,0:T(8,128)(2,1)S(1)}, u32[]{:S(2)}, u32[]{:S(2)}) collective-permute-start(bf16[64,512]{1,0:T(8,128)(2,1)S(1)} %get-tuple-element.3), channel_id=1, source_target_pairs={{0,1},{1,2},{2,3},{3,0},{4,5},{5,6},{6,7},{7,4},{8,9},{9,10},{10,1... | collective-permute-start | bytes 196616 | tf_op jit(solution)/shard_map/ppermute | solution.py:250
  87.0 6.6 %collective-permute-start.3 = (bf16[64,512]{1,0:T(8,128)(2,1)S(1)}, bf16[64,512]{1,0:T(8,128)(2,1)S(1)}, u32[]{:S(2)}, u32[]{:S(2)}) collective-permute-start(bf16[64,512]{1,0:T(8,128)(2,1)S(1)} %get-tuple-element.3), channel_id=1, source_target_pairs={{0,2},{1,3},{2,0},{3,1},{4,6},{5,7},{6,4},{7,5},{8,10},{9,11},{10,... | collective-permute-start | bytes 196616 | tf_op jit(solution)/shard_map/ppermute | solution.py:250
  87.5 6.8 %collective-permute-start.4 = (bf16[64,512]{1,0:T(8,128)(2,1)S(1)}, bf16[64,512]{1,0:T(8,128)(2,1)S(1)}, u32[]{:S(2)}, u32[]{:S(2)}) collective-permute-start(bf16[64,512]{1,0:T(8,128)(2,1)S(1)} %get-tuple-element.3), channel_id=1, source_target_pairs={{0,3},{1,0},{2,1},{3,2},{4,7},{5,4},{6,5},{7,6},{8,11},{9,8},{10,9... | collective-permute-start | bytes 196616 | tf_op jit(solution)/shard_map/ppermute | solution.py:250
  94.3 14.2 %collective-permute-start.5 = (bf16[256,512]{1,0:T(8,128)(2,1)S(1)}, bf16[256,512]{1,0:T(8,128)(2,1)S(1)}, u32[]{:S(2)}, u32[]{:S(2)}) collective-permute-start(bf16[256,512]{1,0:T(8,128)(2,1)S(1)} %pad_maximum_fusion.1), channel_id=1, source_target_pairs={{0,4},{1,5},{2,6},{3,7},{4,8},{5,9},{6,10},{7,11},{8,12},{9,13},{1... | collective-permute-start | bytes 786440 | tf_op jit(solution)/shard_map/ppermute | solution.py:250
  94.3 14.1 %collective-permute-start.6 = (bf16[256,512]{1,0:T(8,128)(2,1)S(1)}, bf16[256,512]{1,0:T(8,128)(2,1)S(1)}, u32[]{:S(2)}, u32[]{:S(2)}) collective-permute-start(bf16[256,512]{1,0:T(8,128)(2,1)S(1)} %pad_maximum_fusion.1), channel_id=1, source_target_pairs={{0,8},{1,9},{2,10},{3,11},{4,12},{5,13},{6,14},{7,15},{8,0},{9,1},... | collective-permute-start | bytes 786440 | tf_op jit(solution)/shard_map/ppermute | solution.py:250
  97.5 11.6 %collective-permute-start.7 = (bf16[256,512]{1,0:T(8,128)(2,1)S(1)}, bf16[256,512]{1,0:T(8,128)(2,1)S(1)}, u32[]{:S(2)}, u32[]{:S(2)}) collective-permute-start(bf16[256,512]{1,0:T(8,128)(2,1)S(1)} %pad_maximum_fusion.1), channel_id=1, source_target_pairs={{0,12},{1,13},{2,14},{3,15},{4,0},{5,1},{6,2},{7,3},{8,4},{9,5},{1... | collective-permute-start | bytes 786440 | tf_op jit(solution)/shard_map/ppermute | solution.py:250
  109.1 20.7 %copy-start.5 = (bf16[1024,512]{1,0:T(8,128)(2,1)}, bf16[1024,512]{1,0:T(8,128)(2,1)S(1)}, u32[]{:S(2)}) copy-start(bf16[1024,512]{1,0:T(8,128)(2,1)S(1)} %constant_dynamic-update-slice_fusion.rest_0_) | copy-start | bytes 3145732
  109.1 84.3 %collective-permute-start.8 = (bf16[1024,512]{1,0:T(8,128)(2,1)S(1)}, bf16[1024,512]{1,0:T(8,128)(2,1)S(1)}, u32[]{:S(2)}, u32[]{:S(2)}) collective-permute-start(bf16[1024,512]{1,0:T(8,128)(2,1)S(1)} %constant_dynamic-update-slice_fusion.rest_0_), channel_id=1, source_target_pairs={{0,16},{1,17},{2,18},{3,19},{4,20},{5,21},{6,22},{7,23},{8,24},{9,... | collective-permute-start | bytes 3145736 | tf_op jit(solution)/shard_map/ppermute | solution.py:250
  110.1 84.9 %collective-permute-start.9 = (bf16[1024,512]{1,0:T(8,128)(2,1)S(1)}, bf16[1024,512]{1,0:T(8,128)(2,1)}, u32[]{:S(2)}, u32[]{:S(2)}) collective-permute-start(bf16[1024,512]{1,0:T(8,128)(2,1)S(1)} %constant_dynamic-update-slice_fusion.rest_0_), channel_id=1, source_target_pairs={{0,32},{1,33},{2,34},{3,35},{4,36},{5,37},{6,38},{7,39},{8,40},{9,... | collective-permute-start | bytes 3145736 | tf_op jit(solution)/shard_map/ppermute | solution.py:250
  114.7 80.3 %collective-permute-start.10 = (bf16[1024,512]{1,0:T(8,128)(2,1)S(1)}, bf16[1024,512]{1,0:T(8,128)(2,1)}, u32[]{:S(2)}, u32[]{:S(2)}) collective-permute-start(bf16[1024,512]{1,0:T(8,128)(2,1)S(1)} %constant_dynamic-update-slice_fusion.rest_0_), channel_id=1, source_target_pairs={{0,48},{1,49},{2,50},{3,51},{4,52},{5,53},{6,54},{7,55},{8,56},{9,... | collective-permute-start | bytes 3145736 | tf_op jit(solution)/shard_map/ppermute | solution.py:250
  121.8 128.9 %all-to-all-start = ((bf16[64,64,512]{2,1,0:T(8,128)(2,1)}), bf16[64,64,512]{2,1,0:T(8,128)(2,1)}, u32[]{:S(2)}, u32[]{:S(2)}) async-start(bf16[64,64,512]{2,1,0:T(8,128)(2,1)} %bitcast.33), calls=%async_computation | async-start | bytes 8388608 | tf_op jit(solution)/shard_map/all_to_all | solution.py:300
  129.8 66.3 %collective-permute-start.11 = (bf16[1024,512]{1,0:T(8,128)(2,1)S(1)}, bf16[1024,512]{1,0:T(8,128)(2,1)S(1)}, u32[]{:S(2)}, u32[]{:S(2)}) collective-permute-start(bf16[1024,512]{1,0:T(8,128)(2,1)S(1)} %constant_dynamic-update-slice_fusion.rest_0_), channel_id=1, source_target_pairs={{0,64},{64,0},{1,65},{65,1},{2,66},{66,2},{3,67},{67,3},{4,68},{68... | collective-permute-start | bytes 3145736 | tf_op jit(solution)/shard_map/ppermute | solution.py:269
  193.4 6.1 %copy-start.8 = (bf16[1024,512]{1,0:T(8,128)(2,1)}, bf16[1024,512]{1,0:T(8,128)(2,1)S(1)}, u32[]{:S(2)}) copy-start(bf16[1024,512]{1,0:T(8,128)(2,1)S(1)} %collective-permute-done.8.rest_1_) | copy-start | bytes 3145732
  193.4 2.8 %collective-permute-start.12 = (bf16[1024,512]{1,0:T(8,128)(2,1)S(1)}, bf16[1024,512]{1,0:T(8,128)(2,1)}, u32[]{:S(2)}, u32[]{:S(2)}) collective-permute-start(bf16[1024,512]{1,0:T(8,128)(2,1)S(1)} %collective-permute-done.8.rest_1_), channel_id=1, source_target_pairs={{0,64},{64,0},{1,65},{65,1},{2,66},{66,2},{3,67},{67,3},{4,68},{68... | collective-permute-start | bytes 3145736 | tf_op jit(solution)/shard_map/ppermute | solution.py:269
  195.0 3.0 %collective-permute-start.13 = (bf16[1024,512]{1,0:T(8,128)(2,1)}, bf16[1024,512]{1,0:T(8,128)(2,1)}, u32[]{:S(2)}, u32[]{:S(2)}) collective-permute-start(bf16[1024,512]{1,0:T(8,128)(2,1)} %collective-permute-done.9.rest_2_), channel_id=1, source_target_pairs={{0,64},{64,0},{1,65},{65,1},{2,66},{66,2},{3,67},{67,3},{4,68},{68... | collective-permute-start | bytes 3145736 | tf_op jit(solution)/shard_map/ppermute | solution.py:269
  195.0 4.5 %collective-permute-start.14 = (bf16[1024,512]{1,0:T(8,128)(2,1)}, bf16[1024,512]{1,0:T(8,128)(2,1)}, u32[]{:S(2)}, u32[]{:S(2)}) collective-permute-start(bf16[1024,512]{1,0:T(8,128)(2,1)} %collective-permute-done.10.rest_3_), channel_id=1, source_target_pairs={{0,64},{64,0},{1,65},{65,1},{2,66},{66,2},{3,67},{67,3},{4,68},{68... | collective-permute-start | bytes 3145736 | tf_op jit(solution)/shard_map/ppermute | solution.py:269
  228.5 6.0 %collective-permute-start.15 = (f32[1,256]{1,0:T(1,128)}, f32[1,256]{1,0:T(1,128)S(1)}, u32[]{:S(2)}, u32[]{:S(2)}) collective-permute-start(f32[1,256]{1,0:T(1,128)} %energy_share.1), channel_id=1, source_target_pairs={{0,1},{1,2},{2,3},{3,0},{4,5},{5,6},{6,7},{7,4},{8,9},{9,10},{10,1... | collective-permute-start | bytes 3080 | tf_op jit(solution)/shard_map/ppermute | solution.py:250
  228.6 7.4 %collective-permute-start.16 = (f32[1,256]{1,0:T(1,128)}, f32[1,256]{1,0:T(1,128)S(1)}, u32[]{:S(2)}, u32[]{:S(2)}) collective-permute-start(f32[1,256]{1,0:T(1,128)} %energy_share.1), channel_id=1, source_target_pairs={{0,2},{1,3},{2,0},{3,1},{4,6},{5,7},{6,4},{7,5},{8,10},{9,11},{10,... | collective-permute-start | bytes 3080 | tf_op jit(solution)/shard_map/ppermute | solution.py:250
  234.2 3.8 %collective-permute-start.17 = (f32[1,256]{1,0:T(1,128)}, f32[1,256]{1,0:T(1,128)S(1)}, u32[]{:S(2)}, u32[]{:S(2)}) collective-permute-start(f32[1,256]{1,0:T(1,128)} %energy_share.1), channel_id=1, source_target_pairs={{0,3},{1,0},{2,1},{3,2},{4,7},{5,4},{6,5},{7,6},{8,11},{9,8},{10,9... | collective-permute-start | bytes 3080 | tf_op jit(solution)/shard_map/ppermute | solution.py:250
  238.6 4.9 %collective-permute-start.18 = (f32[1,256]{1,0:T(1,128)S(1)}, f32[1,256]{1,0:T(1,128)S(1)}, u32[]{:S(2)}, u32[]{:S(2)}) collective-permute-start(f32[1,256]{1,0:T(1,128)S(1)} %fusion.27), channel_id=1, source_target_pairs={{0,4},{1,5},{2,6},{3,7},{4,8},{5,9},{6,10},{7,11},{8,12},{9,13},{1... | collective-permute-start | bytes 3080 | tf_op jit(solution)/shard_map/ppermute | solution.py:250
  238.7 5.2 %collective-permute-start.19 = (f32[1,256]{1,0:T(1,128)S(1)}, f32[1,256]{1,0:T(1,128)S(1)}, u32[]{:S(2)}, u32[]{:S(2)}) collective-permute-start(f32[1,256]{1,0:T(1,128)S(1)} %fusion.27), channel_id=1, source_target_pairs={{0,8},{1,9},{2,10},{3,11},{4,12},{5,13},{6,14},{7,15},{8,0},{9,1},... | collective-permute-start | bytes 3080 | tf_op jit(solution)/shard_map/ppermute | solution.py:250
  240.3 4.1 %collective-permute-start.20 = (f32[1,256]{1,0:T(1,128)S(1)}, f32[1,256]{1,0:T(1,128)S(1)}, u32[]{:S(2)}, u32[]{:S(2)}) collective-permute-start(f32[1,256]{1,0:T(1,128)S(1)} %fusion.27), channel_id=1, source_target_pairs={{0,12},{1,13},{2,14},{3,15},{4,0},{5,1},{6,2},{7,3},{8,4},{9,5},{1... | collective-permute-start | bytes 3080 | tf_op jit(solution)/shard_map/ppermute | solution.py:250
  244.4 4.9 %collective-permute-start.21 = (f32[1,256]{1,0:T(1,128)S(1)}, f32[1,256]{1,0:T(1,128)S(1)}, u32[]{:S(2)}, u32[]{:S(2)}) collective-permute-start(f32[1,256]{1,0:T(1,128)S(1)} %fusion.30), channel_id=1, source_target_pairs={{0,16},{1,17},{2,18},{3,19},{4,20},{5,21},{6,22},{7,23},{8,24},{9,... | collective-permute-start | bytes 3080 | tf_op jit(solution)/shard_map/ppermute | solution.py:250
  244.5 5.2 %collective-permute-start.22 = (f32[1,256]{1,0:T(1,128)S(1)}, f32[1,256]{1,0:T(1,128)S(1)}, u32[]{:S(2)}, u32[]{:S(2)}) collective-permute-start(f32[1,256]{1,0:T(1,128)S(1)} %fusion.30), channel_id=1, source_target_pairs={{0,32},{1,33},{2,34},{3,35},{4,36},{5,37},{6,38},{7,39},{8,40},{9,... | collective-permute-start | bytes 3080 | tf_op jit(solution)/shard_map/ppermute | solution.py:250
  246.2 4.0 %collective-permute-start.23 = (f32[1,256]{1,0:T(1,128)S(1)}, f32[1,256]{1,0:T(1,128)S(1)}, u32[]{:S(2)}, u32[]{:S(2)}) collective-permute-start(f32[1,256]{1,0:T(1,128)S(1)} %fusion.30), channel_id=1, source_target_pairs={{0,48},{1,49},{2,50},{3,51},{4,52},{5,53},{6,54},{7,55},{8,56},{9,... | collective-permute-start | bytes 3080 | tf_op jit(solution)/shard_map/ppermute | solution.py:250
  (6 other events, 24.9 us)
